TPU v7x, 256 devices: a whole 4x4x8 slice. The times are simulated.
256 devices in a mesh: gx: 32 (over y, z), gy: 8 (over x, core).
Axes of the slice: x: 4, y: 4, z: 8, core: 2. Of those that a mesh axis runs over, the one named last changes fastest.
Arguments:
- normed: bfloat16 [163840, 1024], P(('gx', 'gy')), may hold values from -6 to 6
- grad_query: bfloat16 [163840, 1024], P(('gx', 'gy')), may hold values from -0.25 to 0.25
- grad_key: bfloat16 [163840, 1024], P(('gx', 'gy')), may hold values from -0.25 to 0.25
- error: bfloat16 [512, 1024, 1024], P(('gx', 'gy')), may hold values from -8 to 8
- start_factor: float32 [2, 32, 1024], replicated, may hold values from -6 to 6
Outputs:
- new_error: bfloat16 [512, 1024, 1024], P(('gx', 'gy'))
- left_factor: float32 [2, 32, 1024], replicated
- right_factor: float32 [2, 32, 1024], replicated
All inputs are finite; a program needn't handle non-finite values.
Results may differ from a plain program's by a relative error of at most 0.001.
Values sent between devices are 32-bit elements; how exact they have to be, the bound alone decides.
A program may use at most 64 MiB of HBM per device.

v0:
```python
import jax
import jax.numpy as jnp
from jax import lax
from jax.sharding import PartitionSpec as P

HIGHEST = lax.Precision.HIGHEST
CONTRACT = (((0,), (0,)), ((), ()))


def gram_of(factor_rows):
    return jnp.einsum("bki,bli->bkl", factor_rows, factor_rows, precision=HIGHEST)


def solve_rows(gram_matrix, factor_rows):
    width = gram_matrix.shape[-1]
    identity = jnp.eye(width, dtype=jnp.float32)
    trace_value = jnp.trace(gram_matrix, axis1=1, axis2=2)
    shift_value = 1e-06 * (trace_value / width + 1.0)
    lower_factor = jnp.linalg.cholesky(gram_matrix + shift_value[:, None, None] * identity)
    return lax.linalg.triangular_solve(lower_factor, factor_rows, left_side=True, lower=True)


def local_left(merged, start_rows):
    return jnp.einsum("bkj,bij->bki", start_rows, merged, precision=HIGHEST)


def local_right(left_rows, merged):
    return jnp.einsum("bki,bij->bkj", left_rows, merged, precision=HIGHEST)


def single_factors(merged, start_rows, replicas):
    left_total = lax.psum(local_left(merged, start_rows), ("gx", "gy"))
    left_rows = solve_rows(gram_of(left_total), left_total)
    right_total = lax.psum(local_right(left_rows, merged), ("gx", "gy"))
    return (left_rows, right_total / replicas)


def on_device(normed, grad_query, grad_key, error, start_factor):
    replicas = lax.axis_size("gx") * lax.axis_size("gy")
    query_grad = lax.dot_general(normed, grad_query, CONTRACT, preferred_element_type=jnp.float32)
    query_merged = query_grad + error[0].astype(jnp.float32)
    query_left, query_right = single_factors(query_merged[None], start_factor[0:1], replicas)
    key_grad = lax.dot_general(normed, grad_key, CONTRACT, preferred_element_type=jnp.float32)
    key_merged = key_grad + error[1].astype(jnp.float32)
    key_left, key_right = single_factors(key_merged[None], start_factor[1:2], replicas)
    merged = jnp.stack([query_merged, key_merged])
    left_rows = jnp.concatenate([query_left, key_left], axis=0)
    right_rows = jnp.concatenate([query_right, key_right], axis=0)
    approx = jnp.einsum("bki,bkj->bij", left_rows, right_rows, precision=HIGHEST)
    return ((merged - approx).astype(jnp.bfloat16), left_rows, right_rows)


def solution(mesh):
    placed = (
        P(("gx", "gy"), None),
        P(("gx", "gy"), None),
        P(("gx", "gy"), None),
        P(("gx", "gy"), None, None),
        P(),
    )
    return jax.shard_map(
        on_device,
        mesh=mesh,
        in_specs=placed,
        out_specs=(P(("gx", "gy"), None, None), P(), P()),
        check_vma=False,
    )
```

profile of v0, /device:TPU:1, one launch (start us, length us, event | category | flops | bytes accessed | tf_op | source)
XLA Modules:
  0.0 574.7 jit_solution(298892361489647621)
XLA Ops:
  7.2 1.3 copy-done
  8.5 4.0 convert_add_fusion.1
  12.5 1.8 convert_add_fusion
  14.5 4.6 convolution_bitcast_fusion.3
  19.1 4.6 convolution_bitcast_fusion.2
  23.7 0.2 all-reduce.5.cloned.1.call-start
  23.9 252.9 %all-reduce.7.cloned.1.call-done = (f32[1,32,1024]{2,1,0:T(8,128)}, f32[1,32,1024]{2,1,0:T(8,128)}) async-done(((f32[1,32,1024]{2,1,0:T(8,128)}, f32[1,32,1024]{2,1,0:T(8,128)}), (f32[1,32,1024]{2,1,0:T(8,128)}, f32[1,32,1024]{2,1,0:T(8,128)})) %all-reduce.7.cloned.1.call-update) | async-done | bytes 262160 | tf_op jit(solution)/shard_map/psum | solution.py:32
  276.8 1.8 select_reduce_fusion.2
  279.4 2.9 custom-call.10
  282.3 0.6 compare_reduce_fusion
  283.0 0.7 fusion.14
  283.6 2.4 custom-call.11
  286.1 1.2 fusion.1
  287.3 1.8 select_reduce_fusion.3
  289.9 2.9 custom-call.8
  292.9 0.6 compare_reduce_fusion.1
  293.5 0.7 fusion.13
  294.2 2.4 custom-call.9
  296.6 1.4 fusion.6
  298.0 5.3 convolution_bitcast_fusion.1
  303.3 3.1 convolution_bitcast_fusion
  306.5 249.5 %all-reduce.5.cloned.1.call-done = (f32[1,32,1024]{2,1,0:T(8,128)}, f32[1,32,1024]{2,1,0:T(8,128)}) async-done(((f32[1,32,1024]{2,1,0:T(8,128)}, f32[1,32,1024]{2,1,0:T(8,128)}), (f32[1,32,1024]{2,1,0:T(8,128)}, f32[1,32,1024]{2,1,0:T(8,128)})) %all-reduce.5.cloned.1.call-update) | async-done | bytes 262160 | tf_op jit(solution)/shard_map/psum | solution.py:34
  556.0 1.0 broadcast_multiply_fusion
  557.1 10.7 %fusion = bf16[2,1024,1024]{2,1,0:T(8,128)(2,1)} fusion(f32[1,1024,1024]{2,1,0:T(8,128)} %bitcast.81, f32[1,1024,1024]{2,1,0:T(8,128)} %bitcast.80, f32[2,32,1024]{2,1,0:T(8,128)S(1)} %pad_maximum_fusion, f32[2,32,1024]{2,1,0:T(8,128)S(1)} %pad_maximum_fusion.1), kind=kOutput, calls=%fused_computation.1 | convolution fusion | flops 811597824 | bytes 13107200 | tf_op jit(solution)/shard_map/bki,bkj->bij/dot_general | solution.py:49
  (30 shorter events, 0.5 us)
Async XLA Ops:
  7.2 1.3 copy-start
  7.2 5.3 copy-start.8
  7.2 269.6 %all-reduce.7.cloned.1.call-start = ((), (), s32[]{:S(2)}) async-start(), calls=%async_computation.1 | async-start | bytes 524288 | tf_op jit(solution)/shard_map/psum | solution.py:32
  8.5 4.0 copy-start.7
  12.5 2.0 copy-start.1
  12.5 2.0 copy-start.6
  14.5 4.6 copy-start.2
  23.7 532.4 %all-reduce.5.cloned.1.call-start = ((), (), s32[]{:S(2)}) async-start(), calls=%async_computation | async-start | bytes 524288 | tf_op jit(solution)/shard_map/psum | solution.py:34
  296.6 6.7 %copy-start.3 = (f32[1024,1024]{1,0:T(8,128)S(1)}, f32[1024,1024]{1,0:T(8,128)}, u32[]{:S(2)}) copy-start(f32[1024,1024]{1,0:T(8,128)} %copy-done.2) | copy-start | bytes 12582916
  306.5 261.3 %copy-start.4 = (f32[2,32,1024]{2,1,0:T(8,128)}, f32[2,32,1024]{2,1,0:T(8,128)S(1)}, u32[]{:S(2)}) copy-start(f32[2,32,1024]{2,1,0:T(8,128)S(1)} %pad_maximum_fusion) | copy-start | bytes 786436
  557.1 10.7 %copy-start.5 = (f32[2,32,1024]{2,1,0:T(8,128)}, f32[2,32,1024]{2,1,0:T(8,128)S(1)}, u32[]{:S(2)}) copy-start(f32[2,32,1024]{2,1,0:T(8,128)S(1)} %pad_maximum_fusion.1) | copy-start | bytes 786436
Sparse Core Ops, SparseCore 0:
  23.8 252.9 all-reduce.6
  306.6 249.3 all-reduce.4
where the time goes:
time: 576 us; the launch traced here: 575 us
  waiting for transfers between devices  502 us (87%)
  matrix products  40.5 us (7%)
  between operations  15.5 us (3%)
  other arithmetic  14.4 us (2%)
    psum x1, waiting for transfers between devices, single_factors(): left_total = lax.psum(local_left(merged, start_rows), ('gx', 'gy'))  253 us
    psum x1, waiting for transfers between devices, single_factors(): right_total = lax.psum(local_right(left_rows, merged), ('gx', 'gy'))  250 us
  transfers between devices with their start and end apart: 2, of which 2 were waited for; matrix products, arithmetic and copies ran while one was open for 0% of the time, Pallas kernels for 0%

commit v1 on v0

v1 whole, which is shorter than its diff:
```python
import functools

import jax
import jax.numpy as jnp
from jax import lax
from jax.experimental import pallas as pl
from jax.experimental.pallas import tpu as pltpu
from jax.sharding import PartitionSpec as P

HIGHEST = lax.Precision.HIGHEST
CONTRACT = (((0,), (0,)), ((), ()))
MESH_ID = pl.DeviceIdType.MESH
LANES = 128
SUB = 8


def allreduce_kernel(nx, ny, x_ref, o_ref, recv_a, p_t, recv_b, recv_c, recv_d,
                     sa, ra, sb, rb, sc, rc, sd, rd):
    h = lax.axis_index("gx")
    a = lax.axis_index("gy")
    nb, rows = x_ref.shape[0], x_ref.shape[1]
    kb = rows // SUB
    nt = nb * kb

    barrier = pltpu.get_barrier_semaphore()

    def signal_y(j, carry):
        pl.semaphore_signal(barrier, 1, device_id=(h, lax.rem(a + j, ny)),
                            device_id_type=MESH_ID)
        return carry

    def signal_x(j, carry):
        pl.semaphore_signal(barrier, 1, device_id=(lax.rem(h + j, nx), a),
                            device_id_type=MESH_ID)
        return carry

    lax.fori_loop(1, ny, signal_y, 0)
    lax.fori_loop(1, nx, signal_x, 0)
    pl.semaphore_wait(barrier, (ny - 1) + (nx - 1))

    def copy_a(peer, slot_src):
        return pltpu.make_async_remote_copy(
            src_ref=x_ref.at[:, :, pl.ds(pl.multiple_of(peer * LANES, LANES), LANES)],
            dst_ref=recv_a.at[slot_src],
            send_sem=sa.at[peer],
            recv_sem=ra.at[slot_src],
            device_id=(h, peer),
            device_id_type=MESH_ID,
        )

    def start_a(j, carry):
        copy_a(lax.rem(a + j, ny), a).start()
        return carry

    lax.fori_loop(1, ny, start_a, 0)
    recv_a[a] = x_ref[:, :, pl.ds(pl.multiple_of(a * LANES, LANES), LANES)]

    def wait_a(j, carry):
        copy_a(lax.rem(a + j, ny), a).wait_send()
        copy_a(a, lax.rem(a + j, ny)).wait_recv()
        return carry

    lax.fori_loop(1, ny, wait_a, 0)
    part = jnp.sum(recv_a[...], axis=0)
    for u in range(nt):
        p_t[u] = part[u // kb, (u % kb) * SUB:(u % kb + 1) * SUB, :]

    def copy_b(peer, slot_src, tile):
        return pltpu.make_async_remote_copy(
            src_ref=p_t.at[tile],
            dst_ref=recv_b.at[slot_src],
            send_sem=sb.at[peer],
            recv_sem=rb.at[slot_src],
            device_id=(peer, a),
            device_id_type=MESH_ID,
        )

    def start_b(j, carry):
        peer = lax.rem(h + j, nx)
        copy_b(peer, h, lax.rem(peer, nt)).start()
        return carry

    lax.fori_loop(1, nx, start_b, 0)
    own = lax.rem(h, nt)
    recv_b[h] = p_t[own]

    def wait_b(j, carry):
        peer = lax.rem(h + j, nx)
        copy_b(peer, h, lax.rem(peer, nt)).wait_send()
        copy_b(h, peer, own).wait_recv()
        return carry

    lax.fori_loop(1, nx, wait_b, 0)
    recv_c[own] = jnp.sum(recv_b[...], axis=0)

    base = h - own

    def copy_c(peer_tile, slot_tile):
        return pltpu.make_async_remote_copy(
            src_ref=recv_c.at[slot_tile],
            dst_ref=recv_c.at[slot_tile],
            send_sem=sc.at[peer_tile],
            recv_sem=rc.at[slot_tile],
            device_id=(base + peer_tile, a),
            device_id_type=MESH_ID,
        )

    def start_c(j, carry):
        copy_c(lax.rem(own + j, nt), own).start()
        return carry

    lax.fori_loop(1, nt, start_c, 0)

    def wait_c(j, carry):
        other = lax.rem(own + j, nt)
        copy_c(other, own).wait_send()
        copy_c(own, other).wait_recv()
        return carry

    lax.fori_loop(1, nt, wait_c, 0)
    for u in range(nt):
        recv_d[a, u // kb, (u % kb) * SUB:(u % kb + 1) * SUB, :] = recv_c[u]

    def copy_d(peer, slot_src):
        return pltpu.make_async_remote_copy(
            src_ref=recv_d.at[slot_src],
            dst_ref=recv_d.at[slot_src],
            send_sem=sd.at[peer],
            recv_sem=rd.at[slot_src],
            device_id=(h, peer),
            device_id_type=MESH_ID,
        )

    def start_d(j, carry):
        copy_d(lax.rem(a + j, ny), a).start()
        return carry

    lax.fori_loop(1, ny, start_d, 0)

    def wait_d(j, carry):
        copy_d(lax.rem(a + j, ny), a).wait_send()
        copy_d(a, lax.rem(a + j, ny)).wait_recv()
        return carry

    lax.fori_loop(1, ny, wait_d, 0)
    for s in range(ny):
        o_ref[:, :, s * LANES:(s + 1) * LANES] = recv_d[s]


def allreduce(x, nx, ny, collective_id):
    nb, rows, cols = x.shape
    assert cols == ny * LANES and rows % SUB == 0
    nt = nb * (rows // SUB)
    assert nx % nt == 0
    vmem = pltpu.VMEM
    return pl.pallas_call(
        functools.partial(allreduce_kernel, nx, ny),
        out_shape=jax.ShapeDtypeStruct(x.shape, jnp.float32),
        in_specs=[pl.BlockSpec(memory_space=vmem)],
        out_specs=pl.BlockSpec(memory_space=vmem),
        scratch_shapes=[
            vmem((ny, nb, rows, LANES), jnp.float32),
            vmem((nt, SUB, LANES), jnp.float32),
            vmem((nx, SUB, LANES), jnp.float32),
            vmem((nt, SUB, LANES), jnp.float32),
            vmem((ny, nb, rows, LANES), jnp.float32),
            pltpu.SemaphoreType.DMA((ny,)),
            pltpu.SemaphoreType.DMA((ny,)),
            pltpu.SemaphoreType.DMA((nx,)),
            pltpu.SemaphoreType.DMA((nx,)),
            pltpu.SemaphoreType.DMA((nt,)),
            pltpu.SemaphoreType.DMA((nt,)),
            pltpu.SemaphoreType.DMA((ny,)),
            pltpu.SemaphoreType.DMA((ny,)),
        ],
        compiler_params=pltpu.CompilerParams(
            collective_id=collective_id, has_side_effects=True
        ),
    )(x)


def gram_of(factor_rows):
    return jnp.einsum("bki,bli->bkl", factor_rows, factor_rows, precision=HIGHEST)


def solve_rows(gram_matrix, factor_rows):
    width = gram_matrix.shape[-1]
    identity = jnp.eye(width, dtype=jnp.float32)
    trace_value = jnp.trace(gram_matrix, axis1=1, axis2=2)
    shift_value = 1e-06 * (trace_value / width + 1.0)
    lower_factor = jnp.linalg.cholesky(gram_matrix + shift_value[:, None, None] * identity)
    return lax.linalg.triangular_solve(lower_factor, factor_rows, left_side=True, lower=True)


def on_device(nx, ny, normed, grad_query, grad_key, error, start_factor):
    replicas = nx * ny
    query_grad = lax.dot_general(normed, grad_query, CONTRACT, preferred_element_type=jnp.float32)
    key_grad = lax.dot_general(normed, grad_key, CONTRACT, preferred_element_type=jnp.float32)
    merged = jnp.stack([query_grad, key_grad]) + error.astype(jnp.float32)
    left_local = jnp.einsum("bkj,bij->bki", start_factor, merged, precision=HIGHEST)
    left_total = allreduce(left_local, nx, ny, 0)
    left_rows = solve_rows(gram_of(left_total), left_total)
    right_local = jnp.einsum("bki,bij->bkj", left_rows, merged, precision=HIGHEST)
    right_rows = allreduce(right_local, nx, ny, 1) / replicas
    approx = jnp.einsum("bki,bkj->bij", left_rows, right_rows, precision=HIGHEST)
    return ((merged - approx).astype(jnp.bfloat16), left_rows, right_rows)


def solution(mesh):
    nx, ny = mesh.shape["gx"], mesh.shape["gy"]
    placed = (
        P(("gx", "gy"), None),
        P(("gx", "gy"), None),
        P(("gx", "gy"), None),
        P(("gx", "gy"), None, None),
        P(),
    )
    return jax.shard_map(
        functools.partial(on_device, nx, ny),
        mesh=mesh,
        in_specs=placed,
        out_specs=(P(("gx", "gy"), None, None), P(), P()),
        check_vma=False,
    )
```

time: 576 us -> 118 us (0.20)
  waiting for transfers between devices: 502 us -> 0 us
  Pallas kernels: 0 us -> 62.7 us
  between operations: 15.5 us -> 0.78 us
    psum x2 -> x0, waiting for transfers between devices: 502 us -> none  [the longest x1 253 us: single_factors(): left_total = lax.psum(local_left(merged, start_rows), ('gx', 'gy'))]
    pallas_call x0 -> x2, Pallas kernels: none -> 62.7 us  [allreduce(): pl.pallas_call(functools.partial(allreduce_kernel, nx, ny), out_shape=jax...]
    dot_general x4 -> x2, matrix products: 17.6 us -> 17.7 us  [the longest x1 9.07 us: on_device(): jnp.einsum('bki,bij->bkj', left_rows, merged, precision=HIGHEST)]
  transfers between devices with their start and end apart: 2 -> 0, of which waited for: 2 -> 0; matrix products, arithmetic and copies ran while one was open for 0% -> 0% of each run, Pallas kernels for 0% -> 0%
where the time goes in v1:
time: 118 us; the launch traced here: 117 us
  Pallas kernels  62.7 us (53%)
  matrix products  37.2 us (32%)
  other arithmetic  12.1 us (10%)
  local copies, waits for them, and re-layouts  4.71 us (4%)
    pallas_call x2, Pallas kernels, allreduce(): pl.pallas_call(functools.partial(allreduce_kernel, nx, ny), out_shape=jax...  62.7 us
    dot_general x1, matrix products, on_device(): jnp.einsum('bki,bkj->bij', left_rows, right_rows, precision=HIGHEST)  11.6 us
    dot_general x1, matrix products, on_device(): jnp.einsum('bki,bij->bkj', left_rows, merged, precision=HIGHEST)  9.07 us
    dot_general x1, matrix products, on_device(): jnp.einsum('bkj,bij->bki', start_factor, merged, precision=HIGHEST)  8.64 us
    another operation x4, other arithmetic, solve_rows(): jnp.linalg.cholesky(gram_matrix + shift_value[:, None, None] * identity)  6.03 us
    another operation x3, other arithmetic, solve_rows(): lax.linalg.triangular_solve(lower_factor, factor_rows, left_side=True, lo...  5 us
    unnamed x16, local copies, waits for them, and re-layouts  4.63 us
    dot_general x1, matrix products, on_device(): lax.dot_general(normed, grad_query, CONTRACT, preferred_element_type=jnp....  3.15 us

profile of v1, /device:TPU:1, one launch (start us, length us, event | category | flops | bytes accessed | tf_op | source)
XLA Modules:
  0.0 117.5 jit_solution(15682138469092585827)
XLA Ops:
  0.6 0.0 copy-start
  0.7 1.3 %copy-done = bf16[640,1024]{1,0:T(8,128)(2,1)S(1)} copy-done((bf16[640,1024]{1,0:T(8,128)(2,1)S(1)}, bf16[640,1024]{1,0:T(8,128)(2,1)}, u32[]{:S(2)}) %copy-start) | copy-done | bytes 1310744
  2.0 3.1 %convolution_bitcast_fusion.1 = f32[1,1024,1024]{2,1,0:T(8,128)S(1)} fusion(bf16[640,1024]{1,0:T(8,128)(2,1)S(1)} %copy-done, bf16[640,1024]{1,0:T(8,128)(2,1)} %param.6), kind=kOutput, calls=%fused_computation.3 | convolution fusion | flops 1342177280 | bytes 6815744 | tf_op jit(solution)/shard_map/dot_general | solution.py:197
  5.1 0.0 copy-start.1
  5.2 1.9 %convolution_bitcast_fusion = f32[1,1024,1024]{2,1,0:T(8,128)S(1)} fusion(bf16[640,1024]{1,0:T(8,128)(2,1)S(1)} %copy-done, bf16[640,1024]{1,0:T(8,128)(2,1)S(1)} %copy-done.7), kind=kOutput, calls=%fused_computation.2 | convolution fusion | flops 1342177280 | bytes 6815744 | tf_op jit(solution)/shard_map/dot_general | solution.py:198
  7.0 0.2 copy-done.2
  7.3 2.1 %copy-done.3 = f32[1,1024,1024]{2,1,0:T(8,128)} copy-done((f32[1,1024,1024]{2,1,0:T(8,128)}, f32[1,1024,1024]{2,1,0:T(8,128)S(1)}, u32[]{:S(2)}) %copy-start.3) | copy-done | bytes 4194328
  9.4 1.0 copy-done.1
  10.3 0.0 copy-done.6
  10.4 8.6 %convolution_bitcast_fusion.2.x_ref = f32[2,32,1024]{2,1,0:T(8,128)} fusion(f32[2,32,1024]{2,1,0:T(8,128)S(1)} %copy-done.6, f32[1,1024,1024]{2,1,0:T(8,128)S(1)} %convolution_bitcast_fusion, f32[1,1024,1024]{2,1,0:T(8,128)S(1)} %convolution_bitcast_fusion.1, bf16[2,1024,1024]{2,1,0:T(8,128)(2,1)S(1)} %copy-done.1), kind=kOutput, calls=%fused_computation.4 | convolution fusion | flops 811597824 | bytes 13107200 | tf_op jit(solution)/shard_map/bkj,bij->bki/dot_general | solution.py:200
  19.0 35.6 %shard_map.76 = f32[2,32,1024]{2,1,0:T(8,128)} custom-call(f32[2,32,1024]{2,1,0:T(8,128)} %convolution_bitcast_fusion.2.x_ref), custom_call_target="tpu_custom_call" | custom-call | tf_op jit(solution)/shard_map/pallas_call | solution.py:156
  54.6 1.5 %select_reduce_fusion.1 = (f32[2]{0:T(128)S(1)}, f32[2,32,32]{2,1,0:T(8,128)S(1)}) fusion(pred[32,32]{1,0:T(8,128)(4,1)S(1)} %iota_compare_fusion.1, f32[2,32,1024]{2,1,0:T(8,128)} %shard_map.76), kind=kOutput, calls=%fused_computation.14 | convolution fusion | flops 25169918 | bytes 271368 | tf_op jit(solution)/shard_map/bki,bli->bkl/dot_general | solution.py:183
  56.1 0.1 copy.10
  56.2 0.1 fusion.4
  56.3 5.9 %custom-call.7 = f32[2,32,32]{2,1,0:T(8,128)S(1)} custom-call(f32[2,32,32]{2,1,0:T(8,128)S(1)} %fusion.4), custom_call_target="Cholesky" | custom-call | tf_op jit(solution)/shard_map/jit(cholesky)/cholesky | solution.py:191
  62.2 0.1 compare_reduce_fusion
  62.3 0.1 select_bitcast_fusion
  62.4 4.9 %custom-call.8 = f32[2,1,32,32]{2,3,1,0:T(8,128)S(1)} custom-call(f32[2,1,32,32]{3,2,1,0:T(8,128)S(1)} %select_bitcast_fusion), custom_call_target="InvertDiagBlocksLowerTriangular" | custom-call | tf_op jit(solution)/shard_map/triangular_solve | solution.py:192
  67.3 1.4 %fusion.1 = f32[2,32,1024]{2,1,0:T(8,128)S(1)} fusion(f32[2,32,1024]{2,1,0:T(8,128)} %shard_map.76, f32[2,1,32,32]{2,3,1,0:T(8,128)S(1)} %custom-call.8), kind=kOutput, calls=%fused_computation.7 | convolution fusion | flops 25165824 | bytes 532480 | tf_op jit(solution)/shard_map/triangular_solve | solution.py:192
  68.7 0.0 copy-start.4
  68.7 9.1 %fusion.x_ref = f32[2,32,1024]{2,1,0:T(8,128)} fusion(f32[2,32,1024]{2,1,0:T(8,128)S(1)} %fusion.1, f32[1,1024,1024]{2,1,0:T(8,128)} %copy-done.3, f32[1,1024,1024]{2,1,0:T(8,128)} %copy-done.2, bf16[2,1024,1024]{2,1,0:T(8,128)(2,1)} %param.8), kind=kOutput, calls=%fused_computation.5 | convolution fusion | flops 811597824 | bytes 13107200 | tf_op jit(solution)/shard_map/bki,bij->bkj/dot_general | solution.py:203
  77.8 27.1 %shard_map.77 = f32[2,32,1024]{2,1,0:T(8,128)} custom-call(f32[2,32,1024]{2,1,0:T(8,128)} %fusion.x_ref), custom_call_target="tpu_custom_call" | custom-call | tf_op jit(solution)/shard_map/pallas_call | solution.py:156
  104.9 1.0 broadcast_multiply_fusion
  105.9 11.6 %subtract_convert_fusion = bf16[2,1024,1024]{2,1,0:T(8,128)(2,1)} fusion(f32[2,32,1024]{2,1,0:T(8,128)S(1)} %fusion.1, f32[2,32,1024]{2,1,0:T(8,128)S(1)} %broadcast_multiply_fusion, bf16[2,1024,1024]{2,1,0:T(8,128)(2,1)} %param.8, f32[1,1024,1024]{2,1,0:T(8,128)} %copy-done.3, f32[1,1024,1024]{2,1,0:T(8,128)} %copy-done.2), kind=kOutput, calls=%fused_computation.1 | convolution fusion | flops 815792128 | bytes 17301504 | tf_op jit(solution)/shard_map/bki,bkj->bij/dot_general | solution.py:205
  (13 shorter events, 0.1 us)
Async XLA Ops:
  0.6 1.3 %copy-start = (bf16[640,1024]{1,0:T(8,128)(2,1)S(1)}, bf16[640,1024]{1,0:T(8,128)(2,1)}, u32[]{:S(2)}) copy-start(bf16[640,1024]{1,0:T(8,128)(2,1)} %param.5) | copy-start | bytes 3932164
  0.6 4.5 %copy-start.7 = (bf16[640,1024]{1,0:T(8,128)(2,1)S(1)}, bf16[640,1024]{1,0:T(8,128)(2,1)}, u32[]{:S(2)}) copy-start(bf16[640,1024]{1,0:T(8,128)(2,1)} %param.7) | copy-start | bytes 3932164
  5.1 2.1 %copy-start.2 = (f32[1,1024,1024]{2,1,0:T(8,128)}, f32[1,1024,1024]{2,1,0:T(8,128)S(1)}, u32[]{:S(2)}) copy-start(f32[1,1024,1024]{2,1,0:T(8,128)S(1)} %convolution_bitcast_fusion.1) | copy-start | bytes 12582916
  5.1 5.2 %copy-start.1 = (bf16[2,1024,1024]{2,1,0:T(8,128)(2,1)S(1)}, bf16[2,1024,1024]{2,1,0:T(8,128)(2,1)}, u32[]{:S(2)}) copy-start(bf16[2,1024,1024]{2,1,0:T(8,128)(2,1)} %param.8) | copy-start | bytes 12582916
  5.1 5.2 %copy-start.6 = (f32[2,32,1024]{2,1,0:T(8,128)S(1)}, f32[2,32,1024]{2,1,0:T(8,128)}, u32[]{:S(2)}) copy-start(f32[2,32,1024]{2,1,0:T(8,128)} %param.9) | copy-start | bytes 786436
  7.3 2.1 %copy-start.3 = (f32[1,1024,1024]{2,1,0:T(8,128)}, f32[1,1024,1024]{2,1,0:T(8,128)S(1)}, u32[]{:S(2)}) copy-start(f32[1,1024,1024]{2,1,0:T(8,128)S(1)} %convolution_bitcast_fusion) | copy-start | bytes 12582916
  68.7 37.2 %copy-start.4 = (f32[2,32,1024]{2,1,0:T(8,128)}, f32[2,32,1024]{2,1,0:T(8,128)S(1)}, u32[]{:S(2)}) copy-start(f32[2,32,1024]{2,1,0:T(8,128)S(1)} %fusion.1) | copy-start | bytes 786436
  105.8 11.6 %copy-start.5 = (f32[2,32,1024]{2,1,0:T(8,128)}, f32[2,32,1024]{2,1,0:T(8,128)S(1)}, u32[]{:S(2)}) copy-start(f32[2,32,1024]{2,1,0:T(8,128)S(1)} %broadcast_multiply_fusion) | copy-start | bytes 786436

commit v2 on v1

--- a/solution.py
+++ b/solution.py
@@ -8,6 +8,7 @@
 from jax.sharding import PartitionSpec as P
 
 HIGHEST = lax.Precision.HIGHEST
+HIGH = lax.Precision.HIGH
 CONTRACT = (((0,), (0,)), ((), ()))
 MESH_ID = pl.DeviceIdType.MESH
 LANES = 128
@@ -200,9 +201,9 @@
     left_local = jnp.einsum("bkj,bij->bki", start_factor, merged, precision=HIGHEST)
     left_total = allreduce(left_local, nx, ny, 0)
     left_rows = solve_rows(gram_of(left_total), left_total)
-    right_local = jnp.einsum("bki,bij->bkj", left_rows, merged, precision=HIGHEST)
+    right_local = jnp.einsum("bki,bij->bkj", left_rows, merged, precision=HIGH)
     right_rows = allreduce(right_local, nx, ny, 1) / replicas
-    approx = jnp.einsum("bki,bkj->bij", left_rows, right_rows, precision=HIGHEST)
+    approx = jnp.einsum("bki,bkj->bij", left_rows, right_rows, precision=HIGH)
     return ((merged - approx).astype(jnp.bfloat16), left_rows, right_rows)
 
 

time: 118 us -> 112 us (0.949)
  matrix products: 37.2 us -> 31.7 us
    dot_general x2, matrix products: 20.7 us -> 15.1 us  [the longest x1 8.29 us: on_device(): approx = jnp.einsum('bki,bkj->bij', left_rows, right_rows, precision=HIGH)]
where the time goes in v2:
time: 112 us
  Pallas kernels  62.7 us (56%)
  matrix products  31.7 us (28%)
  other arithmetic  12.1 us (11%)
  local copies, waits for them, and re-layouts  4.71 us (4%)
    pallas_call x2, Pallas kernels, allreduce(): pl.pallas_call(functools.partial(allreduce_kernel, nx, ny), out_shape=jax...  62.7 us
    dot_general x1, matrix products, on_device(): jnp.einsum('bkj,bij->bki', start_factor, merged, precision=HIGHEST)  8.64 us
    dot_general x1, matrix products, on_device(): approx = jnp.einsum('bki,bkj->bij', left_rows, right_rows, precision=HIGH)  8.29 us
    dot_general x1, matrix products, on_device(): right_local = jnp.einsum('bki,bij->bkj', left_rows, merged, precision=HIGH)  6.84 us
    another operation x4, other arithmetic, solve_rows(): jnp.linalg.cholesky(gram_matrix + shift_value[:, None, None] * identity)  6.03 us
    another operation x3, other arithmetic, solve_rows(): lax.linalg.triangular_solve(lower_factor, factor_rows, left_side=True, lo...  5 us
    unnamed x16, local copies, waits for them, and re-layouts  4.63 us
    dot_general x1, matrix products, on_device(): lax.dot_general(normed, grad_query, CONTRACT, preferred_element_type=jnp....  3.15 us

profile of v2, /device:TPU:1, one launch (start us, length us, event | category | flops | bytes accessed | tf_op | source)
XLA Modules:
  0.0 111.9 jit_solution(65831725385741876)
XLA Ops:
  0.6 0.0 copy-start
  0.7 1.3 %copy-done = bf16[640,1024]{1,0:T(8,128)(2,1)S(1)} copy-done((bf16[640,1024]{1,0:T(8,128)(2,1)S(1)}, bf16[640,1024]{1,0:T(8,128)(2,1)}, u32[]{:S(2)}) %copy-start) | copy-done | bytes 1310744
  2.0 3.1 %convolution_bitcast_fusion.1 = f32[1,1024,1024]{2,1,0:T(8,128)S(1)} fusion(bf16[640,1024]{1,0:T(8,128)(2,1)S(1)} %copy-done, bf16[640,1024]{1,0:T(8,128)(2,1)} %param.6), kind=kOutput, calls=%fused_computation.3 | convolution fusion | flops 1342177280 | bytes 6815744 | tf_op jit(solution)/shard_map/dot_general | solution.py:198
  5.1 0.0 copy-start.1
  5.2 1.9 %convolution_bitcast_fusion = f32[1,1024,1024]{2,1,0:T(8,128)S(1)} fusion(bf16[640,1024]{1,0:T(8,128)(2,1)S(1)} %copy-done, bf16[640,1024]{1,0:T(8,128)(2,1)S(1)} %copy-done.7), kind=kOutput, calls=%fused_computation.2 | convolution fusion | flops 1342177280 | bytes 6815744 | tf_op jit(solution)/shard_map/dot_general | solution.py:199
  7.0 0.2 copy-done.2
  7.3 2.1 %copy-done.3 = f32[1,1024,1024]{2,1,0:T(8,128)} copy-done((f32[1,1024,1024]{2,1,0:T(8,128)}, f32[1,1024,1024]{2,1,0:T(8,128)S(1)}, u32[]{:S(2)}) %copy-start.3) | copy-done | bytes 4194328
  9.4 1.0 copy-done.1
  10.3 0.0 copy-done.6
  10.4 8.6 %convolution_bitcast_fusion.2.x_ref = f32[2,32,1024]{2,1,0:T(8,128)} fusion(f32[2,32,1024]{2,1,0:T(8,128)S(1)} %copy-done.6, f32[1,1024,1024]{2,1,0:T(8,128)S(1)} %convolution_bitcast_fusion, f32[1,1024,1024]{2,1,0:T(8,128)S(1)} %convolution_bitcast_fusion.1, bf16[2,1024,1024]{2,1,0:T(8,128)(2,1)S(1)} %copy-done.1), kind=kOutput, calls=%fused_computation.4 | convolution fusion | flops 811597824 | bytes 13107200 | tf_op jit(solution)/shard_map/bkj,bij->bki/dot_general | solution.py:201
  19.0 35.6 %shard_map.76 = f32[2,32,1024]{2,1,0:T(8,128)} custom-call(f32[2,32,1024]{2,1,0:T(8,128)} %convolution_bitcast_fusion.2.x_ref), custom_call_target="tpu_custom_call" | custom-call | tf_op jit(solution)/shard_map/pallas_call | solution.py:157
  54.6 1.5 %select_reduce_fusion.1 = (f32[2]{0:T(128)S(1)}, f32[2,32,32]{2,1,0:T(8,128)S(1)}) fusion(pred[32,32]{1,0:T(8,128)(4,1)S(1)} %iota_compare_fusion.1, f32[2,32,1024]{2,1,0:T(8,128)} %shard_map.76), kind=kOutput, calls=%fused_computation.14 | convolution fusion | flops 25169918 | bytes 271368 | tf_op jit(solution)/shard_map/bki,bli->bkl/dot_general | solution.py:184
  56.1 0.1 copy.10
  56.2 0.1 fusion.4
  56.3 5.9 %custom-call.7 = f32[2,32,32]{2,1,0:T(8,128)S(1)} custom-call(f32[2,32,32]{2,1,0:T(8,128)S(1)} %fusion.4), custom_call_target="Cholesky" | custom-call | tf_op jit(solution)/shard_map/jit(cholesky)/cholesky | solution.py:192
  62.2 0.1 compare_reduce_fusion
  62.3 0.1 select_bitcast_fusion
  62.4 4.9 %custom-call.8 = f32[2,1,32,32]{2,3,1,0:T(8,128)S(1)} custom-call(f32[2,1,32,32]{3,2,1,0:T(8,128)S(1)} %select_bitcast_fusion), custom_call_target="InvertDiagBlocksLowerTriangular" | custom-call | tf_op jit(solution)/shard_map/triangular_solve | solution.py:193
  67.3 1.4 %fusion.1 = f32[2,32,1024]{2,1,0:T(8,128)S(1)} fusion(f32[2,32,1024]{2,1,0:T(8,128)} %shard_map.76, f32[2,1,32,32]{2,3,1,0:T(8,128)S(1)} %custom-call.8), kind=kOutput, calls=%fused_computation.7 | convolution fusion | flops 25165824 | bytes 532480 | tf_op jit(solution)/shard_map/triangular_solve | solution.py:193
  68.7 0.0 copy-start.4
  68.7 6.8 %fusion.x_ref = f32[2,32,1024]{2,1,0:T(8,128)} fusion(f32[2,32,1024]{2,1,0:T(8,128)S(1)} %fusion.1, f32[1,1024,1024]{2,1,0:T(8,128)} %copy-done.3, f32[1,1024,1024]{2,1,0:T(8,128)} %copy-done.2, bf16[2,1024,1024]{2,1,0:T(8,128)(2,1)} %param.8), kind=kOutput, calls=%fused_computation.5 | convolution fusion | flops 408944640 | bytes 13107200 | tf_op jit(solution)/shard_map/bki,bij->bkj/dot_general | solution.py:204
  75.5 27.1 %shard_map.77 = f32[2,32,1024]{2,1,0:T(8,128)} custom-call(f32[2,32,1024]{2,1,0:T(8,128)} %fusion.x_ref), custom_call_target="tpu_custom_call" | custom-call | tf_op jit(solution)/shard_map/pallas_call | solution.py:157
  102.6 1.0 broadcast_multiply_fusion
  103.6 8.3 %subtract_convert_fusion = bf16[2,1024,1024]{2,1,0:T(8,128)(2,1)} fusion(f32[2,32,1024]{2,1,0:T(8,128)S(1)} %fusion.1, f32[2,32,1024]{2,1,0:T(8,128)S(1)} %broadcast_multiply_fusion, bf16[2,1024,1024]{2,1,0:T(8,128)(2,1)} %param.8, f32[1,1024,1024]{2,1,0:T(8,128)} %copy-done.3, f32[1,1024,1024]{2,1,0:T(8,128)} %copy-done.2), kind=kOutput, calls=%fused_computation.1 | convolution fusion | flops 413138944 | bytes 17301504 | tf_op jit(solution)/shard_map/bki,bkj->bij/dot_general | solution.py:206
  (13 shorter events, 0.1 us)
Async XLA Ops:
  0.6 1.3 %copy-start = (bf16[640,1024]{1,0:T(8,128)(2,1)S(1)}, bf16[640,1024]{1,0:T(8,128)(2,1)}, u32[]{:S(2)}) copy-start(bf16[640,1024]{1,0:T(8,128)(2,1)} %param.5) | copy-start | bytes 3932164
  0.6 4.5 %copy-start.7 = (bf16[640,1024]{1,0:T(8,128)(2,1)S(1)}, bf16[640,1024]{1,0:T(8,128)(2,1)}, u32[]{:S(2)}) copy-start(bf16[640,1024]{1,0:T(8,128)(2,1)} %param.7) | copy-start | bytes 3932164
  5.1 2.1 %copy-start.2 = (f32[1,1024,1024]{2,1,0:T(8,128)}, f32[1,1024,1024]{2,1,0:T(8,128)S(1)}, u32[]{:S(2)}) copy-start(f32[1,1024,1024]{2,1,0:T(8,128)S(1)} %convolution_bitcast_fusion.1) | copy-start | bytes 12582916
  5.1 5.2 %copy-start.1 = (bf16[2,1024,1024]{2,1,0:T(8,128)(2,1)S(1)}, bf16[2,1024,1024]{2,1,0:T(8,128)(2,1)}, u32[]{:S(2)}) copy-start(bf16[2,1024,1024]{2,1,0:T(8,128)(2,1)} %param.8) | copy-start | bytes 12582916
  5.1 5.2 %copy-start.6 = (f32[2,32,1024]{2,1,0:T(8,128)S(1)}, f32[2,32,1024]{2,1,0:T(8,128)}, u32[]{:S(2)}) copy-start(f32[2,32,1024]{2,1,0:T(8,128)} %param.9) | copy-start | bytes 786436
  7.3 2.1 %copy-start.3 = (f32[1,1024,1024]{2,1,0:T(8,128)}, f32[1,1024,1024]{2,1,0:T(8,128)S(1)}, u32[]{:S(2)}) copy-start(f32[1,1024,1024]{2,1,0:T(8,128)S(1)} %convolution_bitcast_fusion) | copy-start | bytes 12582916
  68.7 34.9 %copy-start.4 = (f32[2,32,1024]{2,1,0:T(8,128)}, f32[2,32,1024]{2,1,0:T(8,128)S(1)}, u32[]{:S(2)}) copy-start(f32[2,32,1024]{2,1,0:T(8,128)S(1)} %fusion.1) | copy-start | bytes 786436
  103.6 8.3 %copy-start.5 = (f32[2,32,1024]{2,1,0:T(8,128)}, f32[2,32,1024]{2,1,0:T(8,128)S(1)}, u32[]{:S(2)}) copy-start(f32[2,32,1024]{2,1,0:T(8,128)S(1)} %broadcast_multiply_fusion) | copy-start | bytes 786436

commit v3 on v2

--- a/solution.py
+++ b/solution.py
@@ -15,7 +15,7 @@
 SUB = 8
 
 
-def allreduce_kernel(nx, ny, x_ref, o_ref, recv_a, p_t, recv_b, recv_c, recv_d,
+def allreduce_kernel(nx, ny, orthonormalize, x_ref, o_ref, recv_a, p_t, recv_b, recv_c, recv_d,
                      sa, ra, sb, rb, sc, rc, sd, rd):
     h = lax.axis_index("gx")
     a = lax.axis_index("gy")
@@ -146,16 +146,51 @@
     lax.fori_loop(1, ny, wait_d, 0)
     for s in range(ny):
         o_ref[:, :, s * LANES:(s + 1) * LANES] = recv_d[s]
-
-
-def allreduce(x, nx, ny, collective_id):
+    if orthonormalize:
+        for b in range(nb):
+            orthonormal_rows(o_ref.at[b])
+
+
+def orthonormal_rows(rows_ref):
+    k = rows_ref.shape[0]
+    rows = rows_ref[...]
+    gram = lax.dot_general(rows, rows, (((1,), (1,)), ((), ())),
+                           precision=HIGHEST, preferred_element_type=jnp.float32)
+    r_idx = lax.broadcasted_iota(jnp.int32, (k, k), 0)
+    c_idx = lax.broadcasted_iota(jnp.int32, (k, k), 1)
+    diag = r_idx == c_idx
+    trace_value = jnp.sum(jnp.where(diag, gram, 0.0))
+    shift_value = 1e-06 * (trace_value / k + 1.0)
+    work = gram + jnp.where(diag, shift_value, 0.0)
+    cols, pivots = [], []
+    for j in range(k):
+        pivot = jnp.sum(jnp.where(diag & (r_idx == j), work, 0.0))
+        root = jnp.sqrt(pivot)
+        col = jnp.sum(jnp.where(c_idx == j, work, 0.0), axis=1, keepdims=True)
+        row = jnp.sum(jnp.where(r_idx == j, work, 0.0), axis=0, keepdims=True)
+        col = jnp.where(r_idx[:, :1] >= j, col / root, 0.0)
+        row = jnp.where(c_idx[:1, :] >= j, row / root, 0.0)
+        work = work - col * row
+        cols.append(col)
+        pivots.append(root)
+    sub_idx = lax.broadcasted_iota(jnp.int32, (k, 1), 0)
+    for i in range(k):
+        solved = rows_ref[i:i + 1, :] / pivots[i]
+        rows_ref[i:i + 1, :] = solved
+        if i + 1 < k:
+            start = ((i + 1) // SUB) * SUB
+            below = jnp.where(sub_idx[start:] > i, cols[i][start:], 0.0)
+            rows_ref[start:, :] = rows_ref[start:, :] - below * solved
+
+
+def allreduce(x, nx, ny, collective_id, orthonormalize=False):
     nb, rows, cols = x.shape
     assert cols == ny * LANES and rows % SUB == 0
     nt = nb * (rows // SUB)
     assert nx % nt == 0
     vmem = pltpu.VMEM
     return pl.pallas_call(
-        functools.partial(allreduce_kernel, nx, ny),
+        functools.partial(allreduce_kernel, nx, ny, orthonormalize),
         out_shape=jax.ShapeDtypeStruct(x.shape, jnp.float32),
         in_specs=[pl.BlockSpec(memory_space=vmem)],
         out_specs=pl.BlockSpec(memory_space=vmem),
@@ -199,8 +234,7 @@
     key_grad = lax.dot_general(normed, grad_key, CONTRACT, preferred_element_type=jnp.float32)
     merged = jnp.stack([query_grad, key_grad]) + error.astype(jnp.float32)
     left_local = jnp.einsum("bkj,bij->bki", start_factor, merged, precision=HIGHEST)
-    left_total = allreduce(left_local, nx, ny, 0)
-    left_rows = solve_rows(gram_of(left_total), left_total)
+    left_rows = allreduce(left_local, nx, ny, 0, orthonormalize=True)
     right_local = jnp.einsum("bki,bij->bkj", left_rows, merged, precision=HIGH)
     right_rows = allreduce(right_local, nx, ny, 1) / replicas
     approx = jnp.einsum("bki,bkj->bij", left_rows, right_rows, precision=HIGH)

time: 112 us -> 113 us (level)
  Pallas kernels: 62.7 us -> 75.5 us
  other arithmetic: 12.1 us -> 0.97 us
  matrix products: 31.7 us -> 30.1 us
    pallas_call x2, Pallas kernels: 62.7 us -> 75.5 us  [allreduce(): pl.pallas_call(functools.partial(allreduce_kernel, nx, ny, orthonormalize...]
    another operation x7 -> x0, other arithmetic: 11 us -> none  [the longest x4 6.03 us: solve_rows(): jnp.linalg.cholesky(gram_matrix + shift_value[:, None, None] * identity)]
    dot_general x1 -> x0, matrix products: 1.48 us -> none  [gram_of(): jnp.einsum('bki,bli->bkl', factor_rows, factor_rows, precision=HIGHEST)]
    another operation x1 -> x0, matrix products: 1.39 us -> none  [solve_rows(): lax.linalg.triangular_solve(lower_factor, factor_rows, left_side=True, lo...]
    dot_general x1, matrix products: 6.84 us -> 8.13 us  [on_device(): right_local = jnp.einsum('bki,bij->bkj', left_rows, merged, precision=HIGH)]
    dot_general x1, matrix products: 1.87 us -> 3.15 us  [on_device(): lax.dot_general(normed, grad_key, CONTRACT, preferred_element_type=jnp.fl...]
    dot_general x1, matrix products: 3.15 us -> 1.87 us  [on_device(): lax.dot_general(normed, grad_query, CONTRACT, preferred_element_type=jnp....]
    unnamed x16 -> x17, local copies, waits for them, and re-layouts: 4.63 us -> 5.37 us
where the time goes in v3:
time: 113 us
  Pallas kernels  75.5 us (67%)
  matrix products  30.1 us (27%)
  local copies, waits for them, and re-layouts  5.37 us (5%)
    pallas_call x2, Pallas kernels, allreduce(): pl.pallas_call(functools.partial(allreduce_kernel, nx, ny, orthonormalize...  75.5 us
    dot_general x1, matrix products, on_device(): jnp.einsum('bkj,bij->bki', start_factor, merged, precision=HIGHEST)  8.64 us
    dot_general x1, matrix products, on_device(): approx = jnp.einsum('bki,bkj->bij', left_rows, right_rows, precision=HIGH)  8.28 us
    dot_general x1, matrix products, on_device(): right_local = jnp.einsum('bki,bij->bkj', left_rows, merged, precision=HIGH)  8.13 us
    unnamed x17, local copies, waits for them, and re-layouts  5.37 us
    dot_general x1, matrix products, on_device(): lax.dot_general(normed, grad_key, CONTRACT, preferred_element_type=jnp.fl...  3.15 us

profile of v3, /device:TPU:1, one launch (start us, length us, event | category | flops | bytes accessed | tf_op | source)
XLA Modules:
  0.0 112.6 jit_solution(6064434600601586606)
XLA Ops:
  0.6 0.0 copy-start
  0.6 0.0 copy-start.7
  0.7 1.3 %copy-done = bf16[640,1024]{1,0:T(8,128)(2,1)S(1)} copy-done((bf16[640,1024]{1,0:T(8,128)(2,1)S(1)}, bf16[640,1024]{1,0:T(8,128)(2,1)}, u32[]{:S(2)}) %copy-start) | copy-done | bytes 1310744
  2.0 3.1 %convolution_bitcast_fusion = f32[1,1024,1024]{2,1,0:T(8,128)S(1)} fusion(bf16[640,1024]{1,0:T(8,128)(2,1)S(1)} %copy-done, bf16[640,1024]{1,0:T(8,128)(2,1)} %param.7), kind=kOutput, calls=%fused_computation.2 | convolution fusion | flops 1342177280 | bytes 6815744 | tf_op jit(solution)/shard_map/dot_general | solution.py:234
  5.1 0.0 copy-done.7
  5.1 0.0 copy-start.2
  5.1 0.0 copy-start.1
  5.1 0.0 copy-start.6
  5.2 1.9 %convolution_bitcast_fusion.1 = f32[1,1024,1024]{2,1,0:T(8,128)S(1)} fusion(bf16[640,1024]{1,0:T(8,128)(2,1)S(1)} %copy-done, bf16[640,1024]{1,0:T(8,128)(2,1)S(1)} %copy-done.7), kind=kOutput, calls=%fused_computation.3 | convolution fusion | flops 1342177280 | bytes 6815744 | tf_op jit(solution)/shard_map/dot_general | solution.py:233
  7.0 0.2 copy-done.2
  7.3 2.1 %copy-done.3 = f32[1,1024,1024]{2,1,0:T(8,128)} copy-done((f32[1,1024,1024]{2,1,0:T(8,128)}, f32[1,1024,1024]{2,1,0:T(8,128)S(1)}, u32[]{:S(2)}) %copy-start.3) | copy-done | bytes 4194328
  9.4 1.0 copy-done.1
  10.4 0.0 copy-done.6
  10.4 8.6 %convolution_bitcast_fusion.2.x_ref = f32[2,32,1024]{2,1,0:T(8,128)} fusion(f32[2,32,1024]{2,1,0:T(8,128)S(1)} %copy-done.6, f32[1,1024,1024]{2,1,0:T(8,128)S(1)} %convolution_bitcast_fusion, f32[1,1024,1024]{2,1,0:T(8,128)S(1)} %convolution_bitcast_fusion.1, bf16[2,1024,1024]{2,1,0:T(8,128)(2,1)S(1)} %copy-done.1), kind=kOutput, calls=%fused_computation.4 | convolution fusion | flops 811597824 | bytes 13107200 | tf_op jit(solution)/shard_map/bkj,bij->bki/dot_general | solution.py:236
  19.0 48.4 %shard_map.76 = f32[2,32,1024]{2,1,0:T(8,128)} custom-call(f32[2,32,1024]{2,1,0:T(8,128)} %convolution_bitcast_fusion.2.x_ref), custom_call_target="tpu_custom_call" | custom-call | tf_op jit(solution)/shard_map/pallas_call | solution.py:192
  67.4 0.0 copy-start.4
  67.4 8.1 %fusion.x_ref = f32[2,32,1024]{2,1,0:T(8,128)} fusion(f32[2,32,1024]{2,1,0:T(8,128)} %shard_map.76, f32[1,1024,1024]{2,1,0:T(8,128)} %copy-done.2, f32[1,1024,1024]{2,1,0:T(8,128)} %copy-done.3, bf16[2,1024,1024]{2,1,0:T(8,128)(2,1)} %param.8), kind=kOutput, calls=%fused_computation.5 | convolution fusion | flops 408944640 | bytes 13107200 | tf_op jit(solution)/shard_map/bki,bij->bkj/dot_general | solution.py:238
  75.5 27.1 %shard_map.77 = f32[2,32,1024]{2,1,0:T(8,128)} custom-call(f32[2,32,1024]{2,1,0:T(8,128)} %fusion.x_ref), custom_call_target="tpu_custom_call" | custom-call | tf_op jit(solution)/shard_map/pallas_call | solution.py:192
  102.6 1.0 broadcast_multiply_fusion
  103.6 0.0 copy-done.4
  103.6 0.0 copy-start.5
  103.6 8.3 %subtract_convert_fusion = bf16[2,1024,1024]{2,1,0:T(8,128)(2,1)} fusion(f32[2,32,1024]{2,1,0:T(8,128)S(1)} %copy-done.4, f32[2,32,1024]{2,1,0:T(8,128)S(1)} %broadcast_multiply_fusion, bf16[2,1024,1024]{2,1,0:T(8,128)(2,1)} %param.8, f32[1,1024,1024]{2,1,0:T(8,128)} %copy-done.2, f32[1,1024,1024]{2,1,0:T(8,128)} %copy-done.3), kind=kOutput, calls=%fused_computation.1 | convolution fusion | flops 413138944 | bytes 17301504 | tf_op jit(solution)/shard_map/bki,bkj->bij/dot_general | solution.py:240
  111.9 0.0 copy-done.5
  111.9 0.7 copy.9
  (1 shorter events, 0.0 us)
Async XLA Ops:
  0.6 1.3 %copy-start = (bf16[640,1024]{1,0:T(8,128)(2,1)S(1)}, bf16[640,1024]{1,0:T(8,128)(2,1)}, u32[]{:S(2)}) copy-start(bf16[640,1024]{1,0:T(8,128)(2,1)} %param.5) | copy-start | bytes 3932164
  0.6 4.5 %copy-start.7 = (bf16[640,1024]{1,0:T(8,128)(2,1)S(1)}, bf16[640,1024]{1,0:T(8,128)(2,1)}, u32[]{:S(2)}) copy-start(bf16[640,1024]{1,0:T(8,128)(2,1)} %param.6) | copy-start | bytes 3932164
  5.1 2.1 %copy-start.2 = (f32[1,1024,1024]{2,1,0:T(8,128)}, f32[1,1024,1024]{2,1,0:T(8,128)S(1)}, u32[]{:S(2)}) copy-start(f32[1,1024,1024]{2,1,0:T(8,128)S(1)} %convolution_bitcast_fusion) | copy-start | bytes 12582916
  5.1 5.2 %copy-start.1 = (bf16[2,1024,1024]{2,1,0:T(8,128)(2,1)S(1)}, bf16[2,1024,1024]{2,1,0:T(8,128)(2,1)}, u32[]{:S(2)}) copy-start(bf16[2,1024,1024]{2,1,0:T(8,128)(2,1)} %param.8) | copy-start | bytes 12582916
  5.1 5.2 %copy-start.6 = (f32[2,32,1024]{2,1,0:T(8,128)S(1)}, f32[2,32,1024]{2,1,0:T(8,128)}, u32[]{:S(2)}) copy-start(f32[2,32,1024]{2,1,0:T(8,128)} %param.9) | copy-start | bytes 786436
  7.3 2.1 %copy-start.3 = (f32[1,1024,1024]{2,1,0:T(8,128)}, f32[1,1024,1024]{2,1,0:T(8,128)S(1)}, u32[]{:S(2)}) copy-start(f32[1,1024,1024]{2,1,0:T(8,128)S(1)} %convolution_bitcast_fusion.1) | copy-start | bytes 12582916
  67.4 36.2 %copy-start.4 = (f32[2,32,1024]{2,1,0:T(8,128)S(1)}, f32[2,32,1024]{2,1,0:T(8,128)}, u32[]{:S(2)}) copy-start(f32[2,32,1024]{2,1,0:T(8,128)} %shard_map.76) | copy-start | bytes 786436
  103.6 8.3 %copy-start.5 = (f32[2,32,1024]{2,1,0:T(8,128)}, f32[2,32,1024]{2,1,0:T(8,128)S(1)}, u32[]{:S(2)}) copy-start(f32[2,32,1024]{2,1,0:T(8,128)S(1)} %broadcast_multiply_fusion) | copy-start | bytes 786436

commit v4 on v3

--- a/solution.py
+++ b/solution.py
@@ -162,25 +162,20 @@
     trace_value = jnp.sum(jnp.where(diag, gram, 0.0))
     shift_value = 1e-06 * (trace_value / k + 1.0)
     work = gram + jnp.where(diag, shift_value, 0.0)
-    cols, pivots = [], []
+    sub_idx = r_idx[:, :1]
+    inverse = jnp.where(diag, 1.0, 0.0)
     for j in range(k):
-        pivot = jnp.sum(jnp.where(diag & (r_idx == j), work, 0.0))
-        root = jnp.sqrt(pivot)
+        row = work[j:j + 1, :]
+        root = jnp.sqrt(row[:, j:j + 1])
         col = jnp.sum(jnp.where(c_idx == j, work, 0.0), axis=1, keepdims=True)
-        row = jnp.sum(jnp.where(r_idx == j, work, 0.0), axis=0, keepdims=True)
-        col = jnp.where(r_idx[:, :1] >= j, col / root, 0.0)
+        col = jnp.where(sub_idx >= j, col / root, 0.0)
         row = jnp.where(c_idx[:1, :] >= j, row / root, 0.0)
         work = work - col * row
-        cols.append(col)
-        pivots.append(root)
-    sub_idx = lax.broadcasted_iota(jnp.int32, (k, 1), 0)
-    for i in range(k):
-        solved = rows_ref[i:i + 1, :] / pivots[i]
-        rows_ref[i:i + 1, :] = solved
-        if i + 1 < k:
-            start = ((i + 1) // SUB) * SUB
-            below = jnp.where(sub_idx[start:] > i, cols[i][start:], 0.0)
-            rows_ref[start:, :] = rows_ref[start:, :] - below * solved
+        solved = inverse[j:j + 1, :] / root
+        below = jnp.where(sub_idx > j, col, 0.0)
+        inverse = jnp.where(sub_idx == j, solved, inverse - below * solved)
+    rows_ref[...] = jnp.dot(inverse, rows, precision=HIGHEST,
+                            preferred_element_type=jnp.float32)
 
 
 def allreduce(x, nx, ny, collective_id, orthonormalize=False):

time: 113 us -> 111 us (0.982)
  Pallas kernels: 75.5 us -> 73.3 us
    pallas_call x2, Pallas kernels: 75.5 us -> 73.3 us  [allreduce(): pl.pallas_call(functools.partial(allreduce_kernel, nx, ny, orthonormalize...]
where the time goes in v4:
time: 111 us
  Pallas kernels  73.3 us (66%)
  matrix products  30.1 us (27%)
  local copies, waits for them, and re-layouts  5.37 us (5%)
    pallas_call x2, Pallas kernels, allreduce(): pl.pallas_call(functools.partial(allreduce_kernel, nx, ny, orthonormalize...  73.3 us
    dot_general x1, matrix products, on_device(): jnp.einsum('bkj,bij->bki', start_factor, merged, precision=HIGHEST)  8.64 us
    dot_general x1, matrix products, on_device(): approx = jnp.einsum('bki,bkj->bij', left_rows, right_rows, precision=HIGH)  8.28 us
    dot_general x1, matrix products, on_device(): right_local = jnp.einsum('bki,bij->bkj', left_rows, merged, precision=HIGH)  8.13 us
    unnamed x17, local copies, waits for them, and re-layouts  5.37 us
    dot_general x1, matrix products, on_device(): lax.dot_general(normed, grad_key, CONTRACT, preferred_element_type=jnp.fl...  3.15 us

profile of v4, /device:TPU:1, one launch (start us, length us, event | category | flops | bytes accessed | tf_op | source)
XLA Modules:
  0.0 110.5 jit_solution(17233840536522293846)
XLA Ops:
  0.6 0.0 copy-start
  0.6 0.0 copy-start.7
  0.7 1.3 %copy-done = bf16[640,1024]{1,0:T(8,128)(2,1)S(1)} copy-done((bf16[640,1024]{1,0:T(8,128)(2,1)S(1)}, bf16[640,1024]{1,0:T(8,128)(2,1)}, u32[]{:S(2)}) %copy-start) | copy-done | bytes 1310744
  2.0 3.1 %convolution_bitcast_fusion = f32[1,1024,1024]{2,1,0:T(8,128)S(1)} fusion(bf16[640,1024]{1,0:T(8,128)(2,1)S(1)} %copy-done, bf16[640,1024]{1,0:T(8,128)(2,1)} %param.7), kind=kOutput, calls=%fused_computation.2 | convolution fusion | flops 1342177280 | bytes 6815744 | tf_op jit(solution)/shard_map/dot_general | solution.py:229
  5.1 0.0 copy-done.7
  5.1 0.0 copy-start.2
  5.1 0.0 copy-start.1
  5.1 0.0 copy-start.6
  5.2 1.9 %convolution_bitcast_fusion.1 = f32[1,1024,1024]{2,1,0:T(8,128)S(1)} fusion(bf16[640,1024]{1,0:T(8,128)(2,1)S(1)} %copy-done, bf16[640,1024]{1,0:T(8,128)(2,1)S(1)} %copy-done.7), kind=kOutput, calls=%fused_computation.3 | convolution fusion | flops 1342177280 | bytes 6815744 | tf_op jit(solution)/shard_map/dot_general | solution.py:228
  7.0 0.2 copy-done.2
  7.3 2.1 %copy-done.3 = f32[1,1024,1024]{2,1,0:T(8,128)} copy-done((f32[1,1024,1024]{2,1,0:T(8,128)}, f32[1,1024,1024]{2,1,0:T(8,128)S(1)}, u32[]{:S(2)}) %copy-start.3) | copy-done | bytes 4194328
  9.4 1.0 copy-done.1
  10.4 0.0 copy-done.6
  10.4 8.6 %convolution_bitcast_fusion.2.x_ref = f32[2,32,1024]{2,1,0:T(8,128)} fusion(f32[2,32,1024]{2,1,0:T(8,128)S(1)} %copy-done.6, f32[1,1024,1024]{2,1,0:T(8,128)S(1)} %convolution_bitcast_fusion, f32[1,1024,1024]{2,1,0:T(8,128)S(1)} %convolution_bitcast_fusion.1, bf16[2,1024,1024]{2,1,0:T(8,128)(2,1)S(1)} %copy-done.1), kind=kOutput, calls=%fused_computation.4 | convolution fusion | flops 811597824 | bytes 13107200 | tf_op jit(solution)/shard_map/bkj,bij->bki/dot_general | solution.py:231
  19.0 46.3 %shard_map.76 = f32[2,32,1024]{2,1,0:T(8,128)} custom-call(f32[2,32,1024]{2,1,0:T(8,128)} %convolution_bitcast_fusion.2.x_ref), custom_call_target="tpu_custom_call" | custom-call | tf_op jit(solution)/shard_map/pallas_call | solution.py:187
  65.3 0.0 copy-start.4
  65.3 8.1 %fusion.x_ref = f32[2,32,1024]{2,1,0:T(8,128)} fusion(f32[2,32,1024]{2,1,0:T(8,128)} %shard_map.76, f32[1,1024,1024]{2,1,0:T(8,128)} %copy-done.2, f32[1,1024,1024]{2,1,0:T(8,128)} %copy-done.3, bf16[2,1024,1024]{2,1,0:T(8,128)(2,1)} %param.8), kind=kOutput, calls=%fused_computation.5 | convolution fusion | flops 408944640 | bytes 13107200 | tf_op jit(solution)/shard_map/bki,bij->bkj/dot_general | solution.py:233
  73.4 27.1 %shard_map.77 = f32[2,32,1024]{2,1,0:T(8,128)} custom-call(f32[2,32,1024]{2,1,0:T(8,128)} %fusion.x_ref), custom_call_target="tpu_custom_call" | custom-call | tf_op jit(solution)/shard_map/pallas_call | solution.py:187
  100.5 1.0 broadcast_multiply_fusion
  101.5 0.0 copy-done.4
  101.5 0.0 copy-start.5
  101.5 8.3 %subtract_convert_fusion = bf16[2,1024,1024]{2,1,0:T(8,128)(2,1)} fusion(f32[2,32,1024]{2,1,0:T(8,128)S(1)} %copy-done.4, f32[2,32,1024]{2,1,0:T(8,128)S(1)} %broadcast_multiply_fusion, bf16[2,1024,1024]{2,1,0:T(8,128)(2,1)} %param.8, f32[1,1024,1024]{2,1,0:T(8,128)} %copy-done.2, f32[1,1024,1024]{2,1,0:T(8,128)} %copy-done.3), kind=kOutput, calls=%fused_computation.1 | convolution fusion | flops 413138944 | bytes 17301504 | tf_op jit(solution)/shard_map/bki,bkj->bij/dot_general | solution.py:235
  109.8 0.0 copy-done.5
  109.8 0.7 copy.9
  (1 shorter events, 0.0 us)
Async XLA Ops:
  0.6 1.3 %copy-start = (bf16[640,1024]{1,0:T(8,128)(2,1)S(1)}, bf16[640,1024]{1,0:T(8,128)(2,1)}, u32[]{:S(2)}) copy-start(bf16[640,1024]{1,0:T(8,128)(2,1)} %param.5) | copy-start | bytes 3932164
  0.6 4.5 %copy-start.7 = (bf16[640,1024]{1,0:T(8,128)(2,1)S(1)}, bf16[640,1024]{1,0:T(8,128)(2,1)}, u32[]{:S(2)}) copy-start(bf16[640,1024]{1,0:T(8,128)(2,1)} %param.6) | copy-start | bytes 3932164
  5.1 2.1 %copy-start.2 = (f32[1,1024,1024]{2,1,0:T(8,128)}, f32[1,1024,1024]{2,1,0:T(8,128)S(1)}, u32[]{:S(2)}) copy-start(f32[1,1024,1024]{2,1,0:T(8,128)S(1)} %convolution_bitcast_fusion) | copy-start | bytes 12582916
  5.1 5.2 %copy-start.1 = (bf16[2,1024,1024]{2,1,0:T(8,128)(2,1)S(1)}, bf16[2,1024,1024]{2,1,0:T(8,128)(2,1)}, u32[]{:S(2)}) copy-start(bf16[2,1024,1024]{2,1,0:T(8,128)(2,1)} %param.8) | copy-start | bytes 12582916
  5.1 5.2 %copy-start.6 = (f32[2,32,1024]{2,1,0:T(8,128)S(1)}, f32[2,32,1024]{2,1,0:T(8,128)}, u32[]{:S(2)}) copy-start(f32[2,32,1024]{2,1,0:T(8,128)} %param.9) | copy-start | bytes 786436
  7.3 2.1 %copy-start.3 = (f32[1,1024,1024]{2,1,0:T(8,128)}, f32[1,1024,1024]{2,1,0:T(8,128)S(1)}, u32[]{:S(2)}) copy-start(f32[1,1024,1024]{2,1,0:T(8,128)S(1)} %convolution_bitcast_fusion.1) | copy-start | bytes 12582916
  65.3 36.2 %copy-start.4 = (f32[2,32,1024]{2,1,0:T(8,128)S(1)}, f32[2,32,1024]{2,1,0:T(8,128)}, u32[]{:S(2)}) copy-start(f32[2,32,1024]{2,1,0:T(8,128)} %shard_map.76) | copy-start | bytes 786436
  101.5 8.3 %copy-start.5 = (f32[2,32,1024]{2,1,0:T(8,128)}, f32[2,32,1024]{2,1,0:T(8,128)S(1)}, u32[]{:S(2)}) copy-start(f32[2,32,1024]{2,1,0:T(8,128)S(1)} %broadcast_multiply_fusion) | copy-start | bytes 786436

commit v5 on v4

--- a/solution.py
+++ b/solution.py
@@ -147,35 +147,38 @@
     for s in range(ny):
         o_ref[:, :, s * LANES:(s + 1) * LANES] = recv_d[s]
     if orthonormalize:
-        for b in range(nb):
-            orthonormal_rows(o_ref.at[b])
+        orthonormal_rows(o_ref)
 
 
 def orthonormal_rows(rows_ref):
-    k = rows_ref.shape[0]
-    rows = rows_ref[...]
-    gram = lax.dot_general(rows, rows, (((1,), (1,)), ((), ())),
-                           precision=HIGHEST, preferred_element_type=jnp.float32)
-    r_idx = lax.broadcasted_iota(jnp.int32, (k, k), 0)
-    c_idx = lax.broadcasted_iota(jnp.int32, (k, k), 1)
+    nb, k = rows_ref.shape[0], rows_ref.shape[1]
+    gram = jnp.stack([
+        lax.dot_general(rows_ref[b], rows_ref[b], (((1,), (1,)), ((), ())),
+                        precision=HIGHEST, preferred_element_type=jnp.float32)
+        for b in range(nb)
+    ])
+    r_idx = lax.broadcasted_iota(jnp.int32, (nb, k, k), 1)
+    c_idx = lax.broadcasted_iota(jnp.int32, (nb, k, k), 2)
     diag = r_idx == c_idx
-    trace_value = jnp.sum(jnp.where(diag, gram, 0.0))
+    trace_value = jnp.sum(jnp.sum(jnp.where(diag, gram, 0.0), axis=2, keepdims=True),
+                          axis=1, keepdims=True)
     shift_value = 1e-06 * (trace_value / k + 1.0)
     work = gram + jnp.where(diag, shift_value, 0.0)
-    sub_idx = r_idx[:, :1]
+    sub_idx = r_idx[:, :, :1]
+    lane_idx = c_idx[:, :1, :]
     inverse = jnp.where(diag, 1.0, 0.0)
     for j in range(k):
-        row = work[j:j + 1, :]
-        root = jnp.sqrt(row[:, j:j + 1])
-        col = jnp.sum(jnp.where(c_idx == j, work, 0.0), axis=1, keepdims=True)
-        col = jnp.where(sub_idx >= j, col / root, 0.0)
-        row = jnp.where(c_idx[:1, :] >= j, row / root, 0.0)
+        row = work[:, j:j + 1, :]
+        inv_root = lax.rsqrt(row[:, :, j:j + 1])
+        col = jnp.where(sub_idx >= j, work[:, :, j:j + 1] * inv_root, 0.0)
+        row = jnp.where(lane_idx >= j, row * inv_root, 0.0)
         work = work - col * row
-        solved = inverse[j:j + 1, :] / root
+        solved = inverse[:, j:j + 1, :] * inv_root
         below = jnp.where(sub_idx > j, col, 0.0)
         inverse = jnp.where(sub_idx == j, solved, inverse - below * solved)
-    rows_ref[...] = jnp.dot(inverse, rows, precision=HIGHEST,
-                            preferred_element_type=jnp.float32)
+    for b in range(nb):
+        rows_ref[b] = jnp.dot(inverse[b], rows_ref[b], precision=HIGHEST,
+                              preferred_element_type=jnp.float32)
 
 
 def allreduce(x, nx, ny, collective_id, orthonormalize=False):

time: 111 us -> 104 us (0.937)
  Pallas kernels: 73.3 us -> 66.2 us
    pallas_call x2, Pallas kernels: 73.3 us -> 66.2 us  [allreduce(): pl.pallas_call(functools.partial(allreduce_kernel, nx, ny, orthonormalize...]
where the time goes in v5:
time: 104 us; the launch traced here: 103 us
  Pallas kernels  66.2 us (64%)
  matrix products  30.1 us (29%)
  local copies, waits for them, and re-layouts  5.37 us (5%)
    pallas_call x2, Pallas kernels, allreduce(): pl.pallas_call(functools.partial(allreduce_kernel, nx, ny, orthonormalize...  66.2 us
    dot_general x1, matrix products, on_device(): jnp.einsum('bkj,bij->bki', start_factor, merged, precision=HIGHEST)  8.64 us
    dot_general x1, matrix products, on_device(): approx = jnp.einsum('bki,bkj->bij', left_rows, right_rows, precision=HIGH)  8.29 us
    dot_general x1, matrix products, on_device(): right_local = jnp.einsum('bki,bij->bkj', left_rows, merged, precision=HIGH)  8.13 us
    unnamed x17, local copies, waits for them, and re-layouts  5.37 us
    dot_general x1, matrix products, on_device(): lax.dot_general(normed, grad_key, CONTRACT, preferred_element_type=jnp.fl...  3.15 us

profile of v5, /device:TPU:1, one launch (start us, length us, event | category | flops | bytes accessed | tf_op | source)
XLA Modules:
  0.0 103.4 jit_solution(10889419403198271158)
XLA Ops:
  0.6 0.0 copy-start
  0.6 0.0 copy-start.7
  0.7 1.3 %copy-done = bf16[640,1024]{1,0:T(8,128)(2,1)S(1)} copy-done((bf16[640,1024]{1,0:T(8,128)(2,1)S(1)}, bf16[640,1024]{1,0:T(8,128)(2,1)}, u32[]{:S(2)}) %copy-start) | copy-done | bytes 1310744
  2.0 3.1 %convolution_bitcast_fusion = f32[1,1024,1024]{2,1,0:T(8,128)S(1)} fusion(bf16[640,1024]{1,0:T(8,128)(2,1)S(1)} %copy-done, bf16[640,1024]{1,0:T(8,128)(2,1)} %param.7), kind=kOutput, calls=%fused_computation.2 | convolution fusion | flops 1342177280 | bytes 6815744 | tf_op jit(solution)/shard_map/dot_general | solution.py:232
  5.1 0.0 copy-done.7
  5.1 0.0 copy-start.2
  5.1 0.0 copy-start.1
  5.1 0.0 copy-start.6
  5.2 1.9 %convolution_bitcast_fusion.1 = f32[1,1024,1024]{2,1,0:T(8,128)S(1)} fusion(bf16[640,1024]{1,0:T(8,128)(2,1)S(1)} %copy-done, bf16[640,1024]{1,0:T(8,128)(2,1)S(1)} %copy-done.7), kind=kOutput, calls=%fused_computation.3 | convolution fusion | flops 1342177280 | bytes 6815744 | tf_op jit(solution)/shard_map/dot_general | solution.py:231
  7.0 0.2 copy-done.2
  7.3 2.1 %copy-done.3 = f32[1,1024,1024]{2,1,0:T(8,128)} copy-done((f32[1,1024,1024]{2,1,0:T(8,128)}, f32[1,1024,1024]{2,1,0:T(8,128)S(1)}, u32[]{:S(2)}) %copy-start.3) | copy-done | bytes 4194328
  9.4 1.0 copy-done.1
  10.4 0.0 copy-done.6
  10.4 8.6 %convolution_bitcast_fusion.2.x_ref = f32[2,32,1024]{2,1,0:T(8,128)} fusion(f32[2,32,1024]{2,1,0:T(8,128)S(1)} %copy-done.6, f32[1,1024,1024]{2,1,0:T(8,128)S(1)} %convolution_bitcast_fusion, f32[1,1024,1024]{2,1,0:T(8,128)S(1)} %convolution_bitcast_fusion.1, bf16[2,1024,1024]{2,1,0:T(8,128)(2,1)S(1)} %copy-done.1), kind=kOutput, calls=%fused_computation.4 | convolution fusion | flops 811597824 | bytes 13107200 | tf_op jit(solution)/shard_map/bkj,bij->bki/dot_general | solution.py:234
  19.0 39.1 %shard_map.76 = f32[2,32,1024]{2,1,0:T(8,128)} custom-call(f32[2,32,1024]{2,1,0:T(8,128)} %convolution_bitcast_fusion.2.x_ref), custom_call_target="tpu_custom_call" | custom-call | tf_op jit(solution)/shard_map/pallas_call | solution.py:190
  58.2 0.0 copy-start.4
  58.2 8.1 %fusion.x_ref = f32[2,32,1024]{2,1,0:T(8,128)} fusion(f32[2,32,1024]{2,1,0:T(8,128)} %shard_map.76, f32[1,1024,1024]{2,1,0:T(8,128)} %copy-done.2, f32[1,1024,1024]{2,1,0:T(8,128)} %copy-done.3, bf16[2,1024,1024]{2,1,0:T(8,128)(2,1)} %param.8), kind=kOutput, calls=%fused_computation.5 | convolution fusion | flops 408944640 | bytes 13107200 | tf_op jit(solution)/shard_map/bki,bij->bkj/dot_general | solution.py:236
  66.3 27.1 %shard_map.77 = f32[2,32,1024]{2,1,0:T(8,128)} custom-call(f32[2,32,1024]{2,1,0:T(8,128)} %fusion.x_ref), custom_call_target="tpu_custom_call" | custom-call | tf_op jit(solution)/shard_map/pallas_call | solution.py:190
  93.4 1.0 broadcast_multiply_fusion
  94.4 0.0 copy-done.4
  94.4 0.0 copy-start.5
  94.4 8.3 %subtract_convert_fusion = bf16[2,1024,1024]{2,1,0:T(8,128)(2,1)} fusion(f32[2,32,1024]{2,1,0:T(8,128)S(1)} %copy-done.4, f32[2,32,1024]{2,1,0:T(8,128)S(1)} %broadcast_multiply_fusion, bf16[2,1024,1024]{2,1,0:T(8,128)(2,1)} %param.8, f32[1,1024,1024]{2,1,0:T(8,128)} %copy-done.2, f32[1,1024,1024]{2,1,0:T(8,128)} %copy-done.3), kind=kOutput, calls=%fused_computation.1 | convolution fusion | flops 413138944 | bytes 17301504 | tf_op jit(solution)/shard_map/bki,bkj->bij/dot_general | solution.py:238
  102.7 0.0 copy-done.5
  102.7 0.7 copy.9
  (1 shorter events, 0.0 us)
Async XLA Ops:
  0.6 1.3 %copy-start = (bf16[640,1024]{1,0:T(8,128)(2,1)S(1)}, bf16[640,1024]{1,0:T(8,128)(2,1)}, u32[]{:S(2)}) copy-start(bf16[640,1024]{1,0:T(8,128)(2,1)} %param.5) | copy-start | bytes 3932164
  0.6 4.5 %copy-start.7 = (bf16[640,1024]{1,0:T(8,128)(2,1)S(1)}, bf16[640,1024]{1,0:T(8,128)(2,1)}, u32[]{:S(2)}) copy-start(bf16[640,1024]{1,0:T(8,128)(2,1)} %param.6) | copy-start | bytes 3932164
  5.1 2.1 %copy-start.2 = (f32[1,1024,1024]{2,1,0:T(8,128)}, f32[1,1024,1024]{2,1,0:T(8,128)S(1)}, u32[]{:S(2)}) copy-start(f32[1,1024,1024]{2,1,0:T(8,128)S(1)} %convolution_bitcast_fusion) | copy-start | bytes 12582916
  5.1 5.2 %copy-start.1 = (bf16[2,1024,1024]{2,1,0:T(8,128)(2,1)S(1)}, bf16[2,1024,1024]{2,1,0:T(8,128)(2,1)}, u32[]{:S(2)}) copy-start(bf16[2,1024,1024]{2,1,0:T(8,128)(2,1)} %param.8) | copy-start | bytes 12582916
  5.1 5.2 %copy-start.6 = (f32[2,32,1024]{2,1,0:T(8,128)S(1)}, f32[2,32,1024]{2,1,0:T(8,128)}, u32[]{:S(2)}) copy-start(f32[2,32,1024]{2,1,0:T(8,128)} %param.9) | copy-start | bytes 786436
  7.3 2.1 %copy-start.3 = (f32[1,1024,1024]{2,1,0:T(8,128)}, f32[1,1024,1024]{2,1,0:T(8,128)S(1)}, u32[]{:S(2)}) copy-start(f32[1,1024,1024]{2,1,0:T(8,128)S(1)} %convolution_bitcast_fusion.1) | copy-start | bytes 12582916
  58.2 36.2 %copy-start.4 = (f32[2,32,1024]{2,1,0:T(8,128)S(1)}, f32[2,32,1024]{2,1,0:T(8,128)}, u32[]{:S(2)}) copy-start(f32[2,32,1024]{2,1,0:T(8,128)} %shard_map.76) | copy-start | bytes 786436
  94.4 8.3 %copy-start.5 = (f32[2,32,1024]{2,1,0:T(8,128)}, f32[2,32,1024]{2,1,0:T(8,128)S(1)}, u32[]{:S(2)}) copy-start(f32[2,32,1024]{2,1,0:T(8,128)S(1)} %broadcast_multiply_fusion) | copy-start | bytes 786436

commit v6 on v5

--- a/solution.py
+++ b/solution.py
@@ -15,8 +15,8 @@
 SUB = 8
 
 
-def allreduce_kernel(nx, ny, orthonormalize, x_ref, o_ref, recv_a, p_t, recv_b, recv_c, recv_d,
-                     sa, ra, sb, rb, sc, rc, sd, rd):
+def allreduce_kernel(nx, ny, orthonormalize, divisor, x_ref, o_ref, recv_a, p_t, recv_b, q_t,
+                     final, sa, ra, sb, rb, se, re):
     h = lax.axis_index("gx")
     a = lax.axis_index("gy")
     nb, rows = x_ref.shape[0], x_ref.shape[1]
@@ -35,9 +35,20 @@
                             device_id_type=MESH_ID)
         return carry
 
+    own = lax.rem(h, nt)
+    base = h - own
+
+    def signal_xy(i, carry):
+        peer_x = base + lax.rem(own + 1 + i // (ny - 1), nt)
+        peer_y = lax.rem(a + 1 + lax.rem(i, ny - 1), ny)
+        pl.semaphore_signal(barrier, 1, device_id=(peer_x, peer_y),
+                            device_id_type=MESH_ID)
+        return carry
+
     lax.fori_loop(1, ny, signal_y, 0)
     lax.fori_loop(1, nx, signal_x, 0)
-    pl.semaphore_wait(barrier, (ny - 1) + (nx - 1))
+    lax.fori_loop(0, (nt - 1) * (ny - 1), signal_xy, 0)
+    pl.semaphore_wait(barrier, (ny - 1) + (nx - 1) + (nt - 1) * (ny - 1))
 
     def copy_a(peer, slot_src):
         return pltpu.make_async_remote_copy(
@@ -82,7 +93,6 @@
         return carry
 
     lax.fori_loop(1, nx, start_b, 0)
-    own = lax.rem(h, nt)
     recv_b[h] = p_t[own]
 
     def wait_b(j, carry):
@@ -92,60 +102,41 @@
         return carry
 
     lax.fori_loop(1, nx, wait_b, 0)
-    recv_c[own] = jnp.sum(recv_b[...], axis=0)
-
-    base = h - own
-
-    def copy_c(peer_tile, slot_tile):
+    q_t[...] = jnp.sum(recv_b[...], axis=0)
+
+    block = nt * ny
+    mine = a * nt + own
+
+    def copy_e(dest, slot):
         return pltpu.make_async_remote_copy(
-            src_ref=recv_c.at[slot_tile],
-            dst_ref=recv_c.at[slot_tile],
-            send_sem=sc.at[peer_tile],
-            recv_sem=rc.at[slot_tile],
-            device_id=(base + peer_tile, a),
+            src_ref=q_t,
+            dst_ref=final.at[slot // nt, lax.rem(slot, nt)],
+            send_sem=se.at[dest],
+            recv_sem=re.at[slot],
+            device_id=(base + lax.rem(dest, nt), dest // nt),
             device_id_type=MESH_ID,
         )
 
-    def start_c(j, carry):
-        copy_c(lax.rem(own + j, nt), own).start()
-        return carry
-
-    lax.fori_loop(1, nt, start_c, 0)
-
-    def wait_c(j, carry):
-        other = lax.rem(own + j, nt)
-        copy_c(other, own).wait_send()
-        copy_c(own, other).wait_recv()
-        return carry
-
-    lax.fori_loop(1, nt, wait_c, 0)
-    for u in range(nt):
-        recv_d[a, u // kb, (u % kb) * SUB:(u % kb + 1) * SUB, :] = recv_c[u]
-
-    def copy_d(peer, slot_src):
-        return pltpu.make_async_remote_copy(
-            src_ref=recv_d.at[slot_src],
-            dst_ref=recv_d.at[slot_src],
-            send_sem=sd.at[peer],
-            recv_sem=rd.at[slot_src],
-            device_id=(h, peer),
-            device_id_type=MESH_ID,
-        )
-
-    def start_d(j, carry):
-        copy_d(lax.rem(a + j, ny), a).start()
-        return carry
-
-    lax.fori_loop(1, ny, start_d, 0)
-
-    def wait_d(j, carry):
-        copy_d(lax.rem(a + j, ny), a).wait_send()
-        copy_d(a, lax.rem(a + j, ny)).wait_recv()
-        return carry
-
-    lax.fori_loop(1, ny, wait_d, 0)
+    def start_e(i, carry):
+        copy_e(lax.rem(mine + i, block), mine).start()
+        return carry
+
+    lax.fori_loop(1, block, start_e, 0)
+    final[a, own] = q_t[...]
+
+    def wait_e(i, carry):
+        other = lax.rem(mine + i, block)
+        copy_e(other, mine).wait_send()
+        copy_e(mine, other).wait_recv()
+        return carry
+
+    lax.fori_loop(1, block, wait_e, 0)
     for s in range(ny):
-        o_ref[:, :, s * LANES:(s + 1) * LANES] = recv_d[s]
+        for u in range(nt):
+            tile = final[s, u]
+            if divisor is not None:
+                tile = tile / divisor
+            o_ref[u // kb, (u % kb) * SUB:(u % kb + 1) * SUB, s * LANES:(s + 1) * LANES] = tile
     if orthonormalize:
         orthonormal_rows(o_ref)
 
@@ -181,14 +172,14 @@
                               preferred_element_type=jnp.float32)
 
 
-def allreduce(x, nx, ny, collective_id, orthonormalize=False):
+def allreduce(x, nx, ny, collective_id, orthonormalize=False, divisor=None):
     nb, rows, cols = x.shape
     assert cols == ny * LANES and rows % SUB == 0
     nt = nb * (rows // SUB)
     assert nx % nt == 0
     vmem = pltpu.VMEM
     return pl.pallas_call(
-        functools.partial(allreduce_kernel, nx, ny, orthonormalize),
+        functools.partial(allreduce_kernel, nx, ny, orthonormalize, divisor),
         out_shape=jax.ShapeDtypeStruct(x.shape, jnp.float32),
         in_specs=[pl.BlockSpec(memory_space=vmem)],
         out_specs=pl.BlockSpec(memory_space=vmem),
@@ -196,16 +187,14 @@
             vmem((ny, nb, rows, LANES), jnp.float32),
             vmem((nt, SUB, LANES), jnp.float32),
             vmem((nx, SUB, LANES), jnp.float32),
-            vmem((nt, SUB, LANES), jnp.float32),
-            vmem((ny, nb, rows, LANES), jnp.float32),
+            vmem((SUB, LANES), jnp.float32),
+            vmem((ny, nt, SUB, LANES), jnp.float32),
             pltpu.SemaphoreType.DMA((ny,)),
             pltpu.SemaphoreType.DMA((ny,)),
             pltpu.SemaphoreType.DMA((nx,)),
             pltpu.SemaphoreType.DMA((nx,)),
-            pltpu.SemaphoreType.DMA((nt,)),
-            pltpu.SemaphoreType.DMA((nt,)),
-            pltpu.SemaphoreType.DMA((ny,)),
-            pltpu.SemaphoreType.DMA((ny,)),
+            pltpu.SemaphoreType.DMA((nt * ny,)),
+            pltpu.SemaphoreType.DMA((nt * ny,)),
         ],
         compiler_params=pltpu.CompilerParams(
             collective_id=collective_id, has_side_effects=True
@@ -234,7 +223,7 @@
     left_local = jnp.einsum("bkj,bij->bki", start_factor, merged, precision=HIGHEST)
     left_rows = allreduce(left_local, nx, ny, 0, orthonormalize=True)
     right_local = jnp.einsum("bki,bij->bkj", left_rows, merged, precision=HIGH)
-    right_rows = allreduce(right_local, nx, ny, 1) / replicas
+    right_rows = allreduce(right_local, nx, ny, 1, divisor=float(replicas))
     approx = jnp.einsum("bki,bkj->bij", left_rows, right_rows, precision=HIGH)
     return ((merged - approx).astype(jnp.bfloat16), left_rows, right_rows)
 

time: 104 us -> 109 us (1.048)
  Pallas kernels: 66.2 us -> 72.1 us
    pallas_call x2, Pallas kernels: 66.2 us -> 72.1 us  [allreduce(): pl.pallas_call(functools.partial(allreduce_kernel, nx, ny, orthonormalize...]
    unnamed x17 -> x18, local copies, waits for them, and re-layouts: 5.37 us -> 6.07 us
where the time goes in v6:
time: 109 us
  Pallas kernels  72.1 us (66%)
  matrix products  30 us (28%)
  local copies, waits for them, and re-layouts  6.07 us (6%)
    pallas_call x2, Pallas kernels, allreduce(): pl.pallas_call(functools.partial(allreduce_kernel, nx, ny, orthonormalize...  72.1 us
    dot_general x1, matrix products, on_device(): jnp.einsum('bkj,bij->bki', start_factor, merged, precision=HIGHEST)  8.64 us
    dot_general x1, matrix products, on_device(): approx = jnp.einsum('bki,bkj->bij', left_rows, right_rows, precision=HIGH)  8.24 us
    dot_general x1, matrix products, on_device(): right_local = jnp.einsum('bki,bij->bkj', left_rows, merged, precision=HIGH)  8.13 us
    unnamed x18, local copies, waits for them, and re-layouts  6.07 us
    dot_general x1, matrix products, on_device(): lax.dot_general(normed, grad_key, CONTRACT, preferred_element_type=jnp.fl...  3.15 us

profile of v6, /device:TPU:1, one launch (start us, length us, event | category | flops | bytes accessed | tf_op | source)
XLA Modules:
  0.0 108.9 jit_solution(18092956090446314553)
XLA Ops:
  0.6 0.0 copy-start
  0.6 0.0 copy-start.7
  0.7 1.3 %copy-done = bf16[640,1024]{1,0:T(8,128)(2,1)S(1)} copy-done((bf16[640,1024]{1,0:T(8,128)(2,1)S(1)}, bf16[640,1024]{1,0:T(8,128)(2,1)}, u32[]{:S(2)}) %copy-start) | copy-done | bytes 1310744
  2.0 3.1 %convolution_bitcast_fusion = f32[1,1024,1024]{2,1,0:T(8,128)S(1)} fusion(bf16[640,1024]{1,0:T(8,128)(2,1)S(1)} %copy-done, bf16[640,1024]{1,0:T(8,128)(2,1)} %param.7), kind=kOutput, calls=%fused_computation.2 | convolution fusion | flops 1342177280 | bytes 6815744 | tf_op jit(solution)/shard_map/dot_general | solution.py:221
  5.1 0.0 copy-done.7
  5.1 0.0 copy-start.2
  5.1 0.0 copy-start.1
  5.1 0.0 copy-start.6
  5.2 1.9 %convolution_bitcast_fusion.1 = f32[1,1024,1024]{2,1,0:T(8,128)S(1)} fusion(bf16[640,1024]{1,0:T(8,128)(2,1)S(1)} %copy-done, bf16[640,1024]{1,0:T(8,128)(2,1)S(1)} %copy-done.7), kind=kOutput, calls=%fused_computation.3 | convolution fusion | flops 1342177280 | bytes 6815744 | tf_op jit(solution)/shard_map/dot_general | solution.py:220
  7.0 0.2 copy-done.2
  7.3 2.1 %copy-done.3 = f32[1,1024,1024]{2,1,0:T(8,128)} copy-done((f32[1,1024,1024]{2,1,0:T(8,128)}, f32[1,1024,1024]{2,1,0:T(8,128)S(1)}, u32[]{:S(2)}) %copy-start.3) | copy-done | bytes 4194328
  9.4 1.0 copy-done.1
  10.4 0.0 copy-done.6
  10.4 8.6 %convolution_bitcast_fusion.2.x_ref = f32[2,32,1024]{2,1,0:T(8,128)} fusion(f32[2,32,1024]{2,1,0:T(8,128)S(1)} %copy-done.6, f32[1,1024,1024]{2,1,0:T(8,128)S(1)} %convolution_bitcast_fusion, f32[1,1024,1024]{2,1,0:T(8,128)S(1)} %convolution_bitcast_fusion.1, bf16[2,1024,1024]{2,1,0:T(8,128)(2,1)S(1)} %copy-done.1), kind=kOutput, calls=%fused_computation.4 | convolution fusion | flops 811597824 | bytes 13107200 | tf_op jit(solution)/shard_map/bkj,bij->bki/dot_general | solution.py:223
  19.0 42.1 %shard_map.76 = f32[2,32,1024]{2,1,0:T(8,128)} custom-call(f32[2,32,1024]{2,1,0:T(8,128)} %convolution_bitcast_fusion.2.x_ref), custom_call_target="tpu_custom_call" | custom-call | tf_op jit(solution)/shard_map/pallas_call | solution.py:181
  61.1 0.0 copy-start.4
  61.1 8.1 %fusion.x_ref = f32[2,32,1024]{2,1,0:T(8,128)} fusion(f32[2,32,1024]{2,1,0:T(8,128)} %shard_map.76, f32[1,1024,1024]{2,1,0:T(8,128)} %copy-done.2, f32[1,1024,1024]{2,1,0:T(8,128)} %copy-done.3, bf16[2,1024,1024]{2,1,0:T(8,128)(2,1)} %param.8), kind=kOutput, calls=%fused_computation.5 | convolution fusion | flops 408944640 | bytes 13107200 | tf_op jit(solution)/shard_map/bki,bij->bkj/dot_general | solution.py:225
  69.3 30.0 %shard_map.77 = f32[2,32,1024]{2,1,0:T(8,128)} custom-call(f32[2,32,1024]{2,1,0:T(8,128)} %fusion.x_ref), custom_call_target="tpu_custom_call" | custom-call | tf_op jit(solution)/shard_map/pallas_call | solution.py:181
  99.2 0.0 copy-done.4
  99.2 0.0 copy-start.5
  99.2 8.2 %subtract_convert_fusion = bf16[2,1024,1024]{2,1,0:T(8,128)(2,1)} fusion(f32[2,32,1024]{2,1,0:T(8,128)S(1)} %copy-done.4, f32[2,32,1024]{2,1,0:T(8,128)} %shard_map.77, bf16[2,1024,1024]{2,1,0:T(8,128)(2,1)} %param.8, f32[1,1024,1024]{2,1,0:T(8,128)} %copy-done.2, f32[1,1024,1024]{2,1,0:T(8,128)} %copy-done.3), kind=kOutput, calls=%fused_computation.1 | convolution fusion | flops 413138944 | bytes 17301504 | tf_op jit(solution)/shard_map/bki,bkj->bij/dot_general | solution.py:227
  107.5 0.7 copy.10
  108.2 0.0 copy-done.5
  108.2 0.7 copy.11
  (1 shorter events, 0.0 us)
Async XLA Ops:
  0.6 1.3 %copy-start = (bf16[640,1024]{1,0:T(8,128)(2,1)S(1)}, bf16[640,1024]{1,0:T(8,128)(2,1)}, u32[]{:S(2)}) copy-start(bf16[640,1024]{1,0:T(8,128)(2,1)} %param.5) | copy-start | bytes 3932164
  0.6 4.5 %copy-start.7 = (bf16[640,1024]{1,0:T(8,128)(2,1)S(1)}, bf16[640,1024]{1,0:T(8,128)(2,1)}, u32[]{:S(2)}) copy-start(bf16[640,1024]{1,0:T(8,128)(2,1)} %param.6) | copy-start | bytes 3932164
  5.1 2.1 %copy-start.2 = (f32[1,1024,1024]{2,1,0:T(8,128)}, f32[1,1024,1024]{2,1,0:T(8,128)S(1)}, u32[]{:S(2)}) copy-start(f32[1,1024,1024]{2,1,0:T(8,128)S(1)} %convolution_bitcast_fusion) | copy-start | bytes 12582916
  5.1 5.2 %copy-start.1 = (bf16[2,1024,1024]{2,1,0:T(8,128)(2,1)S(1)}, bf16[2,1024,1024]{2,1,0:T(8,128)(2,1)}, u32[]{:S(2)}) copy-start(bf16[2,1024,1024]{2,1,0:T(8,128)(2,1)} %param.8) | copy-start | bytes 12582916
  5.1 5.2 %copy-start.6 = (f32[2,32,1024]{2,1,0:T(8,128)S(1)}, f32[2,32,1024]{2,1,0:T(8,128)}, u32[]{:S(2)}) copy-start(f32[2,32,1024]{2,1,0:T(8,128)} %param.9) | copy-start | bytes 786436
  7.3 2.1 %copy-start.3 = (f32[1,1024,1024]{2,1,0:T(8,128)}, f32[1,1024,1024]{2,1,0:T(8,128)S(1)}, u32[]{:S(2)}) copy-start(f32[1,1024,1024]{2,1,0:T(8,128)S(1)} %convolution_bitcast_fusion.1) | copy-start | bytes 12582916
  61.1 38.1 %copy-start.4 = (f32[2,32,1024]{2,1,0:T(8,128)S(1)}, f32[2,32,1024]{2,1,0:T(8,128)}, u32[]{:S(2)}) copy-start(f32[2,32,1024]{2,1,0:T(8,128)} %shard_map.76) | copy-start | bytes 786436
  99.2 9.0 %copy-start.5 = (f32[2,32,1024]{2,1,0:T(8,128)S(1)}, f32[2,32,1024]{2,1,0:T(8,128)}, u32[]{:S(2)}) copy-start(f32[2,32,1024]{2,1,0:T(8,128)} %shard_map.77) | copy-start | bytes 786436

commit v7 on v5

--- a/solution.py
+++ b/solution.py
@@ -231,12 +231,43 @@
     query_grad = lax.dot_general(normed, grad_query, CONTRACT, preferred_element_type=jnp.float32)
     key_grad = lax.dot_general(normed, grad_key, CONTRACT, preferred_element_type=jnp.float32)
     merged = jnp.stack([query_grad, key_grad]) + error.astype(jnp.float32)
-    left_local = jnp.einsum("bkj,bij->bki", start_factor, merged, precision=HIGHEST)
+    m_hi, m_mid, m_lo = split3(merged)
+    s_hi, s_mid, s_lo = split3(start_factor)
+    left_local = combine6(*rows_times(
+        [[s_hi, s_mid, s_lo], [s_hi, s_mid], [s_hi]], [m_hi, m_mid, m_lo], "bkj,bij->bki"))
     left_rows = allreduce(left_local, nx, ny, 0, orthonormalize=True)
-    right_local = jnp.einsum("bki,bij->bkj", left_rows, merged, precision=HIGH)
+    l_hi, l_mid, l_lo = split3(left_rows)
+    first, second = rows_times([[l_hi, l_mid], [l_hi]], [m_hi, m_mid], "bki,bij->bkj")
+    right_local = first[0] + (first[1] + second[0])
     right_rows = allreduce(right_local, nx, ny, 1) / replicas
-    approx = jnp.einsum("bki,bkj->bij", left_rows, right_rows, precision=HIGH)
+    r_hi, r_mid, r_lo = split3(right_rows)
+    lefts = jnp.concatenate([l_hi, l_hi, l_mid, l_hi, l_mid, l_lo], axis=1)
+    rights = jnp.concatenate([r_hi, r_mid, r_hi, r_lo, r_mid, r_hi], axis=1)
+    approx = jnp.einsum("bki,bkj->bij", lefts, rights, preferred_element_type=jnp.float32)
     return ((merged - approx).astype(jnp.bfloat16), left_rows, right_rows)
+
+
+def split3(x):
+    hi = lax.reduce_precision(x, exponent_bits=8, mantissa_bits=7)
+    rest = x - hi
+    mid = lax.reduce_precision(rest, exponent_bits=8, mantissa_bits=7)
+    lo = rest - mid
+    return (hi.astype(jnp.bfloat16), mid.astype(jnp.bfloat16), lo.astype(jnp.bfloat16))
+
+
+def rows_times(row_groups, big_pieces, spec):
+    out = []
+    for group, big in zip(row_groups, big_pieces):
+        k = group[0].shape[1]
+        prod = jnp.einsum(spec, jnp.concatenate(group, axis=1), big,
+                          preferred_element_type=jnp.float32)
+        out.append([prod[:, g * k:(g + 1) * k] for g in range(len(group))])
+    return out
+
+
+def combine6(first, second, third):
+    small = (first[2] + second[1]) + third[0]
+    return first[0] + ((first[1] + second[0]) + small)
 
 
 def solution(mesh):

time: 104 us -> 99.2 us (0.954)
  matrix products: 30.1 us -> 22.8 us
  other arithmetic: 0.97 us -> 4.83 us
  local copies, waits for them, and re-layouts: 5.37 us -> 4.04 us
    dot_general x3 -> x6, matrix products: 25.1 us -> 17.8 us  [the longest x5 11.1 us: rows_times(): jnp.einsum(spec, jnp.concatenate(group, axis=1), big, preferred_element_t...]
    unnamed x0 -> x7, other arithmetic: none -> 3.05 us
    add x0 -> x1, other arithmetic: none -> 1.67 us  [on_device(): merged = jnp.stack([query_grad, key_grad]) + error.astype(jnp.float32)]
    unnamed x17 -> x20, local copies, waits for them, and re-layouts: 5.37 us -> 4.04 us
where the time goes in v7:
time: 99.2 us; the launch traced here: 98.8 us
  Pallas kernels  66.3 us (67%)
  matrix products  22.8 us (23%)
  other arithmetic  4.83 us (5%)
  local copies, waits for them, and re-layouts  4.04 us (4%)
    pallas_call x2, Pallas kernels, allreduce(): pl.pallas_call(functools.partial(allreduce_kernel, nx, ny, orthonormalize...  66.3 us
    dot_general x5, matrix products, rows_times(): jnp.einsum(spec, jnp.concatenate(group, axis=1), big, preferred_element_t...  11.1 us
    dot_general x1, matrix products, on_device(): jnp.einsum('bki,bkj->bij', lefts, rights, preferred_element_type=jnp.floa...  6.71 us
    unnamed x20, local copies, waits for them, and re-layouts  4.04 us
    dot_general x1, matrix products, on_device(): lax.dot_general(normed, grad_key, CONTRACT, preferred_element_type=jnp.fl...  3.15 us
    unnamed x7, other arithmetic  3.05 us

profile of v7, /device:TPU:1, one launch (start us, length us, event | category | flops | bytes accessed | tf_op | source)
XLA Modules:
  0.0 98.8 jit_solution(2473048351003879353)
XLA Ops:
  0.6 0.0 copy-start
  0.7 1.3 %copy-done = bf16[640,1024]{1,0:T(8,128)(2,1)S(1)} copy-done((bf16[640,1024]{1,0:T(8,128)(2,1)S(1)}, bf16[640,1024]{1,0:T(8,128)(2,1)}, u32[]{:S(2)}) %copy-start) | copy-done | bytes 1310744
  2.0 3.1 %convolution_bitcast_fusion = f32[1,1024,1024]{2,1,0:T(8,128)S(1)} fusion(bf16[640,1024]{1,0:T(8,128)(2,1)S(1)} %copy-done, bf16[640,1024]{1,0:T(8,128)(2,1)} %param.7), kind=kOutput, calls=%fused_computation.8 | convolution fusion | flops 1342177280 | bytes 6815744 | tf_op jit(solution)/shard_map/dot_general | solution.py:232
  5.1 0.0 copy-start.5
  5.1 1.9 %convolution_bitcast_fusion.1 = f32[1,1024,1024]{2,1,0:T(8,128)S(1)} fusion(bf16[640,1024]{1,0:T(8,128)(2,1)S(1)} %copy-done, bf16[640,1024]{1,0:T(8,128)(2,1)S(1)} %copy-done.7), kind=kOutput, calls=%fused_computation.9 | convolution fusion | flops 1342177280 | bytes 6815744 | tf_op jit(solution)/shard_map/dot_general | solution.py:231
  7.0 0.3 copy-done.5
  7.3 1.7 %maximum_add_fusion = f32[2,1024,1024]{2,1,0:T(8,128)S(1)} fusion(f32[1,1024,1024]{2,1,0:T(8,128)S(1)} %convolution_bitcast_fusion, f32[1,1024,1024]{2,1,0:T(8,128)S(1)} %convolution_bitcast_fusion.1, bf16[2,1024,1024]{2,1,0:T(8,128)(2,1)S(1)} %copy-done.5), kind=kLoop, calls=%fused_computation.5 | loop fusion | flops 6291456 | bytes 20971520 | tf_op jit(solution)/shard_map/add | solution.py:233
  9.0 0.1 fusion.24
  9.1 1.4 %fusion.4 = f32[2,96,1024]{2,1,0:T(8,128)S(1)} fusion(f32[2,1024,1024]{2,1,0:T(8,128)S(1)} %maximum_add_fusion, bf16[2,32,1024]{2,1,0:T(8,128)(2,1)S(1)} %get-tuple-element.9, bf16[2,32,1024]{2,1,0:T(8,128)(2,1)S(1)} %get-tuple-element.10, bf16[2,32,1024]{2,1,0:T(8,128)(2,1)S(1)} %get-tuple-element.11), kind=kOutput, calls=%fused_computation.11 | convolution fusion | flops 408027136 | bytes 9568256 | tf_op jit(solution)/shard_map/bkj,bij->bki/dot_general | solution.py:262
  10.5 1.4 %fusion.18 = f32[2,64,1024]{2,1,0:T(8,128)S(1)} fusion(f32[2,1024,1024]{2,1,0:T(8,128)S(1)} %maximum_add_fusion, bf16[2,32,1024]{2,1,0:T(8,128)(2,1)S(1)} %get-tuple-element.10, bf16[2,32,1024]{2,1,0:T(8,128)(2,1)S(1)} %get-tuple-element.11), kind=kOutput, calls=%fused_computation.18 | convolution fusion | flops 277348352 | bytes 9175040 | tf_op jit(solution)/shard_map/bkj,bij->bki/dot_general | solution.py:262
  11.9 0.3 copy-done.1
  12.2 2.2 %fusion.15.x_ref = f32[2,32,1024]{2,1,0:T(8,128)} fusion(bf16[2,32,1024]{2,1,0:T(8,128)(2,1)S(1)} %get-tuple-element.11, f32[2,1024,1024]{2,1,0:T(8,128)S(1)} %maximum_add_fusion, f32[2,64,1024]{2,1,0:T(8,128)S(1)} %fusion.18, f32[2,96,1024]{2,1,0:T(8,128)S(1)} %fusion.4), kind=kOutput, calls=%fused_computation.17 | convolution fusion | flops 145031168 | bytes 10092544 | tf_op jit(solution)/shard_map/bkj,bij->bki/dot_general | solution.py:262
  14.5 39.1 %shard_map.76 = f32[2,32,1024]{2,1,0:T(8,128)} custom-call(f32[2,32,1024]{2,1,0:T(8,128)} %fusion.15.x_ref), custom_call_target="tpu_custom_call" | custom-call | tf_op jit(solution)/shard_map/pallas_call | solution.py:190
  53.6 1.0 constant_dynamic-update-slice_fusion.4
  54.6 1.0 constant_dynamic-update-slice_fusion.2
  55.6 4.4 %fusion.3 = f32[2,64,1024]{2,1,0:T(8,128)S(1)} fusion(f32[2,1024,1024]{2,1,0:T(8,128)} %copy-done.1, bf16[2,32,1024]{2,1,0:T(8,128)(2,1)S(1)} %get-tuple-element.6, bf16[2,32,1024]{2,1,0:T(8,128)(2,1)S(1)} %get-tuple-element.8), kind=kOutput, calls=%fused_computation.10 | convolution fusion | flops 273154048 | bytes 9175040 | tf_op jit(solution)/shard_map/bki,bij->bkj/dot_general | solution.py:262
  60.0 1.4 %copy-done.2 = f32[2,1024,1024]{2,1,0:T(8,128)S(1)} copy-done((f32[2,1024,1024]{2,1,0:T(8,128)S(1)}, f32[2,1024,1024]{2,1,0:T(8,128)}, u32[]{:S(2)}) %copy-start.2) | copy-done | bytes 8388632
  61.4 1.7 %fusion.5.x_ref = f32[2,32,1024]{2,1,0:T(8,128)} fusion(bf16[2,32,1024]{2,1,0:T(8,128)(2,1)S(1)} %get-tuple-element.8, f32[2,1024,1024]{2,1,0:T(8,128)S(1)} %copy-done.2, f32[2,64,1024]{2,1,0:T(8,128)S(1)} %fusion.3), kind=kOutput, calls=%fused_computation.13 | convolution fusion | flops 142737408 | bytes 9306112 | tf_op jit(solution)/shard_map/bki,bij->bkj/dot_general | solution.py:262
  63.0 27.1 %shard_map.77 = f32[2,32,1024]{2,1,0:T(8,128)} custom-call(f32[2,32,1024]{2,1,0:T(8,128)} %fusion.5.x_ref), custom_call_target="tpu_custom_call" | custom-call | tf_op jit(solution)/shard_map/pallas_call | solution.py:190
  90.2 1.0 constant_dynamic-update-slice_fusion.9
  91.1 0.0 copy-start.3
  91.4 0.1 fusion.34
  91.4 6.7 %subtract_convert_fusion = bf16[2,1024,1024]{2,1,0:T(8,128)(2,1)} fusion(f32[2,1024,1024]{2,1,0:T(8,128)} %copy-done.1, bf16[2,192,1024]{2,1,0:T(8,128)(2,1)S(1)} %get-tuple-element.12, bf16[2,192,1024]{2,1,0:T(8,128)(2,1)S(1)} %get-tuple-element.13), kind=kOutput, calls=%fused_computation.6 | convolution fusion | flops 809500672 | bytes 14155776 | tf_op jit(solution)/shard_map/bki,bkj->bij/dot_general | solution.py:246
  98.1 0.7 copy.19
  (16 shorter events, 0.2 us)
Async XLA Ops:
  0.6 1.3 %copy-start = (bf16[640,1024]{1,0:T(8,128)(2,1)S(1)}, bf16[640,1024]{1,0:T(8,128)(2,1)}, u32[]{:S(2)}) copy-start(bf16[640,1024]{1,0:T(8,128)(2,1)} %param.5) | copy-start | bytes 3932164
  0.6 4.5 %copy-start.7 = (bf16[640,1024]{1,0:T(8,128)(2,1)S(1)}, bf16[640,1024]{1,0:T(8,128)(2,1)}, u32[]{:S(2)}) copy-start(bf16[640,1024]{1,0:T(8,128)(2,1)} %param.6) | copy-start | bytes 3932164
  5.1 2.2 %copy-start.5 = (bf16[2,1024,1024]{2,1,0:T(8,128)(2,1)S(1)}, bf16[2,1024,1024]{2,1,0:T(8,128)(2,1)}, u32[]{:S(2)}) copy-start(bf16[2,1024,1024]{2,1,0:T(8,128)(2,1)} %param.8) | copy-start | bytes 12582916
  7.3 1.7 %copy-start.6 = (f32[2,32,1024]{2,1,0:T(8,128)S(1)}, f32[2,32,1024]{2,1,0:T(8,128)}, u32[]{:S(2)}) copy-start(f32[2,32,1024]{2,1,0:T(8,128)} %param.9) | copy-start | bytes 786436
  9.0 3.2 %copy-start.1 = (f32[2,1024,1024]{2,1,0:T(8,128)}, f32[2,1024,1024]{2,1,0:T(8,128)S(1)}, u32[]{:S(2)}) copy-start(f32[2,1024,1024]{2,1,0:T(8,128)S(1)} %maximum_add_fusion) | copy-start | bytes 25165828
  55.6 5.8 %copy-start.2 = (f32[2,1024,1024]{2,1,0:T(8,128)S(1)}, f32[2,1024,1024]{2,1,0:T(8,128)}, u32[]{:S(2)}) copy-start(f32[2,1024,1024]{2,1,0:T(8,128)} %copy-done.1) | copy-start | bytes 25165828
  61.4 30.0 %copy-start.4 = (f32[2,32,1024]{2,1,0:T(8,128)S(1)}, f32[2,32,1024]{2,1,0:T(8,128)}, u32[]{:S(2)}) copy-start(f32[2,32,1024]{2,1,0:T(8,128)} %shard_map.76) | copy-start | bytes 786436
  91.1 7.0 %copy-start.3 = (f32[2,32,1024]{2,1,0:T(8,128)}, f32[2,32,1024]{2,1,0:T(8,128)S(1)}, u32[]{:S(2)}) copy-start(f32[2,32,1024]{2,1,0:T(8,128)S(1)} %get-tuple-element.19) | copy-start | bytes 786436

commit v8 on v7

--- a/solution.py
+++ b/solution.py
@@ -15,7 +15,23 @@
 SUB = 8
 
 
-def allreduce_kernel(nx, ny, orthonormalize, x_ref, o_ref, recv_a, p_t, recv_b, recv_c, recv_d,
+def allreduce_kernel(nx, ny, orthonormalize, divisor, patterns, x_ref, o_ref, *refs):
+    stacked = refs[:len(patterns)]
+    allreduce_body(nx, ny, orthonormalize, divisor, x_ref, o_ref, *refs[len(patterns):])
+    for b in range(o_ref.shape[0]):
+        value = o_ref[b]
+        k = value.shape[0]
+        hi = value.astype(jnp.bfloat16)
+        rest = value - hi.astype(jnp.float32)
+        mid = rest.astype(jnp.bfloat16)
+        lo = (rest - mid.astype(jnp.float32)).astype(jnp.bfloat16)
+        parts = (hi, mid, lo)
+        for pattern, out_ref in zip(patterns, stacked):
+            for g, piece in enumerate(pattern):
+                out_ref[b, g * k:(g + 1) * k, :] = parts[piece]
+
+
+def allreduce_body(nx, ny, orthonormalize, divisor, x_ref, o_ref, recv_a, p_t, recv_b, recv_c, recv_d,
                      sa, ra, sb, rb, sc, rc, sd, rd):
     h = lax.axis_index("gx")
     a = lax.axis_index("gy")
@@ -145,7 +161,10 @@
 
     lax.fori_loop(1, ny, wait_d, 0)
     for s in range(ny):
-        o_ref[:, :, s * LANES:(s + 1) * LANES] = recv_d[s]
+        block = recv_d[s]
+        if divisor is not None:
+            block = block / divisor
+        o_ref[:, :, s * LANES:(s + 1) * LANES] = block
     if orthonormalize:
         orthonormal_rows(o_ref)
 
@@ -181,17 +200,18 @@
                               preferred_element_type=jnp.float32)
 
 
-def allreduce(x, nx, ny, collective_id, orthonormalize=False):
+def allreduce(x, nx, ny, collective_id, orthonormalize=False, divisor=None, patterns=()):
     nb, rows, cols = x.shape
     assert cols == ny * LANES and rows % SUB == 0
     nt = nb * (rows // SUB)
     assert nx % nt == 0
     vmem = pltpu.VMEM
     return pl.pallas_call(
-        functools.partial(allreduce_kernel, nx, ny, orthonormalize),
-        out_shape=jax.ShapeDtypeStruct(x.shape, jnp.float32),
+        functools.partial(allreduce_kernel, nx, ny, orthonormalize, divisor, patterns),
+        out_shape=[jax.ShapeDtypeStruct(x.shape, jnp.float32)] + [
+            jax.ShapeDtypeStruct((nb, len(p) * rows, cols), jnp.bfloat16) for p in patterns],
         in_specs=[pl.BlockSpec(memory_space=vmem)],
-        out_specs=pl.BlockSpec(memory_space=vmem),
+        out_specs=[pl.BlockSpec(memory_space=vmem)] * (1 + len(patterns)),
         scratch_shapes=[
             vmem((ny, nb, rows, LANES), jnp.float32),
             vmem((nt, SUB, LANES), jnp.float32),
@@ -235,14 +255,14 @@
     s_hi, s_mid, s_lo = split3(start_factor)
     left_local = combine6(*rows_times(
         [[s_hi, s_mid, s_lo], [s_hi, s_mid], [s_hi]], [m_hi, m_mid, m_lo], "bkj,bij->bki"))
-    left_rows = allreduce(left_local, nx, ny, 0, orthonormalize=True)
-    l_hi, l_mid, l_lo = split3(left_rows)
-    first, second = rows_times([[l_hi, l_mid], [l_hi]], [m_hi, m_mid], "bki,bij->bkj")
-    right_local = first[0] + (first[1] + second[0])
-    right_rows = allreduce(right_local, nx, ny, 1) / replicas
-    r_hi, r_mid, r_lo = split3(right_rows)
-    lefts = jnp.concatenate([l_hi, l_hi, l_mid, l_hi, l_mid, l_lo], axis=1)
-    rights = jnp.concatenate([r_hi, r_mid, r_hi, r_lo, r_mid, r_hi], axis=1)
+    left_rows, lefts, left_pair = allreduce(
+        left_local, nx, ny, 0, orthonormalize=True, patterns=((0, 0, 1, 0, 1, 2), (0, 1)))
+    k = left_rows.shape[1]
+    pair = jnp.einsum("bki,bij->bkj", left_pair, m_hi, preferred_element_type=jnp.float32)
+    cross = jnp.einsum("bki,bij->bkj", lefts[:, :k], m_mid, preferred_element_type=jnp.float32)
+    right_local = pair[:, :k] + (pair[:, k:] + cross)
+    right_rows, rights = allreduce(
+        right_local, nx, ny, 1, divisor=float(replicas), patterns=((0, 1, 0, 2, 1, 0),))
     approx = jnp.einsum("bki,bkj->bij", lefts, rights, preferred_element_type=jnp.float32)
     return ((merged - approx).astype(jnp.bfloat16), left_rows, right_rows)
 

time: 99.2 us -> 98.2 us (0.990)
  other arithmetic: 4.83 us -> 2.2 us
    dot_general x0 -> x2, matrix products: none -> 6.1 us  [the longest x1 4.45 us: on_device(): jnp.einsum('bki,bij->bkj', left_pair, m_hi, preferred_element_type=jnp.fl...]
    dot_general x5 -> x3, matrix products: 11.1 us -> 5.02 us  [rows_times(): jnp.einsum(spec, jnp.concatenate(group, axis=1), big, preferred_element_t...]
    unnamed x7 -> x0, other arithmetic: 3.05 us -> none
where the time goes in v8:
time: 98.2 us; the launch traced here: 98 us
  Pallas kernels  67 us (68%)
  matrix products  23.1 us (24%)
  local copies, waits for them, and re-layouts  4.87 us (5%)
  other arithmetic  2.2 us (2%)
    pallas_call x2, Pallas kernels, allreduce(): pl.pallas_call(functools.partial(allreduce_kernel, nx, ny, orthonormalize...  67 us
    dot_general x1, matrix products, on_device(): jnp.einsum('bki,bkj->bij', lefts, rights, preferred_element_type=jnp.floa...  7 us
    dot_general x3, matrix products, rows_times(): jnp.einsum(spec, jnp.concatenate(group, axis=1), big, preferred_element_t...  5.02 us
    unnamed x20, local copies, waits for them, and re-layouts  4.87 us
    dot_general x1, matrix products, on_device(): jnp.einsum('bki,bij->bkj', left_pair, m_hi, preferred_element_type=jnp.fl...  4.45 us
    dot_general x1, matrix products, on_device(): lax.dot_general(normed, grad_key, CONTRACT, preferred_element_type=jnp.fl...  3.15 us
    add x1, other arithmetic, on_device(): merged = jnp.stack([query_grad, key_grad]) + error.astype(jnp.float32)  2.15 us

profile of v8, /device:TPU:1, one launch (start us, length us, event | category | flops | bytes accessed | tf_op | source)
XLA Modules:
  0.0 98.0 jit_solution(4835330582262293252)
XLA Ops:
  0.6 0.0 copy-start
  0.6 0.0 copy-start.8
  0.7 1.3 %copy-done = bf16[640,1024]{1,0:T(8,128)(2,1)S(1)} copy-done((bf16[640,1024]{1,0:T(8,128)(2,1)S(1)}, bf16[640,1024]{1,0:T(8,128)(2,1)}, u32[]{:S(2)}) %copy-start) | copy-done | bytes 1310744
  2.0 3.2 %convolution_bitcast_fusion = f32[1,1024,1024]{2,1,0:T(8,128)S(1)} fusion(bf16[640,1024]{1,0:T(8,128)(2,1)S(1)} %copy-done, bf16[640,1024]{1,0:T(8,128)(2,1)} %param.7), kind=kOutput, calls=%fused_computation.8 | convolution fusion | flops 1342177280 | bytes 6815744 | tf_op jit(solution)/shard_map/dot_general | solution.py:252
  5.1 0.0 copy-done.8
  5.1 0.0 copy-start.3
  5.1 1.9 %convolution_bitcast_fusion.1 = f32[1,1024,1024]{2,1,0:T(8,128)S(1)} fusion(bf16[640,1024]{1,0:T(8,128)(2,1)S(1)} %copy-done, bf16[640,1024]{1,0:T(8,128)(2,1)S(1)} %copy-done.8), kind=kOutput, calls=%fused_computation.9 | convolution fusion | flops 1342177280 | bytes 6815744 | tf_op jit(solution)/shard_map/dot_general | solution.py:251
  7.0 0.3 copy-done.3
  7.3 2.1 %maximum_add_fusion = f32[2,1024,1024]{2,1,0:T(8,128)S(1)} fusion(f32[1,1024,1024]{2,1,0:T(8,128)S(1)} %convolution_bitcast_fusion, f32[1,1024,1024]{2,1,0:T(8,128)S(1)} %convolution_bitcast_fusion.1, bf16[2,1024,1024]{2,1,0:T(8,128)(2,1)S(1)} %copy-done.3), kind=kLoop, calls=%fused_computation.5 | loop fusion | flops 6291456 | bytes 20971520 | tf_op jit(solution)/shard_map/add | solution.py:253
  9.5 0.1 fusion.24
  9.6 1.4 %fusion.4 = f32[2,96,1024]{2,1,0:T(8,128)S(1)} fusion(f32[2,1024,1024]{2,1,0:T(8,128)S(1)} %maximum_add_fusion, bf16[2,32,1024]{2,1,0:T(8,128)(2,1)S(1)} %get-tuple-element.13, bf16[2,32,1024]{2,1,0:T(8,128)(2,1)S(1)} %get-tuple-element.14, bf16[2,32,1024]{2,1,0:T(8,128)(2,1)S(1)} %get-tuple-element.15), kind=kOutput, calls=%fused_computation.11 | convolution fusion | flops 408027136 | bytes 9568256 | tf_op jit(solution)/shard_map/bkj,bij->bki/dot_general | solution.py:282
  11.0 1.4 %fusion.18 = f32[2,64,1024]{2,1,0:T(8,128)S(1)} fusion(f32[2,1024,1024]{2,1,0:T(8,128)S(1)} %maximum_add_fusion, bf16[2,32,1024]{2,1,0:T(8,128)(2,1)S(1)} %get-tuple-element.14, bf16[2,32,1024]{2,1,0:T(8,128)(2,1)S(1)} %get-tuple-element.15), kind=kOutput, calls=%fused_computation.18 | convolution fusion | flops 277348352 | bytes 9175040 | tf_op jit(solution)/shard_map/bkj,bij->bki/dot_general | solution.py:282
  12.4 0.3 copy-done.1
  12.7 2.2 %fusion.15.x_ref = f32[2,32,1024]{2,1,0:T(8,128)} fusion(bf16[2,32,1024]{2,1,0:T(8,128)(2,1)S(1)} %get-tuple-element.15, f32[2,1024,1024]{2,1,0:T(8,128)S(1)} %maximum_add_fusion, f32[2,64,1024]{2,1,0:T(8,128)S(1)} %fusion.18, f32[2,96,1024]{2,1,0:T(8,128)S(1)} %fusion.4), kind=kOutput, calls=%fused_computation.17 | convolution fusion | flops 145031168 | bytes 10092544 | tf_op jit(solution)/shard_map/bkj,bij->bki/dot_general | solution.py:282
  14.9 39.6 %shard_map.76 = (f32[2,32,1024]{2,1,0:T(8,128)}, bf16[2,192,1024]{2,1,0:T(8,128)(2,1)}, bf16[2,64,1024]{2,1,0:T(8,128)(2,1)}) custom-call(f32[2,32,1024]{2,1,0:T(8,128)} %fusion.15.x_ref), custom_call_target="tpu_custom_call" | custom-call | tf_op jit(solution)/shard_map/pallas_call | solution.py:209
  54.5 4.4 %fusion.3 = f32[2,64,1024]{2,1,0:T(8,128)S(1)} fusion(bf16[2,64,1024]{2,1,0:T(8,128)(2,1)} %get-tuple-element.9, f32[2,1024,1024]{2,1,0:T(8,128)} %copy-done.1), kind=kOutput, calls=%fused_computation.10 | convolution fusion | flops 272629760 | bytes 9175040 | tf_op jit(solution)/shard_map/bki,bij->bkj/dot_general | solution.py:261
  58.9 1.4 %copy-done.2 = f32[2,1024,1024]{2,1,0:T(8,128)S(1)} copy-done((f32[2,1024,1024]{2,1,0:T(8,128)S(1)}, f32[2,1024,1024]{2,1,0:T(8,128)}, u32[]{:S(2)}) %copy-start.2) | copy-done | bytes 8388632
  60.3 0.1 copy-done.4
  60.5 1.7 %fusion.5.x_ref = f32[2,32,1024]{2,1,0:T(8,128)} fusion(f32[2,1024,1024]{2,1,0:T(8,128)S(1)} %copy-done.2, f32[2,64,1024]{2,1,0:T(8,128)S(1)} %fusion.3, bf16[2,192,1024]{2,1,0:T(8,128)(2,1)S(1)} %copy-done.4), kind=kOutput, calls=%fused_computation.13 | convolution fusion | flops 142737408 | bytes 9306112 | tf_op jit(solution)/shard_map/bki,bij->bkj/dot_general | solution.py:262
  62.1 27.5 %shard_map.77 = (f32[2,32,1024]{2,1,0:T(8,128)}, bf16[2,192,1024]{2,1,0:T(8,128)(2,1)}) custom-call(f32[2,32,1024]{2,1,0:T(8,128)} %fusion.5.x_ref), custom_call_target="tpu_custom_call" | custom-call | tf_op jit(solution)/shard_map/pallas_call | solution.py:209
  89.6 7.0 %subtract_convert_fusion = bf16[2,1024,1024]{2,1,0:T(8,128)(2,1)} fusion(f32[2,1024,1024]{2,1,0:T(8,128)} %copy-done.1, bf16[2,192,1024]{2,1,0:T(8,128)(2,1)S(1)} %copy-done.4, bf16[2,192,1024]{2,1,0:T(8,128)(2,1)} %get-tuple-element.10), kind=kOutput, calls=%fused_computation.6 | convolution fusion | flops 809500672 | bytes 14155776 | tf_op jit(solution)/shard_map/bki,bkj->bij/dot_general | solution.py:266
  96.6 0.7 copy.10
  97.3 0.0 copy-done.7
  97.3 0.7 copy.11
  (8 shorter events, 0.0 us)
Async XLA Ops:
  0.6 1.3 %copy-start = (bf16[640,1024]{1,0:T(8,128)(2,1)S(1)}, bf16[640,1024]{1,0:T(8,128)(2,1)}, u32[]{:S(2)}) copy-start(bf16[640,1024]{1,0:T(8,128)(2,1)} %param.5) | copy-start | bytes 3932164
  0.6 4.5 %copy-start.8 = (bf16[640,1024]{1,0:T(8,128)(2,1)S(1)}, bf16[640,1024]{1,0:T(8,128)(2,1)}, u32[]{:S(2)}) copy-start(bf16[640,1024]{1,0:T(8,128)(2,1)} %param.6) | copy-start | bytes 3932164
  5.1 2.2 %copy-start.3 = (bf16[2,1024,1024]{2,1,0:T(8,128)(2,1)S(1)}, bf16[2,1024,1024]{2,1,0:T(8,128)(2,1)}, u32[]{:S(2)}) copy-start(bf16[2,1024,1024]{2,1,0:T(8,128)(2,1)} %param.8) | copy-start | bytes 12582916
  7.3 2.2 %copy-start.5 = (f32[2,32,1024]{2,1,0:T(8,128)S(1)}, f32[2,32,1024]{2,1,0:T(8,128)}, u32[]{:S(2)}) copy-start(f32[2,32,1024]{2,1,0:T(8,128)} %param.9) | copy-start | bytes 786436
  9.5 3.2 %copy-start.1 = (f32[2,1024,1024]{2,1,0:T(8,128)}, f32[2,1024,1024]{2,1,0:T(8,128)S(1)}, u32[]{:S(2)}) copy-start(f32[2,1024,1024]{2,1,0:T(8,128)S(1)} %maximum_add_fusion) | copy-start | bytes 25165828
  54.5 5.8 %copy-start.2 = (f32[2,1024,1024]{2,1,0:T(8,128)S(1)}, f32[2,1024,1024]{2,1,0:T(8,128)}, u32[]{:S(2)}) copy-start(f32[2,1024,1024]{2,1,0:T(8,128)} %copy-done.1) | copy-start | bytes 25165828
  54.5 6.0 %copy-start.4 = (bf16[2,192,1024]{2,1,0:T(8,128)(2,1)S(1)}, bf16[2,192,1024]{2,1,0:T(8,128)(2,1)}, u32[]{:S(2)}) copy-start(bf16[2,192,1024]{2,1,0:T(8,128)(2,1)} %get-tuple-element.8) | copy-start | bytes 2359300
  89.6 7.0 %copy-start.6 = (f32[2,32,1024]{2,1,0:T(8,128)S(1)}, f32[2,32,1024]{2,1,0:T(8,128)}, u32[]{:S(2)}) copy-start(f32[2,32,1024]{2,1,0:T(8,128)} %get-tuple-element.20) | copy-start | bytes 786436
  89.6 7.7 %copy-start.7 = (f32[2,32,1024]{2,1,0:T(8,128)S(1)}, f32[2,32,1024]{2,1,0:T(8,128)}, u32[]{:S(2)}) copy-start(f32[2,32,1024]{2,1,0:T(8,128)} %get-tuple-element.21) | copy-start | bytes 786436

commit v9 on v8

--- a/solution.py
+++ b/solution.py
@@ -228,7 +228,8 @@
             pltpu.SemaphoreType.DMA((ny,)),
         ],
         compiler_params=pltpu.CompilerParams(
-            collective_id=collective_id, has_side_effects=True
+            collective_id=collective_id, has_side_effects=True,
+            vmem_limit_bytes=8 * 1024 * 1024,
         ),
     )(x)
 

time: 98.2 us -> 84.5 us (0.86)
  matrix products: 23.1 us -> 14.5 us
  Pallas kernels: 67 us -> 63.9 us
  local copies, waits for them, and re-layouts: 4.87 us -> 3.03 us
    dot_general x1, matrix products: 7 us -> 3.37 us  [on_device(): jnp.einsum('bki,bkj->bij', lefts, rights, preferred_element_type=jnp.floa...]
    dot_general x1, matrix products: 4.45 us -> 0.87 us  [on_device(): jnp.einsum('bki,bij->bkj', left_pair, m_hi, preferred_element_type=jnp.fl...]
    pallas_call x2, Pallas kernels: 67 us -> 63.9 us  [allreduce(): pl.pallas_call(functools.partial(allreduce_kernel, nx, ny, orthonormalize...]
    unnamed x20 -> x10, local copies, waits for them, and re-layouts: 4.87 us -> 3.03 us
where the time goes in v9:
time: 84.5 us; the launch traced here: 84.4 us
  Pallas kernels  63.9 us (76%)
  matrix products  14.5 us (17%)
  local copies, waits for them, and re-layouts  3.03 us (4%)
  other arithmetic  2.21 us (3%)
    pallas_call x2, Pallas kernels, allreduce(): pl.pallas_call(functools.partial(allreduce_kernel, nx, ny, orthonormalize...  63.9 us
    dot_general x3, matrix products, rows_times(): jnp.einsum(spec, jnp.concatenate(group, axis=1), big, preferred_element_t...  4.34 us
    dot_general x1, matrix products, on_device(): jnp.einsum('bki,bkj->bij', lefts, rights, preferred_element_type=jnp.floa...  3.37 us
    dot_general x1, matrix products, on_device(): lax.dot_general(normed, grad_key, CONTRACT, preferred_element_type=jnp.fl...  3.15 us
    unnamed x10, local copies, waits for them, and re-layouts  3.03 us
    add x1, other arithmetic, on_device(): merged = jnp.stack([query_grad, key_grad]) + error.astype(jnp.float32)  2.15 us
    dot_general x1, matrix products, on_device(): lax.dot_general(normed, grad_query, CONTRACT, preferred_element_type=jnp....  1.86 us

profile of v9, /device:TPU:1, one launch (start us, length us, event | category | flops | bytes accessed | tf_op | source)
XLA Modules:
  0.0 84.4 jit_solution(5407753009431543766)
XLA Ops:
  0.6 0.0 copy-start
  0.6 0.0 copy-start.3
  0.7 1.3 %copy-done = bf16[640,1024]{1,0:T(8,128)(2,1)S(1)} copy-done((bf16[640,1024]{1,0:T(8,128)(2,1)S(1)}, bf16[640,1024]{1,0:T(8,128)(2,1)}, u32[]{:S(2)}) %copy-start) | copy-done | bytes 1310744
  2.0 3.2 %convolution_bitcast_fusion = f32[1,1024,1024]{2,1,0:T(8,128)S(1)} fusion(bf16[640,1024]{1,0:T(8,128)(2,1)S(1)} %copy-done, bf16[640,1024]{1,0:T(8,128)(2,1)} %param.7), kind=kOutput, calls=%fused_computation.8 | convolution fusion | flops 1342177280 | bytes 6815744 | tf_op jit(solution)/shard_map/dot_general | solution.py:253
  5.1 0.0 copy-done.3
  5.1 0.0 copy-start.1
  5.1 1.9 %convolution_bitcast_fusion.1 = f32[1,1024,1024]{2,1,0:T(8,128)S(1)} fusion(bf16[640,1024]{1,0:T(8,128)(2,1)S(1)} %copy-done, bf16[640,1024]{1,0:T(8,128)(2,1)S(1)} %copy-done.3), kind=kOutput, calls=%fused_computation.9 | convolution fusion | flops 1342177280 | bytes 6815744 | tf_op jit(solution)/shard_map/dot_general | solution.py:252
  7.0 0.3 copy-done.1
  7.3 0.0 copy-start.2
  7.3 2.1 %maximum_add_fusion = f32[2,1024,1024]{2,1,0:T(8,128)S(1)} fusion(f32[1,1024,1024]{2,1,0:T(8,128)S(1)} %convolution_bitcast_fusion, f32[1,1024,1024]{2,1,0:T(8,128)S(1)} %convolution_bitcast_fusion.1, bf16[2,1024,1024]{2,1,0:T(8,128)(2,1)S(1)} %copy-done.1), kind=kLoop, calls=%fused_computation.5 | loop fusion | flops 6291456 | bytes 20971520 | tf_op jit(solution)/shard_map/add | solution.py:254
  9.5 0.0 copy-done.2
  9.5 0.1 fusion.24
  9.6 1.4 %fusion.4 = f32[2,96,1024]{2,1,0:T(8,128)S(1)} fusion(f32[2,1024,1024]{2,1,0:T(8,128)S(1)} %maximum_add_fusion, bf16[2,32,1024]{2,1,0:T(8,128)(2,1)S(1)} %get-tuple-element.13, bf16[2,32,1024]{2,1,0:T(8,128)(2,1)S(1)} %get-tuple-element.14, bf16[2,32,1024]{2,1,0:T(8,128)(2,1)S(1)} %get-tuple-element.15), kind=kOutput, calls=%fused_computation.11 | convolution fusion | flops 408027136 | bytes 9568256 | tf_op jit(solution)/shard_map/bkj,bij->bki/dot_general | solution.py:283
  11.0 1.4 %fusion.18 = f32[2,64,1024]{2,1,0:T(8,128)S(1)} fusion(f32[2,1024,1024]{2,1,0:T(8,128)S(1)} %maximum_add_fusion, bf16[2,32,1024]{2,1,0:T(8,128)(2,1)S(1)} %get-tuple-element.14, bf16[2,32,1024]{2,1,0:T(8,128)(2,1)S(1)} %get-tuple-element.15), kind=kOutput, calls=%fused_computation.18 | convolution fusion | flops 277348352 | bytes 9175040 | tf_op jit(solution)/shard_map/bkj,bij->bki/dot_general | solution.py:283
  12.4 1.5 %fusion.15.x_ref = f32[2,32,1024]{2,1,0:T(8,128)S(1)} fusion(bf16[2,32,1024]{2,1,0:T(8,128)(2,1)S(1)} %get-tuple-element.15, f32[2,1024,1024]{2,1,0:T(8,128)S(1)} %maximum_add_fusion, f32[2,64,1024]{2,1,0:T(8,128)S(1)} %fusion.18, f32[2,96,1024]{2,1,0:T(8,128)S(1)} %fusion.4), kind=kOutput, calls=%fused_computation.17 | convolution fusion | flops 145031168 | bytes 10092544 | tf_op jit(solution)/shard_map/bkj,bij->bki/dot_general | solution.py:283
  13.9 38.0 %shard_map.76 = (f32[2,32,1024]{2,1,0:T(8,128)S(1)}, bf16[2,192,1024]{2,1,0:T(8,128)(2,1)S(1)}, bf16[2,64,1024]{2,1,0:T(8,128)(2,1)S(1)}) custom-call(f32[2,32,1024]{2,1,0:T(8,128)S(1)} %fusion.15.x_ref), custom_call_target="tpu_custom_call" | custom-call | tf_op jit(solution)/shard_map/pallas_call | solution.py:209
  51.9 0.9 %fusion.3 = f32[2,64,1024]{2,1,0:T(8,128)S(1)} fusion(bf16[2,64,1024]{2,1,0:T(8,128)(2,1)S(1)} %get-tuple-element.9, f32[2,1024,1024]{2,1,0:T(8,128)S(1)} %maximum_add_fusion), kind=kOutput, calls=%fused_computation.10 | convolution fusion | flops 272629760 | bytes 9175040 | tf_op jit(solution)/shard_map/bki,bij->bkj/dot_general | solution.py:262
  52.8 0.9 %fusion.5.x_ref = f32[2,32,1024]{2,1,0:T(8,128)S(1)} fusion(f32[2,1024,1024]{2,1,0:T(8,128)S(1)} %maximum_add_fusion, f32[2,64,1024]{2,1,0:T(8,128)S(1)} %fusion.3, bf16[2,192,1024]{2,1,0:T(8,128)(2,1)S(1)} %get-tuple-element.8), kind=kOutput, calls=%fused_computation.13 | convolution fusion | flops 142737408 | bytes 9306112 | tf_op jit(solution)/shard_map/bki,bij->bkj/dot_general | solution.py:263
  53.7 25.9 %shard_map.77 = (f32[2,32,1024]{2,1,0:T(8,128)S(1)}, bf16[2,192,1024]{2,1,0:T(8,128)(2,1)S(1)}) custom-call(f32[2,32,1024]{2,1,0:T(8,128)S(1)} %fusion.5.x_ref), custom_call_target="tpu_custom_call" | custom-call | tf_op jit(solution)/shard_map/pallas_call | solution.py:209
  79.6 3.4 %subtract_convert_fusion = bf16[2,1024,1024]{2,1,0:T(8,128)(2,1)} fusion(f32[2,1024,1024]{2,1,0:T(8,128)S(1)} %maximum_add_fusion, bf16[2,192,1024]{2,1,0:T(8,128)(2,1)S(1)} %get-tuple-element.8, bf16[2,192,1024]{2,1,0:T(8,128)(2,1)S(1)} %get-tuple-element.10), kind=kOutput, calls=%fused_computation.6 | convolution fusion | flops 809500672 | bytes 14155776 | tf_op jit(solution)/shard_map/bki,bkj->bij/dot_general | solution.py:267
  83.0 0.7 copy.10
  83.7 0.7 copy.11
Async XLA Ops:
  0.6 1.3 %copy-start = (bf16[640,1024]{1,0:T(8,128)(2,1)S(1)}, bf16[640,1024]{1,0:T(8,128)(2,1)}, u32[]{:S(2)}) copy-start(bf16[640,1024]{1,0:T(8,128)(2,1)} %param.5) | copy-start | bytes 3932164
  0.6 4.5 %copy-start.3 = (bf16[640,1024]{1,0:T(8,128)(2,1)S(1)}, bf16[640,1024]{1,0:T(8,128)(2,1)}, u32[]{:S(2)}) copy-start(bf16[640,1024]{1,0:T(8,128)(2,1)} %param.6) | copy-start | bytes 3932164
  5.1 2.2 %copy-start.1 = (bf16[2,1024,1024]{2,1,0:T(8,128)(2,1)S(1)}, bf16[2,1024,1024]{2,1,0:T(8,128)(2,1)}, u32[]{:S(2)}) copy-start(bf16[2,1024,1024]{2,1,0:T(8,128)(2,1)} %param.8) | copy-start | bytes 12582916
  7.3 2.2 %copy-start.2 = (f32[2,32,1024]{2,1,0:T(8,128)S(1)}, f32[2,32,1024]{2,1,0:T(8,128)}, u32[]{:S(2)}) copy-start(f32[2,32,1024]{2,1,0:T(8,128)} %param.9) | copy-start | bytes 786436

commit v10 on v9

--- a/solution.py
+++ b/solution.py
@@ -251,7 +251,8 @@
     replicas = nx * ny
     query_grad = lax.dot_general(normed, grad_query, CONTRACT, preferred_element_type=jnp.float32)
     key_grad = lax.dot_general(normed, grad_key, CONTRACT, preferred_element_type=jnp.float32)
-    merged = jnp.stack([query_grad, key_grad]) + error.astype(jnp.float32)
+    merged = jnp.stack([query_grad + error[0].astype(jnp.float32),
+                        key_grad + error[1].astype(jnp.float32)])
     m_hi, m_mid, m_lo = split3(merged)
     s_hi, s_mid, s_lo = split3(start_factor)
     left_local = combine6(*rows_times(

time: 84.5 us -> 82.7 us (0.979)
  local copies, waits for them, and re-layouts: 3.03 us -> 1.68 us
  other arithmetic: 2.21 us -> 1.11 us
    add x1 -> x0, other arithmetic: 2.15 us -> none  [on_device(): merged = jnp.stack([query_grad, key_grad]) + error.astype(jnp.float32)]
    dot_general x1, matrix products: 1.86 us -> 3.99 us  [on_device(): lax.dot_general(normed, grad_query, CONTRACT, preferred_element_type=jnp....]
    unnamed x10 -> x8, local copies, waits for them, and re-layouts: 3.03 us -> 1.68 us
    dot_general x1, matrix products: 3.15 us -> 1.85 us  [on_device(): lax.dot_general(normed, grad_key, CONTRACT, preferred_element_type=jnp.fl...]
    convert_element_type x1, other arithmetic: 0.06 us -> 1.11 us  [split3(): lo.astype(jnp.bfloat16)]
where the time goes in v10:
time: 82.7 us; the launch traced here: 82.6 us
  Pallas kernels  63.9 us (77%)
  matrix products  15.2 us (18%)
  local copies, waits for them, and re-layouts  1.68 us (2%)
  other arithmetic  1.11 us (1%)
    pallas_call x2, Pallas kernels, allreduce(): pl.pallas_call(functools.partial(allreduce_kernel, nx, ny, orthonormalize...  63.9 us
    dot_general x3, matrix products, rows_times(): jnp.einsum(spec, jnp.concatenate(group, axis=1), big, preferred_element_t...  4.47 us
    dot_general x1, matrix products, on_device(): lax.dot_general(normed, grad_query, CONTRACT, preferred_element_type=jnp....  3.99 us
    dot_general x1, matrix products, on_device(): jnp.einsum('bki,bkj->bij', lefts, rights, preferred_element_type=jnp.floa...  2.94 us
    dot_general x1, matrix products, on_device(): lax.dot_general(normed, grad_key, CONTRACT, preferred_element_type=jnp.fl...  1.85 us
    unnamed x8, local copies, waits for them, and re-layouts  1.68 us

profile of v10, /device:TPU:1, one launch (start us, length us, event | category | flops | bytes accessed | tf_op | source)
XLA Modules:
  0.0 82.6 jit_solution(13563005349472058327)
XLA Ops:
  0.6 0.0 copy-start
  0.6 1.1 %fusion.24 = (bf16[2,32,1024]{2,1,0:T(8,128)(2,1)S(1)}, bf16[2,32,1024]{2,1,0:T(8,128)(2,1)S(1)}, bf16[2,32,1024]{2,1,0:T(8,128)(2,1)S(1)}) fusion(f32[2,32,1024]{2,1,0:T(8,128)} %param.9), kind=kLoop, calls=%fused_computation.28 | loop fusion | flops 458752 | bytes 655360 | tf_op jit(solution)/shard_map/convert_element_type | solution.py:277
  1.8 0.3 copy-done
  2.0 0.0 copy-start.1
  2.0 0.0 copy-start.2
  2.0 4.0 %fusion.2 = f32[1,1024,1024]{2,1,0:T(8,128)S(1)} fusion(bf16[2,1024,1024]{2,1,0:T(8,128)(2,1)} %param.8, bf16[640,1024]{1,0:T(8,128)(2,1)S(1)} %copy-done, bf16[640,1024]{1,0:T(8,128)(2,1)} %param.6), kind=kOutput, calls=%fused_computation.10 | convolution fusion | flops 1344274432 | bytes 8912896 | tf_op jit(solution)/shard_map/dot_general | solution.py:252
  6.0 0.0 copy-done.1
  6.0 0.0 copy-done.2
  6.1 1.9 %fusion.1 = f32[1,1024,1024]{2,1,0:T(8,128)S(1)} fusion(bf16[2,1024,1024]{2,1,0:T(8,128)(2,1)S(1)} %copy-done.1, bf16[640,1024]{1,0:T(8,128)(2,1)S(1)} %copy-done, bf16[640,1024]{1,0:T(8,128)(2,1)S(1)} %copy-done.2), kind=kOutput, calls=%fused_computation.8 | convolution fusion | flops 1344274432 | bytes 8912896 | tf_op jit(solution)/shard_map/dot_general | solution.py:253
  7.9 1.4 %fusion.25 = f32[2,64,1024]{2,1,0:T(8,128)S(1)} fusion(bf16[2,32,1024]{2,1,0:T(8,128)(2,1)S(1)} %get-tuple-element.14, bf16[2,32,1024]{2,1,0:T(8,128)(2,1)S(1)} %get-tuple-element.15, f32[1,1024,1024]{2,1,0:T(8,128)S(1)} %fusion.1, f32[1,1024,1024]{2,1,0:T(8,128)S(1)} %fusion.2), kind=kOutput, calls=%fused_computation.31 | convolution fusion | flops 279445504 | bytes 9175040 | tf_op jit(solution)/shard_map/bkj,bij->bki/dot_general | solution.py:284
  9.3 1.4 %fusion.18 = f32[2,96,1024]{2,1,0:T(8,128)S(1)} fusion(bf16[2,32,1024]{2,1,0:T(8,128)(2,1)S(1)} %get-tuple-element.13, bf16[2,32,1024]{2,1,0:T(8,128)(2,1)S(1)} %get-tuple-element.14, bf16[2,32,1024]{2,1,0:T(8,128)(2,1)S(1)} %get-tuple-element.15, f32[1,1024,1024]{2,1,0:T(8,128)S(1)} %fusion.1, f32[1,1024,1024]{2,1,0:T(8,128)S(1)} %fusion.2), kind=kOutput, calls=%fused_computation.18 | convolution fusion | flops 410124288 | bytes 9568256 | tf_op jit(solution)/shard_map/bkj,bij->bki/dot_general | solution.py:284
  10.8 1.6 %fusion.15.x_ref = f32[2,32,1024]{2,1,0:T(8,128)S(1)} fusion(bf16[2,32,1024]{2,1,0:T(8,128)(2,1)S(1)} %get-tuple-element.15, f32[1,1024,1024]{2,1,0:T(8,128)S(1)} %fusion.1, f32[1,1024,1024]{2,1,0:T(8,128)S(1)} %fusion.2, f32[2,64,1024]{2,1,0:T(8,128)S(1)} %fusion.25, f32[2,96,1024]{2,1,0:T(8,128)S(1)} %fusion.18), kind=kOutput, calls=%fused_computation.17 | convolution fusion | flops 147128320 | bytes 10092544 | tf_op jit(solution)/shard_map/bkj,bij->bki/dot_general | solution.py:284
  12.4 38.0 %shard_map.76 = (f32[2,32,1024]{2,1,0:T(8,128)S(1)}, bf16[2,192,1024]{2,1,0:T(8,128)(2,1)S(1)}, bf16[2,64,1024]{2,1,0:T(8,128)(2,1)S(1)}) custom-call(f32[2,32,1024]{2,1,0:T(8,128)S(1)} %fusion.15.x_ref), custom_call_target="tpu_custom_call" | custom-call | tf_op jit(solution)/shard_map/pallas_call | solution.py:209
  50.4 1.0 %fusion.30 = f32[2,64,1024]{2,1,0:T(8,128)S(1)} fusion(bf16[2,64,1024]{2,1,0:T(8,128)(2,1)S(1)} %get-tuple-element.9, f32[1,1024,1024]{2,1,0:T(8,128)S(1)} %fusion.1, f32[1,1024,1024]{2,1,0:T(8,128)S(1)} %fusion.2), kind=kOutput, calls=%fused_computation.36 | convolution fusion | flops 274726912 | bytes 9175040 | tf_op jit(solution)/shard_map/bki,bij->bkj/dot_general | solution.py:263
  51.4 0.9 %fusion.5.x_ref = f32[2,32,1024]{2,1,0:T(8,128)S(1)} fusion(f32[2,64,1024]{2,1,0:T(8,128)S(1)} %fusion.30, bf16[2,192,1024]{2,1,0:T(8,128)(2,1)S(1)} %get-tuple-element.8, f32[1,1024,1024]{2,1,0:T(8,128)S(1)} %fusion.1, f32[1,1024,1024]{2,1,0:T(8,128)S(1)} %fusion.2), kind=kOutput, calls=%fused_computation.13 | convolution fusion | flops 144834560 | bytes 9306112 | tf_op jit(solution)/shard_map/bki,bij->bkj/dot_general | solution.py:264
  52.4 25.9 %shard_map.77 = (f32[2,32,1024]{2,1,0:T(8,128)S(1)}, bf16[2,192,1024]{2,1,0:T(8,128)(2,1)S(1)}) custom-call(f32[2,32,1024]{2,1,0:T(8,128)S(1)} %fusion.5.x_ref), custom_call_target="tpu_custom_call" | custom-call | tf_op jit(solution)/shard_map/pallas_call | solution.py:209
  78.3 2.9 %subtract_convert_fusion = bf16[2,1024,1024]{2,1,0:T(8,128)(2,1)} fusion(f32[1,1024,1024]{2,1,0:T(8,128)S(1)} %fusion.1, f32[1,1024,1024]{2,1,0:T(8,128)S(1)} %fusion.2, bf16[2,192,1024]{2,1,0:T(8,128)(2,1)S(1)} %get-tuple-element.8, bf16[2,192,1024]{2,1,0:T(8,128)(2,1)S(1)} %get-tuple-element.10), kind=kOutput, calls=%fused_computation.6 | convolution fusion | flops 811597824 | bytes 14155776 | tf_op jit(solution)/shard_map/bki,bkj->bij/dot_general | solution.py:268
  81.2 0.7 copy.10
  81.9 0.7 copy.11
Async XLA Ops:
  0.6 1.4 %copy-start = (bf16[640,1024]{1,0:T(8,128)(2,1)S(1)}, bf16[640,1024]{1,0:T(8,128)(2,1)}, u32[]{:S(2)}) copy-start(bf16[640,1024]{1,0:T(8,128)(2,1)} %param.5) | copy-start | bytes 3932164
  2.0 4.0 %copy-start.1 = (bf16[2,1024,1024]{2,1,0:T(8,128)(2,1)S(1)}, bf16[2,1024,1024]{2,1,0:T(8,128)(2,1)}, u32[]{:S(2)}) copy-start(bf16[2,1024,1024]{2,1,0:T(8,128)(2,1)} %param.8) | copy-start | bytes 12582916
  2.0 4.0 %copy-start.2 = (bf16[640,1024]{1,0:T(8,128)(2,1)S(1)}, bf16[640,1024]{1,0:T(8,128)(2,1)}, u32[]{:S(2)}) copy-start(bf16[640,1024]{1,0:T(8,128)(2,1)} %param.7) | copy-start | bytes 3932164

commit v11 on v9

--- a/solution.py
+++ b/solution.py
@@ -32,7 +32,7 @@
 
 
 def allreduce_body(nx, ny, orthonormalize, divisor, x_ref, o_ref, recv_a, p_t, recv_b, recv_c, recv_d,
-                     sa, ra, sb, rb, sc, rc, sd, rd):
+                     sa, ra, sb, rb, sc, rc, sd, rd, with_barrier=True):
     h = lax.axis_index("gx")
     a = lax.axis_index("gy")
     nb, rows = x_ref.shape[0], x_ref.shape[1]
@@ -51,9 +51,10 @@
                             device_id_type=MESH_ID)
         return carry
 
-    lax.fori_loop(1, ny, signal_y, 0)
-    lax.fori_loop(1, nx, signal_x, 0)
-    pl.semaphore_wait(barrier, (ny - 1) + (nx - 1))
+    if with_barrier:
+        lax.fori_loop(1, ny, signal_y, 0)
+        lax.fori_loop(1, nx, signal_x, 0)
+        pl.semaphore_wait(barrier, (ny - 1) + (nx - 1))
 
     def copy_a(peer, slot_src):
         return pltpu.make_async_remote_copy(
@@ -198,6 +199,86 @@
     for b in range(nb):
         rows_ref[b] = jnp.dot(inverse[b], rows_ref[b], precision=HIGHEST,
                               preferred_element_type=jnp.float32)
+
+
+def write_pieces(value_ref, patterns, stacked):
+    for b in range(value_ref.shape[0]):
+        value = value_ref[b]
+        k = value.shape[0]
+        hi = value.astype(jnp.bfloat16)
+        rest = value - hi.astype(jnp.float32)
+        mid = rest.astype(jnp.bfloat16)
+        lo = (rest - mid.astype(jnp.float32)).astype(jnp.bfloat16)
+        parts = (hi, mid, lo)
+        for pattern, out_ref in zip(patterns, stacked):
+            for g, piece in enumerate(pattern):
+                out_ref[b, g * k:(g + 1) * k, :] = parts[piece]
+
+
+def factors_kernel(nx, ny, divisor, x_ref, mq_ref, mk_ref, left_ref, lefts_ref, right_ref,
+                   rights_ref, pair_ref, local_ref, *scratch):
+    first, second = scratch[:13], scratch[13:]
+    allreduce_body(nx, ny, True, None, x_ref, left_ref, *first)
+    write_pieces(left_ref, ((0, 0, 1, 0, 1, 2), (0, 1)), (lefts_ref, pair_ref))
+    k = left_ref.shape[1]
+    width = 256
+    for b, m_ref in enumerate((mq_ref, mk_ref)):
+        pair = pair_ref[b]
+        top = lefts_ref[b, :k, :]
+        for c in range(m_ref.shape[1] // width):
+            block = m_ref[:, c * width:(c + 1) * width]
+            hi = block.astype(jnp.bfloat16)
+            mid = (block - hi.astype(jnp.float32)).astype(jnp.bfloat16)
+            both = jnp.dot(pair, hi, preferred_element_type=jnp.float32)
+            cross = jnp.dot(top, mid, preferred_element_type=jnp.float32)
+            local_ref[b, :, c * width:(c + 1) * width] = both[:k] + (both[k:] + cross)
+    allreduce_body(nx, ny, False, divisor, local_ref, right_ref, *second, with_barrier=False)
+    write_pieces(right_ref, ((0, 1, 0, 2, 1, 0),), (rights_ref,))
+
+
+def allreduce_scratch(nx, ny, nb, rows):
+    vmem = pltpu.VMEM
+    nt = nb * (rows // SUB)
+    return [
+        vmem((ny, nb, rows, LANES), jnp.float32),
+        vmem((nt, SUB, LANES), jnp.float32),
+        vmem((nx, SUB, LANES), jnp.float32),
+        vmem((nt, SUB, LANES), jnp.float32),
+        vmem((ny, nb, rows, LANES), jnp.float32),
+        pltpu.SemaphoreType.DMA((ny,)),
+        pltpu.SemaphoreType.DMA((ny,)),
+        pltpu.SemaphoreType.DMA((nx,)),
+        pltpu.SemaphoreType.DMA((nx,)),
+        pltpu.SemaphoreType.DMA((nt,)),
+        pltpu.SemaphoreType.DMA((nt,)),
+        pltpu.SemaphoreType.DMA((ny,)),
+        pltpu.SemaphoreType.DMA((ny,)),
+    ]
+
+
+def factors(x, query_merged, key_merged, nx, ny, divisor):
+    nb, rows, cols = x.shape
+    assert cols == ny * LANES and rows % SUB == 0
+    assert nx % (nb * (rows // SUB)) == 0
+    vmem = pltpu.VMEM
+    f32, bf16 = jnp.float32, jnp.bfloat16
+    return pl.pallas_call(
+        functools.partial(factors_kernel, nx, ny, divisor),
+        out_shape=[
+            jax.ShapeDtypeStruct(x.shape, f32),
+            jax.ShapeDtypeStruct((nb, 6 * rows, cols), bf16),
+            jax.ShapeDtypeStruct(x.shape, f32),
+            jax.ShapeDtypeStruct((nb, 6 * rows, cols), bf16),
+        ],
+        in_specs=[pl.BlockSpec(memory_space=vmem)] * 3,
+        out_specs=[pl.BlockSpec(memory_space=vmem)] * 4,
+        scratch_shapes=[vmem((nb, 2 * rows, cols), bf16), vmem(x.shape, f32)]
+        + allreduce_scratch(nx, ny, nb, rows) + allreduce_scratch(nx, ny, nb, rows),
+        compiler_params=pltpu.CompilerParams(
+            collective_id=0, has_side_effects=True,
+            vmem_limit_bytes=24 * 1024 * 1024,
+        ),
+    )(x, query_merged, key_merged)
 
 
 def allreduce(x, nx, ny, collective_id, orthonormalize=False, divisor=None, patterns=()):
@@ -251,19 +332,15 @@
     replicas = nx * ny
     query_grad = lax.dot_general(normed, grad_query, CONTRACT, preferred_element_type=jnp.float32)
     key_grad = lax.dot_general(normed, grad_key, CONTRACT, preferred_element_type=jnp.float32)
-    merged = jnp.stack([query_grad, key_grad]) + error.astype(jnp.float32)
+    query_merged = query_grad + error[0].astype(jnp.float32)
+    key_merged = key_grad + error[1].astype(jnp.float32)
+    merged = jnp.stack([query_merged, key_merged])
     m_hi, m_mid, m_lo = split3(merged)
     s_hi, s_mid, s_lo = split3(start_factor)
     left_local = combine6(*rows_times(
         [[s_hi, s_mid, s_lo], [s_hi, s_mid], [s_hi]], [m_hi, m_mid, m_lo], "bkj,bij->bki"))
-    left_rows, lefts, left_pair = allreduce(
-        left_local, nx, ny, 0, orthonormalize=True, patterns=((0, 0, 1, 0, 1, 2), (0, 1)))
-    k = left_rows.shape[1]
-    pair = jnp.einsum("bki,bij->bkj", left_pair, m_hi, preferred_element_type=jnp.float32)
-    cross = jnp.einsum("bki,bij->bkj", lefts[:, :k], m_mid, preferred_element_type=jnp.float32)
-    right_local = pair[:, :k] + (pair[:, k:] + cross)
-    right_rows, rights = allreduce(
-        right_local, nx, ny, 1, divisor=float(replicas), patterns=((0, 1, 0, 2, 1, 0),))
+    left_rows, lefts, right_rows, rights = factors(
+        left_local, query_merged, key_merged, nx, ny, float(replicas))
     approx = jnp.einsum("bki,bkj->bij", lefts, rights, preferred_element_type=jnp.float32)
     return ((merged - approx).astype(jnp.bfloat16), left_rows, right_rows)
 

time: 84.5 us -> 80.6 us (0.954)
  local copies, waits for them, and re-layouts: 3.03 us -> 1.69 us
  matrix products: 14.5 us -> 13.3 us
  other arithmetic: 2.21 us -> 1.11 us
    add x1 -> x0, other arithmetic: 2.15 us -> none  [on_device(): merged = jnp.stack([query_grad, key_grad]) + error.astype(jnp.float32)]
    dot_general x1, matrix products: 1.86 us -> 3.99 us  [on_device(): lax.dot_general(normed, grad_query, CONTRACT, preferred_element_type=jnp....]
    dot_general x2 -> x0, matrix products: 1.8 us -> none  [the longest x1 0.94 us: on_device(): jnp.einsum('bki,bij->bkj', lefts[:, :k], m_mid, preferred_element_type=jn...]
    unnamed x10 -> x8, local copies, waits for them, and re-layouts: 3.03 us -> 1.69 us
    dot_general x1, matrix products: 3.15 us -> 1.9 us  [on_device(): lax.dot_general(normed, grad_key, CONTRACT, preferred_element_type=jnp.fl...]
    convert_element_type x1, other arithmetic: 0.06 us -> 1.11 us  [split3(): lo.astype(jnp.bfloat16)]
    pallas_call x2 -> x1, Pallas kernels: 63.9 us -> 63.6 us  [factors(): pl.pallas_call(functools.partial(factors_kernel, nx, ny, divisor), out_sh...]
where the time goes in v11:
time: 80.6 us; the launch traced here: 80.5 us
  Pallas kernels  63.6 us (79%)
  matrix products  13.3 us (17%)
  local copies, waits for them, and re-layouts  1.69 us (2%)
  other arithmetic  1.11 us (1%)
    pallas_call x1, Pallas kernels, factors(): pl.pallas_call(functools.partial(factors_kernel, nx, ny, divisor), out_sh...  63.6 us
    dot_general x3, matrix products, rows_times(): jnp.einsum(spec, jnp.concatenate(group, axis=1), big, preferred_element_t...  4.44 us
    dot_general x1, matrix products, on_device(): lax.dot_general(normed, grad_query, CONTRACT, preferred_element_type=jnp....  3.99 us
    dot_general x1, matrix products, on_device(): jnp.einsum('bki,bkj->bij', lefts, rights, preferred_element_type=jnp.floa...  2.99 us
    dot_general x1, matrix products, on_device(): lax.dot_general(normed, grad_key, CONTRACT, preferred_element_type=jnp.fl...  1.9 us
    unnamed x8, local copies, waits for them, and re-layouts  1.69 us

profile of v11, /device:TPU:1, one launch (start us, length us, event | category | flops | bytes accessed | tf_op | source)
XLA Modules:
  0.0 80.5 jit_solution(1989318461212911761)
XLA Ops:
  0.6 0.0 copy-start
  0.6 1.1 %fusion.22 = (bf16[2,32,1024]{2,1,0:T(8,128)(2,1)S(1)}, bf16[2,32,1024]{2,1,0:T(8,128)(2,1)S(1)}, bf16[2,32,1024]{2,1,0:T(8,128)(2,1)S(1)}) fusion(f32[2,32,1024]{2,1,0:T(8,128)} %param.9), kind=kLoop, calls=%fused_computation.25 | loop fusion | flops 458752 | bytes 655360 | tf_op jit(solution)/shard_map/convert_element_type | solution.py:353
  1.8 0.3 copy-done
  2.0 0.0 copy-start.1
  2.0 0.0 copy-start.2
  2.0 4.0 %convert_add_fusion.1.mq_ref = f32[1024,1024]{1,0:T(8,128)S(1)} fusion(bf16[2,1024,1024]{2,1,0:T(8,128)(2,1)} %param.8, bf16[640,1024]{1,0:T(8,128)(2,1)S(1)} %copy-done, bf16[640,1024]{1,0:T(8,128)(2,1)} %param.6), kind=kOutput, calls=%fused_computation.9 | convolution fusion | flops 1344274432 | bytes 8912896 | tf_op jit(solution)/shard_map/dot_general | solution.py:333
  6.0 0.0 copy-done.1
  6.0 0.0 copy-done.2
  6.1 1.9 %convert_add_fusion.mk_ref = f32[1024,1024]{1,0:T(8,128)S(1)} fusion(bf16[2,1024,1024]{2,1,0:T(8,128)(2,1)S(1)} %copy-done.1, bf16[640,1024]{1,0:T(8,128)(2,1)S(1)} %copy-done, bf16[640,1024]{1,0:T(8,128)(2,1)S(1)} %copy-done.2), kind=kOutput, calls=%fused_computation.8 | convolution fusion | flops 1344274432 | bytes 8912896 | tf_op jit(solution)/shard_map/dot_general | solution.py:334
  8.0 1.4 %fusion.2 = f32[2,64,1024]{2,1,0:T(8,128)S(1)} fusion(f32[1,1024,1024]{2,1,0:T(8,128)S(1)} %bitcast.27, f32[1,1024,1024]{2,1,0:T(8,128)S(1)} %bitcast.23, bf16[2,32,1024]{2,1,0:T(8,128)(2,1)S(1)} %get-tuple-element.12, bf16[2,32,1024]{2,1,0:T(8,128)(2,1)S(1)} %get-tuple-element.13), kind=kOutput, calls=%fused_computation.10 | convolution fusion | flops 279445504 | bytes 9175040 | tf_op jit(solution)/shard_map/bkj,bij->bki/dot_general | solution.py:360
  9.4 1.4 %fusion.1 = f32[2,96,1024]{2,1,0:T(8,128)S(1)} fusion(f32[1,1024,1024]{2,1,0:T(8,128)S(1)} %bitcast.28, f32[1,1024,1024]{2,1,0:T(8,128)S(1)} %bitcast.24, bf16[2,32,1024]{2,1,0:T(8,128)(2,1)S(1)} %get-tuple-element.11, bf16[2,32,1024]{2,1,0:T(8,128)(2,1)S(1)} %get-tuple-element.12, bf16[2,32,1024]{2,1,0:T(8,128)(2,1)S(1)} %get-tuple-element.13), kind=kOutput, calls=%fused_computation.7 | convolution fusion | flops 410124288 | bytes 9568256 | tf_op jit(solution)/shard_map/bkj,bij->bki/dot_general | solution.py:360
  10.8 1.6 %fusion.14.x_ref = f32[2,32,1024]{2,1,0:T(8,128)S(1)} fusion(bf16[2,32,1024]{2,1,0:T(8,128)(2,1)S(1)} %get-tuple-element.13, f32[1,1024,1024]{2,1,0:T(8,128)S(1)} %bitcast.29, f32[1,1024,1024]{2,1,0:T(8,128)S(1)} %bitcast.25, f32[2,64,1024]{2,1,0:T(8,128)S(1)} %fusion.2, f32[2,96,1024]{2,1,0:T(8,128)S(1)} %fusion.1), kind=kOutput, calls=%fused_computation.15 | convolution fusion | flops 147128320 | bytes 10092544 | tf_op jit(solution)/shard_map/bkj,bij->bki/dot_general | solution.py:360
  12.4 63.6 %shard_map.76 = (f32[2,32,1024]{2,1,0:T(8,128)S(1)}, bf16[2,192,1024]{2,1,0:T(8,128)(2,1)S(1)}, f32[2,32,1024]{2,1,0:T(8,128)S(1)}, bf16[2,192,1024]{2,1,0:T(8,128)(2,1)S(1)}) custom-call(f32[2,32,1024]{2,1,0:T(8,128)S(1)} %fusion.14.x_ref, f32[1024,1024]{1,0:T(8,128)S(1)} %convert_add_fusion.1.mq_ref, f32[1024,1024]{1,0:T(8,128)S(1)} %convert_add_fusion.mk_ref), custom_call_target="tpu_custom_call" | custom-call | tf_op jit(solution)/shard_map/pallas_call | solution.py:265
  76.1 3.0 %subtract_convert_fusion = bf16[2,1024,1024]{2,1,0:T(8,128)(2,1)} fusion(f32[1,1024,1024]{2,1,0:T(8,128)S(1)} %bitcast.30, f32[1,1024,1024]{2,1,0:T(8,128)S(1)} %bitcast.26, bf16[2,192,1024]{2,1,0:T(8,128)(2,1)S(1)} %get-tuple-element.7, bf16[2,192,1024]{2,1,0:T(8,128)(2,1)S(1)} %get-tuple-element.8), kind=kOutput, calls=%fused_computation.6 | convolution fusion | flops 811597824 | bytes 14155776 | tf_op jit(solution)/shard_map/bki,bkj->bij/dot_general | solution.py:344
  79.1 0.7 copy.10
  79.8 0.7 copy.11
Async XLA Ops:
  0.6 1.4 %copy-start = (bf16[640,1024]{1,0:T(8,128)(2,1)S(1)}, bf16[640,1024]{1,0:T(8,128)(2,1)}, u32[]{:S(2)}) copy-start(bf16[640,1024]{1,0:T(8,128)(2,1)} %param.5) | copy-start | bytes 3932164
  2.0 4.0 %copy-start.1 = (bf16[2,1024,1024]{2,1,0:T(8,128)(2,1)S(1)}, bf16[2,1024,1024]{2,1,0:T(8,128)(2,1)}, u32[]{:S(2)}) copy-start(bf16[2,1024,1024]{2,1,0:T(8,128)(2,1)} %param.8) | copy-start | bytes 12582916
  2.0 4.0 %copy-start.2 = (bf16[640,1024]{1,0:T(8,128)(2,1)S(1)}, bf16[640,1024]{1,0:T(8,128)(2,1)}, u32[]{:S(2)}) copy-start(bf16[640,1024]{1,0:T(8,128)(2,1)} %param.7) | copy-start | bytes 3932164

commit v12 on v11

--- a/solution.py
+++ b/solution.py
@@ -127,17 +127,16 @@
         copy_c(lax.rem(own + j, nt), own).start()
         return carry
 
-    lax.fori_loop(1, nt, start_c, 0)
-
-    def wait_c(j, carry):
-        other = lax.rem(own + j, nt)
-        copy_c(other, own).wait_send()
-        copy_c(own, other).wait_recv()
-        return carry
-
-    lax.fori_loop(1, nt, wait_c, 0)
-    for u in range(nt):
-        recv_d[a, u // kb, (u % kb) * SUB:(u % kb + 1) * SUB, :] = recv_c[u]
+    def copy_d_tile(peer, tile):
+        row0 = pl.multiple_of(lax.rem(tile, kb) * SUB, SUB)
+        return pltpu.make_async_remote_copy(
+            src_ref=recv_c.at[tile],
+            dst_ref=recv_d.at[a, tile // kb, pl.ds(row0, SUB), :],
+            send_sem=sd.at[peer],
+            recv_sem=rd.at[a],
+            device_id=(h, peer),
+            device_id_type=MESH_ID,
+        )
 
     def copy_d(peer, slot_src):
         return pltpu.make_async_remote_copy(
@@ -149,11 +148,29 @@
             device_id_type=MESH_ID,
         )
 
-    def start_d(j, carry):
-        copy_d(lax.rem(a + j, ny), a).start()
-        return carry
-
-    lax.fori_loop(1, ny, start_d, 0)
+    def forward(tile):
+        def start_d(j, carry):
+            copy_d_tile(lax.rem(a + j, ny), tile).start()
+            return carry
+
+        lax.fori_loop(1, ny, start_d, 0)
+
+    lax.fori_loop(1, nt, start_c, 0)
+    forward(own)
+
+    def wait_c(j, carry):
+        other = lax.rem(own + j, nt)
+        copy_c(own, other).wait_recv()
+        forward(other)
+        return carry
+
+    lax.fori_loop(1, nt, wait_c, 0)
+
+    def wait_c_send(j, carry):
+        copy_c(lax.rem(own + j, nt), own).wait_send()
+        return carry
+
+    lax.fori_loop(1, nt, wait_c_send, 0)
 
     def wait_d(j, carry):
         copy_d(lax.rem(a + j, ny), a).wait_send()
@@ -161,6 +178,8 @@
         return carry
 
     lax.fori_loop(1, ny, wait_d, 0)
+    for u in range(nt):
+        recv_d[a, u // kb, (u % kb) * SUB:(u % kb + 1) * SUB, :] = recv_c[u]
     for s in range(ny):
         block = recv_d[s]
         if divisor is not None:

time: 80.6 us -> 79.6 us (0.988)
  Pallas kernels: 63.6 us -> 62.7 us
    pallas_call x1, Pallas kernels: 63.6 us -> 62.7 us  [factors(): pl.pallas_call(functools.partial(factors_kernel, nx, ny, divisor), out_sh...]
where the time goes in v12:
time: 79.6 us; the launch traced here: 79.5 us
  Pallas kernels  62.7 us (79%)
  matrix products  13.3 us (17%)
  local copies, waits for them, and re-layouts  1.69 us (2%)
  other arithmetic  1.11 us (1%)
    pallas_call x1, Pallas kernels, factors(): pl.pallas_call(functools.partial(factors_kernel, nx, ny, divisor), out_sh...  62.7 us
    dot_general x3, matrix products, rows_times(): jnp.einsum(spec, jnp.concatenate(group, axis=1), big, preferred_element_t...  4.44 us
    dot_general x1, matrix products, on_device(): lax.dot_general(normed, grad_query, CONTRACT, preferred_element_type=jnp....  3.99 us
    dot_general x1, matrix products, on_device(): jnp.einsum('bki,bkj->bij', lefts, rights, preferred_element_type=jnp.floa...  2.99 us
    dot_general x1, matrix products, on_device(): lax.dot_general(normed, grad_key, CONTRACT, preferred_element_type=jnp.fl...  1.9 us
    unnamed x8, local copies, waits for them, and re-layouts  1.69 us

profile of v12, /device:TPU:1, one launch (start us, length us, event | category | flops | bytes accessed | tf_op | source)
XLA Modules:
  0.0 79.5 jit_solution(12480047445530370957)
XLA Ops:
  0.6 0.0 copy-start
  0.6 1.1 %fusion.22 = (bf16[2,32,1024]{2,1,0:T(8,128)(2,1)S(1)}, bf16[2,32,1024]{2,1,0:T(8,128)(2,1)S(1)}, bf16[2,32,1024]{2,1,0:T(8,128)(2,1)S(1)}) fusion(f32[2,32,1024]{2,1,0:T(8,128)} %param.9), kind=kLoop, calls=%fused_computation.25 | loop fusion | flops 458752 | bytes 655360 | tf_op jit(solution)/shard_map/convert_element_type | solution.py:372
  1.8 0.3 copy-done
  2.0 0.0 copy-start.1
  2.0 0.0 copy-start.2
  2.0 4.0 %convert_add_fusion.1.mq_ref = f32[1024,1024]{1,0:T(8,128)S(1)} fusion(bf16[2,1024,1024]{2,1,0:T(8,128)(2,1)} %param.8, bf16[640,1024]{1,0:T(8,128)(2,1)S(1)} %copy-done, bf16[640,1024]{1,0:T(8,128)(2,1)} %param.6), kind=kOutput, calls=%fused_computation.9 | convolution fusion | flops 1344274432 | bytes 8912896 | tf_op jit(solution)/shard_map/dot_general | solution.py:352
  6.0 0.0 copy-done.1
  6.0 0.0 copy-done.2
  6.1 1.9 %convert_add_fusion.mk_ref = f32[1024,1024]{1,0:T(8,128)S(1)} fusion(bf16[2,1024,1024]{2,1,0:T(8,128)(2,1)S(1)} %copy-done.1, bf16[640,1024]{1,0:T(8,128)(2,1)S(1)} %copy-done, bf16[640,1024]{1,0:T(8,128)(2,1)S(1)} %copy-done.2), kind=kOutput, calls=%fused_computation.8 | convolution fusion | flops 1344274432 | bytes 8912896 | tf_op jit(solution)/shard_map/dot_general | solution.py:353
  8.0 1.4 %fusion.2 = f32[2,64,1024]{2,1,0:T(8,128)S(1)} fusion(f32[1,1024,1024]{2,1,0:T(8,128)S(1)} %bitcast.27, f32[1,1024,1024]{2,1,0:T(8,128)S(1)} %bitcast.23, bf16[2,32,1024]{2,1,0:T(8,128)(2,1)S(1)} %get-tuple-element.12, bf16[2,32,1024]{2,1,0:T(8,128)(2,1)S(1)} %get-tuple-element.13), kind=kOutput, calls=%fused_computation.10 | convolution fusion | flops 279445504 | bytes 9175040 | tf_op jit(solution)/shard_map/bkj,bij->bki/dot_general | solution.py:379
  9.4 1.4 %fusion.1 = f32[2,96,1024]{2,1,0:T(8,128)S(1)} fusion(f32[1,1024,1024]{2,1,0:T(8,128)S(1)} %bitcast.28, f32[1,1024,1024]{2,1,0:T(8,128)S(1)} %bitcast.24, bf16[2,32,1024]{2,1,0:T(8,128)(2,1)S(1)} %get-tuple-element.11, bf16[2,32,1024]{2,1,0:T(8,128)(2,1)S(1)} %get-tuple-element.12, bf16[2,32,1024]{2,1,0:T(8,128)(2,1)S(1)} %get-tuple-element.13), kind=kOutput, calls=%fused_computation.7 | convolution fusion | flops 410124288 | bytes 9568256 | tf_op jit(solution)/shard_map/bkj,bij->bki/dot_general | solution.py:379
  10.8 1.6 %fusion.14.x_ref = f32[2,32,1024]{2,1,0:T(8,128)S(1)} fusion(bf16[2,32,1024]{2,1,0:T(8,128)(2,1)S(1)} %get-tuple-element.13, f32[1,1024,1024]{2,1,0:T(8,128)S(1)} %bitcast.29, f32[1,1024,1024]{2,1,0:T(8,128)S(1)} %bitcast.25, f32[2,64,1024]{2,1,0:T(8,128)S(1)} %fusion.2, f32[2,96,1024]{2,1,0:T(8,128)S(1)} %fusion.1), kind=kOutput, calls=%fused_computation.15 | convolution fusion | flops 147128320 | bytes 10092544 | tf_op jit(solution)/shard_map/bkj,bij->bki/dot_general | solution.py:379
  12.4 62.7 %shard_map.76 = (f32[2,32,1024]{2,1,0:T(8,128)S(1)}, bf16[2,192,1024]{2,1,0:T(8,128)(2,1)S(1)}, f32[2,32,1024]{2,1,0:T(8,128)S(1)}, bf16[2,192,1024]{2,1,0:T(8,128)(2,1)S(1)}) custom-call(f32[2,32,1024]{2,1,0:T(8,128)S(1)} %fusion.14.x_ref, f32[1024,1024]{1,0:T(8,128)S(1)} %convert_add_fusion.1.mq_ref, f32[1024,1024]{1,0:T(8,128)S(1)} %convert_add_fusion.mk_ref), custom_call_target="tpu_custom_call" | custom-call | tf_op jit(solution)/shard_map/pallas_call | solution.py:284
  75.1 3.0 %subtract_convert_fusion = bf16[2,1024,1024]{2,1,0:T(8,128)(2,1)} fusion(f32[1,1024,1024]{2,1,0:T(8,128)S(1)} %bitcast.30, f32[1,1024,1024]{2,1,0:T(8,128)S(1)} %bitcast.26, bf16[2,192,1024]{2,1,0:T(8,128)(2,1)S(1)} %get-tuple-element.7, bf16[2,192,1024]{2,1,0:T(8,128)(2,1)S(1)} %get-tuple-element.8), kind=kOutput, calls=%fused_computation.6 | convolution fusion | flops 811597824 | bytes 14155776 | tf_op jit(solution)/shard_map/bki,bkj->bij/dot_general | solution.py:363
  78.1 0.7 copy.10
  78.8 0.7 copy.11
Async XLA Ops:
  0.6 1.4 %copy-start = (bf16[640,1024]{1,0:T(8,128)(2,1)S(1)}, bf16[640,1024]{1,0:T(8,128)(2,1)}, u32[]{:S(2)}) copy-start(bf16[640,1024]{1,0:T(8,128)(2,1)} %param.5) | copy-start | bytes 3932164
  2.0 4.0 %copy-start.1 = (bf16[2,1024,1024]{2,1,0:T(8,128)(2,1)S(1)}, bf16[2,1024,1024]{2,1,0:T(8,128)(2,1)}, u32[]{:S(2)}) copy-start(bf16[2,1024,1024]{2,1,0:T(8,128)(2,1)} %param.8) | copy-start | bytes 12582916
  2.0 4.0 %copy-start.2 = (bf16[640,1024]{1,0:T(8,128)(2,1)S(1)}, bf16[640,1024]{1,0:T(8,128)(2,1)}, u32[]{:S(2)}) copy-start(bf16[640,1024]{1,0:T(8,128)(2,1)} %param.7) | copy-start | bytes 3932164

commit v13 on v12

--- a/solution.py
+++ b/solution.py
@@ -32,7 +32,7 @@
 
 
 def allreduce_body(nx, ny, orthonormalize, divisor, x_ref, o_ref, recv_a, p_t, recv_b, recv_c, recv_d,
-                     sa, ra, sb, rb, sc, rc, sd, rd, with_barrier=True):
+                     sa, ra, sb, rb, sc, rc, sd, rd, with_barrier=True, idle_work=None):
     h = lax.axis_index("gx")
     a = lax.axis_index("gy")
     nb, rows = x_ref.shape[0], x_ref.shape[1]
@@ -72,6 +72,8 @@
 
     lax.fori_loop(1, ny, start_a, 0)
     recv_a[a] = x_ref[:, :, pl.ds(pl.multiple_of(a * LANES, LANES), LANES)]
+    if idle_work is not None:
+        idle_work()
 
     def wait_a(j, carry):
         copy_a(lax.rem(a + j, ny), a).wait_send()
@@ -235,22 +237,27 @@
 
 
 def factors_kernel(nx, ny, divisor, x_ref, mq_ref, mk_ref, left_ref, lefts_ref, right_ref,
-                   rights_ref, pair_ref, local_ref, *scratch):
+                   rights_ref, pair_ref, local_ref, m_hi_ref, m_mid_ref, *scratch):
     first, second = scratch[:13], scratch[13:]
-    allreduce_body(nx, ny, True, None, x_ref, left_ref, *first)
+    width = 256
+    merged_refs = (mq_ref, mk_ref)
+
+    def split_merged():
+        for b, m_ref in enumerate(merged_refs):
+            for c in range(m_ref.shape[1] // width):
+                block = m_ref[:, c * width:(c + 1) * width]
+                hi = block.astype(jnp.bfloat16)
+                m_hi_ref[b, :, c * width:(c + 1) * width] = hi
+                m_mid_ref[b, :, c * width:(c + 1) * width] = (
+                    block - hi.astype(jnp.float32)).astype(jnp.bfloat16)
+
+    allreduce_body(nx, ny, True, None, x_ref, left_ref, *first, idle_work=split_merged)
     write_pieces(left_ref, ((0, 0, 1, 0, 1, 2), (0, 1)), (lefts_ref, pair_ref))
     k = left_ref.shape[1]
-    width = 256
-    for b, m_ref in enumerate((mq_ref, mk_ref)):
-        pair = pair_ref[b]
-        top = lefts_ref[b, :k, :]
-        for c in range(m_ref.shape[1] // width):
-            block = m_ref[:, c * width:(c + 1) * width]
-            hi = block.astype(jnp.bfloat16)
-            mid = (block - hi.astype(jnp.float32)).astype(jnp.bfloat16)
-            both = jnp.dot(pair, hi, preferred_element_type=jnp.float32)
-            cross = jnp.dot(top, mid, preferred_element_type=jnp.float32)
-            local_ref[b, :, c * width:(c + 1) * width] = both[:k] + (both[k:] + cross)
+    for b in range(len(merged_refs)):
+        both = jnp.dot(pair_ref[b], m_hi_ref[b], preferred_element_type=jnp.float32)
+        cross = jnp.dot(lefts_ref[b, :k, :], m_mid_ref[b], preferred_element_type=jnp.float32)
+        local_ref[b] = both[:k] + (both[k:] + cross)
     allreduce_body(nx, ny, False, divisor, local_ref, right_ref, *second, with_barrier=False)
     write_pieces(right_ref, ((0, 1, 0, 2, 1, 0),), (rights_ref,))
 
@@ -291,7 +298,8 @@
         ],
         in_specs=[pl.BlockSpec(memory_space=vmem)] * 3,
         out_specs=[pl.BlockSpec(memory_space=vmem)] * 4,
-        scratch_shapes=[vmem((nb, 2 * rows, cols), bf16), vmem(x.shape, f32)]
+        scratch_shapes=[vmem((nb, 2 * rows, cols), bf16), vmem(x.shape, f32),
+                        vmem((2,) + query_merged.shape, bf16), vmem((2,) + query_merged.shape, bf16)]
         + allreduce_scratch(nx, ny, nb, rows) + allreduce_scratch(nx, ny, nb, rows),
         compiler_params=pltpu.CompilerParams(
             collective_id=0, has_side_effects=True,

time: 79.6 us -> 79 us (level)
  no operation moved by 1% of the time
where the time goes in v13:
time: 79 us; the launch traced here: 78.9 us
  Pallas kernels  62.1 us (79%)
  matrix products  13.3 us (17%)
  local copies, waits for them, and re-layouts  1.69 us (2%)
  other arithmetic  1.11 us (1%)
    pallas_call x1, Pallas kernels, factors(): pl.pallas_call(functools.partial(factors_kernel, nx, ny, divisor), out_sh...  62.1 us
    dot_general x3, matrix products, rows_times(): jnp.einsum(spec, jnp.concatenate(group, axis=1), big, preferred_element_t...  4.44 us
    dot_general x1, matrix products, on_device(): lax.dot_general(normed, grad_query, CONTRACT, preferred_element_type=jnp....  3.99 us
    dot_general x1, matrix products, on_device(): jnp.einsum('bki,bkj->bij', lefts, rights, preferred_element_type=jnp.floa...  2.99 us
    dot_general x1, matrix products, on_device(): lax.dot_general(normed, grad_key, CONTRACT, preferred_element_type=jnp.fl...  1.9 us
    unnamed x8, local copies, waits for them, and re-layouts  1.69 us

profile of v13, /device:TPU:1, one launch (start us, length us, event | category | flops | bytes accessed | tf_op | source)
XLA Modules:
  0.0 78.9 jit_solution(12778998252482319666)
XLA Ops:
  0.6 0.0 copy-start
  0.6 1.1 %fusion.22 = (bf16[2,32,1024]{2,1,0:T(8,128)(2,1)S(1)}, bf16[2,32,1024]{2,1,0:T(8,128)(2,1)S(1)}, bf16[2,32,1024]{2,1,0:T(8,128)(2,1)S(1)}) fusion(f32[2,32,1024]{2,1,0:T(8,128)} %param.9), kind=kLoop, calls=%fused_computation.25 | loop fusion | flops 458752 | bytes 655360 | tf_op jit(solution)/shard_map/convert_element_type | solution.py:380
  1.8 0.3 copy-done
  2.0 0.0 copy-start.1
  2.0 0.0 copy-start.2
  2.0 4.0 %convert_add_fusion.1.mq_ref = f32[1024,1024]{1,0:T(8,128)S(1)} fusion(bf16[2,1024,1024]{2,1,0:T(8,128)(2,1)} %param.8, bf16[640,1024]{1,0:T(8,128)(2,1)S(1)} %copy-done, bf16[640,1024]{1,0:T(8,128)(2,1)} %param.6), kind=kOutput, calls=%fused_computation.9 | convolution fusion | flops 1344274432 | bytes 8912896 | tf_op jit(solution)/shard_map/dot_general | solution.py:360
  6.0 0.0 copy-done.1
  6.0 0.0 copy-done.2
  6.1 1.9 %convert_add_fusion.mk_ref = f32[1024,1024]{1,0:T(8,128)S(1)} fusion(bf16[2,1024,1024]{2,1,0:T(8,128)(2,1)S(1)} %copy-done.1, bf16[640,1024]{1,0:T(8,128)(2,1)S(1)} %copy-done, bf16[640,1024]{1,0:T(8,128)(2,1)S(1)} %copy-done.2), kind=kOutput, calls=%fused_computation.8 | convolution fusion | flops 1344274432 | bytes 8912896 | tf_op jit(solution)/shard_map/dot_general | solution.py:361
  8.0 1.4 %fusion.2 = f32[2,64,1024]{2,1,0:T(8,128)S(1)} fusion(f32[1,1024,1024]{2,1,0:T(8,128)S(1)} %bitcast.27, f32[1,1024,1024]{2,1,0:T(8,128)S(1)} %bitcast.23, bf16[2,32,1024]{2,1,0:T(8,128)(2,1)S(1)} %get-tuple-element.12, bf16[2,32,1024]{2,1,0:T(8,128)(2,1)S(1)} %get-tuple-element.13), kind=kOutput, calls=%fused_computation.10 | convolution fusion | flops 279445504 | bytes 9175040 | tf_op jit(solution)/shard_map/bkj,bij->bki/dot_general | solution.py:387
  9.4 1.4 %fusion.1 = f32[2,96,1024]{2,1,0:T(8,128)S(1)} fusion(f32[1,1024,1024]{2,1,0:T(8,128)S(1)} %bitcast.28, f32[1,1024,1024]{2,1,0:T(8,128)S(1)} %bitcast.24, bf16[2,32,1024]{2,1,0:T(8,128)(2,1)S(1)} %get-tuple-element.11, bf16[2,32,1024]{2,1,0:T(8,128)(2,1)S(1)} %get-tuple-element.12, bf16[2,32,1024]{2,1,0:T(8,128)(2,1)S(1)} %get-tuple-element.13), kind=kOutput, calls=%fused_computation.7 | convolution fusion | flops 410124288 | bytes 9568256 | tf_op jit(solution)/shard_map/bkj,bij->bki/dot_general | solution.py:387
  10.8 1.6 %fusion.14.x_ref = f32[2,32,1024]{2,1,0:T(8,128)S(1)} fusion(bf16[2,32,1024]{2,1,0:T(8,128)(2,1)S(1)} %get-tuple-element.13, f32[1,1024,1024]{2,1,0:T(8,128)S(1)} %bitcast.29, f32[1,1024,1024]{2,1,0:T(8,128)S(1)} %bitcast.25, f32[2,64,1024]{2,1,0:T(8,128)S(1)} %fusion.2, f32[2,96,1024]{2,1,0:T(8,128)S(1)} %fusion.1), kind=kOutput, calls=%fused_computation.15 | convolution fusion | flops 147128320 | bytes 10092544 | tf_op jit(solution)/shard_map/bkj,bij->bki/dot_general | solution.py:387
  12.4 62.1 %shard_map.76 = (f32[2,32,1024]{2,1,0:T(8,128)S(1)}, bf16[2,192,1024]{2,1,0:T(8,128)(2,1)S(1)}, f32[2,32,1024]{2,1,0:T(8,128)S(1)}, bf16[2,192,1024]{2,1,0:T(8,128)(2,1)S(1)}) custom-call(f32[2,32,1024]{2,1,0:T(8,128)S(1)} %fusion.14.x_ref, f32[1024,1024]{1,0:T(8,128)S(1)} %convert_add_fusion.1.mq_ref, f32[1024,1024]{1,0:T(8,128)S(1)} %convert_add_fusion.mk_ref), custom_call_target="tpu_custom_call" | custom-call | tf_op jit(solution)/shard_map/pallas_call | solution.py:291
  74.5 3.0 %subtract_convert_fusion = bf16[2,1024,1024]{2,1,0:T(8,128)(2,1)} fusion(f32[1,1024,1024]{2,1,0:T(8,128)S(1)} %bitcast.30, f32[1,1024,1024]{2,1,0:T(8,128)S(1)} %bitcast.26, bf16[2,192,1024]{2,1,0:T(8,128)(2,1)S(1)} %get-tuple-element.7, bf16[2,192,1024]{2,1,0:T(8,128)(2,1)S(1)} %get-tuple-element.8), kind=kOutput, calls=%fused_computation.6 | convolution fusion | flops 811597824 | bytes 14155776 | tf_op jit(solution)/shard_map/bki,bkj->bij/dot_general | solution.py:371
  77.5 0.7 copy.10
  78.2 0.7 copy.11
Async XLA Ops:
  0.6 1.4 %copy-start = (bf16[640,1024]{1,0:T(8,128)(2,1)S(1)}, bf16[640,1024]{1,0:T(8,128)(2,1)}, u32[]{:S(2)}) copy-start(bf16[640,1024]{1,0:T(8,128)(2,1)} %param.5) | copy-start | bytes 3932164
  2.0 4.0 %copy-start.1 = (bf16[2,1024,1024]{2,1,0:T(8,128)(2,1)S(1)}, bf16[2,1024,1024]{2,1,0:T(8,128)(2,1)}, u32[]{:S(2)}) copy-start(bf16[2,1024,1024]{2,1,0:T(8,128)(2,1)} %param.8) | copy-start | bytes 12582916
  2.0 4.0 %copy-start.2 = (bf16[640,1024]{1,0:T(8,128)(2,1)S(1)}, bf16[640,1024]{1,0:T(8,128)(2,1)}, u32[]{:S(2)}) copy-start(bf16[640,1024]{1,0:T(8,128)(2,1)} %param.7) | copy-start | bytes 3932164

commit v14 on v13

--- a/solution.py
+++ b/solution.py
@@ -369,7 +369,15 @@
     left_rows, lefts, right_rows, rights = factors(
         left_local, query_merged, key_merged, nx, ny, float(replicas))
     approx = jnp.einsum("bki,bkj->bij", lefts, rights, preferred_element_type=jnp.float32)
-    return ((merged - approx).astype(jnp.bfloat16), left_rows, right_rows)
+    k = left_rows.shape[1]
+    left_out = exact_sum(lefts[:, :k], lefts[:, 2 * k:3 * k], lefts[:, 5 * k:])
+    right_out = exact_sum(rights[:, :k], rights[:, k:2 * k], rights[:, 3 * k:4 * k])
+    return ((merged - approx).astype(jnp.bfloat16), left_out, right_out)
+
+
+def exact_sum(hi, mid, lo):
+    f32 = jnp.float32
+    return (hi.astype(f32) + mid.astype(f32)) + lo.astype(f32)
 
 
 def split3(x):

time: 79 us -> 79.2 us (level)
  local copies, waits for them, and re-layouts: 1.69 us -> 0.29 us
  other arithmetic: 1.11 us -> 2 us
    unnamed x8 -> x6, local copies, waits for them, and re-layouts: 1.69 us -> 0.29 us
    add x0 -> x1, other arithmetic: none -> 0.89 us  [exact_sum(): return hi.astype(f32) + mid.astype(f32) + lo.astype(f32)]
where the time goes in v14:
time: 79.2 us; the launch traced here: 79.1 us
  Pallas kernels  62.8 us (79%)
  matrix products  13.3 us (17%)
  other arithmetic  2 us (3%)
    pallas_call x1, Pallas kernels, factors(): pl.pallas_call(functools.partial(factors_kernel, nx, ny, divisor), out_sh...  62.8 us
    dot_general x3, matrix products, rows_times(): jnp.einsum(spec, jnp.concatenate(group, axis=1), big, preferred_element_t...  4.44 us
    dot_general x1, matrix products, on_device(): lax.dot_general(normed, grad_query, CONTRACT, preferred_element_type=jnp....  3.99 us
    dot_general x1, matrix products, on_device(): jnp.einsum('bki,bkj->bij', lefts, rights, preferred_element_type=jnp.floa...  2.99 us
    dot_general x1, matrix products, on_device(): lax.dot_general(normed, grad_key, CONTRACT, preferred_element_type=jnp.fl...  1.9 us

profile of v14, /device:TPU:1, one launch (start us, length us, event | category | flops | bytes accessed | tf_op | source)
XLA Modules:
  0.0 79.1 jit_solution(9616744880223207959)
XLA Ops:
  0.6 0.0 copy-start
  0.6 1.1 %fusion.22 = (bf16[2,32,1024]{2,1,0:T(8,128)(2,1)S(1)}, bf16[2,32,1024]{2,1,0:T(8,128)(2,1)S(1)}, bf16[2,32,1024]{2,1,0:T(8,128)(2,1)S(1)}) fusion(f32[2,32,1024]{2,1,0:T(8,128)} %param.9), kind=kLoop, calls=%fused_computation.25 | loop fusion | flops 458752 | bytes 655360 | tf_op jit(solution)/shard_map/convert_element_type | solution.py:388
  1.8 0.3 copy-done
  2.0 0.0 copy-start.1
  2.0 0.0 copy-start.2
  2.0 4.0 %convert_add_fusion.1.mq_ref = f32[1024,1024]{1,0:T(8,128)S(1)} fusion(bf16[2,1024,1024]{2,1,0:T(8,128)(2,1)} %param.8, bf16[640,1024]{1,0:T(8,128)(2,1)S(1)} %copy-done, bf16[640,1024]{1,0:T(8,128)(2,1)} %param.6), kind=kOutput, calls=%fused_computation.9 | convolution fusion | flops 1344274432 | bytes 8912896 | tf_op jit(solution)/shard_map/dot_general | solution.py:360
  6.0 0.0 copy-done.1
  6.0 0.0 copy-done.2
  6.1 1.9 %convert_add_fusion.mk_ref = f32[1024,1024]{1,0:T(8,128)S(1)} fusion(bf16[2,1024,1024]{2,1,0:T(8,128)(2,1)S(1)} %copy-done.1, bf16[640,1024]{1,0:T(8,128)(2,1)S(1)} %copy-done, bf16[640,1024]{1,0:T(8,128)(2,1)S(1)} %copy-done.2), kind=kOutput, calls=%fused_computation.8 | convolution fusion | flops 1344274432 | bytes 8912896 | tf_op jit(solution)/shard_map/dot_general | solution.py:361
  8.0 1.4 %fusion.2 = f32[2,64,1024]{2,1,0:T(8,128)S(1)} fusion(f32[1,1024,1024]{2,1,0:T(8,128)S(1)} %bitcast.27, f32[1,1024,1024]{2,1,0:T(8,128)S(1)} %bitcast.23, bf16[2,32,1024]{2,1,0:T(8,128)(2,1)S(1)} %get-tuple-element.8, bf16[2,32,1024]{2,1,0:T(8,128)(2,1)S(1)} %get-tuple-element.9), kind=kOutput, calls=%fused_computation.10 | convolution fusion | flops 279445504 | bytes 9175040 | tf_op jit(solution)/shard_map/bkj,bij->bki/dot_general | solution.py:395
  9.4 1.4 %fusion.1 = f32[2,96,1024]{2,1,0:T(8,128)S(1)} fusion(f32[1,1024,1024]{2,1,0:T(8,128)S(1)} %bitcast.28, f32[1,1024,1024]{2,1,0:T(8,128)S(1)} %bitcast.24, bf16[2,32,1024]{2,1,0:T(8,128)(2,1)S(1)} %get-tuple-element.7, bf16[2,32,1024]{2,1,0:T(8,128)(2,1)S(1)} %get-tuple-element.8, bf16[2,32,1024]{2,1,0:T(8,128)(2,1)S(1)} %get-tuple-element.9), kind=kOutput, calls=%fused_computation.7 | convolution fusion | flops 410124288 | bytes 9568256 | tf_op jit(solution)/shard_map/bkj,bij->bki/dot_general | solution.py:395
  10.8 1.6 %fusion.14.x_ref = f32[2,32,1024]{2,1,0:T(8,128)S(1)} fusion(bf16[2,32,1024]{2,1,0:T(8,128)(2,1)S(1)} %get-tuple-element.9, f32[1,1024,1024]{2,1,0:T(8,128)S(1)} %bitcast.29, f32[1,1024,1024]{2,1,0:T(8,128)S(1)} %bitcast.25, f32[2,64,1024]{2,1,0:T(8,128)S(1)} %fusion.2, f32[2,96,1024]{2,1,0:T(8,128)S(1)} %fusion.1), kind=kOutput, calls=%fused_computation.15 | convolution fusion | flops 147128320 | bytes 10092544 | tf_op jit(solution)/shard_map/bkj,bij->bki/dot_general | solution.py:395
  12.4 62.8 %shard_map.76 = (f32[2,32,1024]{2,1,0:T(8,128)}, bf16[2,192,1024]{2,1,0:T(8,128)(2,1)S(1)}, f32[2,32,1024]{2,1,0:T(8,128)}, bf16[2,192,1024]{2,1,0:T(8,128)(2,1)S(1)}) custom-call(f32[2,32,1024]{2,1,0:T(8,128)S(1)} %fusion.14.x_ref, f32[1024,1024]{1,0:T(8,128)S(1)} %convert_add_fusion.1.mq_ref, f32[1024,1024]{1,0:T(8,128)S(1)} %convert_add_fusion.mk_ref), custom_call_target="tpu_custom_call" | custom-call | tf_op jit(solution)/shard_map/pallas_call | solution.py:291
  75.2 3.0 %subtract_convert_fusion = bf16[2,1024,1024]{2,1,0:T(8,128)(2,1)} fusion(f32[1,1024,1024]{2,1,0:T(8,128)S(1)} %bitcast.30, f32[1,1024,1024]{2,1,0:T(8,128)S(1)} %bitcast.26, bf16[2,192,1024]{2,1,0:T(8,128)(2,1)S(1)} %get-tuple-element.5, bf16[2,192,1024]{2,1,0:T(8,128)(2,1)S(1)} %get-tuple-element.6), kind=kOutput, calls=%fused_computation.6 | convolution fusion | flops 811597824 | bytes 14155776 | tf_op jit(solution)/shard_map/bki,bkj->bij/dot_general | solution.py:371
  78.2 0.9 %convert_add_fusion.2 = (f32[2,32,1024]{2,1,0:T(8,128)}, f32[2,32,1024]{2,1,0:T(8,128)}) fusion(bf16[2,192,1024]{2,1,0:T(8,128)(2,1)S(1)} %get-tuple-element.6, bf16[2,192,1024]{2,1,0:T(8,128)(2,1)S(1)} %get-tuple-element.5), kind=kLoop, calls=%fused_computation.31 | loop fusion | flops 655360 | bytes 1310720 | tf_op jit(solution)/shard_map/add | solution.py:380
Async XLA Ops:
  0.6 1.4 %copy-start = (bf16[640,1024]{1,0:T(8,128)(2,1)S(1)}, bf16[640,1024]{1,0:T(8,128)(2,1)}, u32[]{:S(2)}) copy-start(bf16[640,1024]{1,0:T(8,128)(2,1)} %param.5) | copy-start | bytes 3932164
  2.0 4.0 %copy-start.1 = (bf16[2,1024,1024]{2,1,0:T(8,128)(2,1)S(1)}, bf16[2,1024,1024]{2,1,0:T(8,128)(2,1)}, u32[]{:S(2)}) copy-start(bf16[2,1024,1024]{2,1,0:T(8,128)(2,1)} %param.8) | copy-start | bytes 12582916
  2.0 4.0 %copy-start.2 = (bf16[640,1024]{1,0:T(8,128)(2,1)S(1)}, bf16[640,1024]{1,0:T(8,128)(2,1)}, u32[]{:S(2)}) copy-start(bf16[640,1024]{1,0:T(8,128)(2,1)} %param.7) | copy-start | bytes 3932164

commit v15 on v14

--- a/solution.py
+++ b/solution.py
@@ -32,7 +32,8 @@
 
 
 def allreduce_body(nx, ny, orthonormalize, divisor, x_ref, o_ref, recv_a, p_t, recv_b, recv_c, recv_d,
-                     sa, ra, sb, rb, sc, rc, sd, rd, with_barrier=True, idle_work=None):
+                     sa, ra, sb, rb, sc, rc, sd, rd, with_barrier=True, idle_work=None,
+                     produce=None):
     h = lax.axis_index("gx")
     a = lax.axis_index("gy")
     nb, rows = x_ref.shape[0], x_ref.shape[1]
@@ -70,7 +71,27 @@
         copy_a(lax.rem(a + j, ny), a).start()
         return carry
 
-    lax.fori_loop(1, ny, start_a, 0)
+    def start_part(b):
+        def start_one(j, carry):
+            peer = lax.rem(a + j, ny)
+            pltpu.make_async_remote_copy(
+                src_ref=x_ref.at[b, :, pl.ds(pl.multiple_of(peer * LANES, LANES), LANES)],
+                dst_ref=recv_a.at[a, b],
+                send_sem=sa.at[peer],
+                recv_sem=ra.at[a],
+                device_id=(h, peer),
+                device_id_type=MESH_ID,
+            ).start()
+            return carry
+
+        lax.fori_loop(1, ny, start_one, 0)
+
+    if produce is None:
+        lax.fori_loop(1, ny, start_a, 0)
+    else:
+        for b in range(nb):
+            produce(b)
+            start_part(b)
     recv_a[a] = x_ref[:, :, pl.ds(pl.multiple_of(a * LANES, LANES), LANES)]
     if idle_work is not None:
         idle_work()
@@ -254,11 +275,13 @@
     allreduce_body(nx, ny, True, None, x_ref, left_ref, *first, idle_work=split_merged)
     write_pieces(left_ref, ((0, 0, 1, 0, 1, 2), (0, 1)), (lefts_ref, pair_ref))
     k = left_ref.shape[1]
-    for b in range(len(merged_refs)):
+    def right_product(b):
         both = jnp.dot(pair_ref[b], m_hi_ref[b], preferred_element_type=jnp.float32)
         cross = jnp.dot(lefts_ref[b, :k, :], m_mid_ref[b], preferred_element_type=jnp.float32)
         local_ref[b] = both[:k] + (both[k:] + cross)
-    allreduce_body(nx, ny, False, divisor, local_ref, right_ref, *second, with_barrier=False)
+
+    allreduce_body(nx, ny, False, divisor, local_ref, right_ref, *second, with_barrier=False,
+                   produce=right_product)
     write_pieces(right_ref, ((0, 1, 0, 2, 1, 0),), (rights_ref,))
 
 

time: 79.2 us -> 78.6 us (level)
  no operation moved by 1% of the time
where the time goes in v15:
time: 78.6 us; the launch traced here: 78.5 us
  Pallas kernels  62.2 us (79%)
  matrix products  13.3 us (17%)
  other arithmetic  2 us (3%)
    pallas_call x1, Pallas kernels, factors(): pl.pallas_call(functools.partial(factors_kernel, nx, ny, divisor), out_sh...  62.2 us
    dot_general x3, matrix products, rows_times(): jnp.einsum(spec, jnp.concatenate(group, axis=1), big, preferred_element_t...  4.44 us
    dot_general x1, matrix products, on_device(): lax.dot_general(normed, grad_query, CONTRACT, preferred_element_type=jnp....  3.99 us
    dot_general x1, matrix products, on_device(): jnp.einsum('bki,bkj->bij', lefts, rights, preferred_element_type=jnp.floa...  2.99 us
    dot_general x1, matrix products, on_device(): lax.dot_general(normed, grad_key, CONTRACT, preferred_element_type=jnp.fl...  1.9 us

profile of v15, /device:TPU:1, one launch (start us, length us, event | category | flops | bytes accessed | tf_op | source)
XLA Modules:
  0.0 78.5 jit_solution(14171696845247781809)
XLA Ops:
  0.6 0.0 copy-start
  0.6 1.1 %fusion.22 = (bf16[2,32,1024]{2,1,0:T(8,128)(2,1)S(1)}, bf16[2,32,1024]{2,1,0:T(8,128)(2,1)S(1)}, bf16[2,32,1024]{2,1,0:T(8,128)(2,1)S(1)}) fusion(f32[2,32,1024]{2,1,0:T(8,128)} %param.9), kind=kLoop, calls=%fused_computation.25 | loop fusion | flops 458752 | bytes 655360 | tf_op jit(solution)/shard_map/convert_element_type | solution.py:411
  1.8 0.3 copy-done
  2.0 0.0 copy-start.1
  2.0 0.0 copy-start.2
  2.0 4.0 %convert_add_fusion.1.mq_ref = f32[1024,1024]{1,0:T(8,128)S(1)} fusion(bf16[2,1024,1024]{2,1,0:T(8,128)(2,1)} %param.8, bf16[640,1024]{1,0:T(8,128)(2,1)S(1)} %copy-done, bf16[640,1024]{1,0:T(8,128)(2,1)} %param.6), kind=kOutput, calls=%fused_computation.9 | convolution fusion | flops 1344274432 | bytes 8912896 | tf_op jit(solution)/shard_map/dot_general | solution.py:383
  6.0 0.0 copy-done.1
  6.0 0.0 copy-done.2
  6.1 1.9 %convert_add_fusion.mk_ref = f32[1024,1024]{1,0:T(8,128)S(1)} fusion(bf16[2,1024,1024]{2,1,0:T(8,128)(2,1)S(1)} %copy-done.1, bf16[640,1024]{1,0:T(8,128)(2,1)S(1)} %copy-done, bf16[640,1024]{1,0:T(8,128)(2,1)S(1)} %copy-done.2), kind=kOutput, calls=%fused_computation.8 | convolution fusion | flops 1344274432 | bytes 8912896 | tf_op jit(solution)/shard_map/dot_general | solution.py:384
  8.0 1.4 %fusion.2 = f32[2,64,1024]{2,1,0:T(8,128)S(1)} fusion(f32[1,1024,1024]{2,1,0:T(8,128)S(1)} %bitcast.27, f32[1,1024,1024]{2,1,0:T(8,128)S(1)} %bitcast.23, bf16[2,32,1024]{2,1,0:T(8,128)(2,1)S(1)} %get-tuple-element.8, bf16[2,32,1024]{2,1,0:T(8,128)(2,1)S(1)} %get-tuple-element.9), kind=kOutput, calls=%fused_computation.10 | convolution fusion | flops 279445504 | bytes 9175040 | tf_op jit(solution)/shard_map/bkj,bij->bki/dot_general | solution.py:418
  9.4 1.4 %fusion.1 = f32[2,96,1024]{2,1,0:T(8,128)S(1)} fusion(f32[1,1024,1024]{2,1,0:T(8,128)S(1)} %bitcast.28, f32[1,1024,1024]{2,1,0:T(8,128)S(1)} %bitcast.24, bf16[2,32,1024]{2,1,0:T(8,128)(2,1)S(1)} %get-tuple-element.7, bf16[2,32,1024]{2,1,0:T(8,128)(2,1)S(1)} %get-tuple-element.8, bf16[2,32,1024]{2,1,0:T(8,128)(2,1)S(1)} %get-tuple-element.9), kind=kOutput, calls=%fused_computation.7 | convolution fusion | flops 410124288 | bytes 9568256 | tf_op jit(solution)/shard_map/bkj,bij->bki/dot_general | solution.py:418
  10.8 1.6 %fusion.14.x_ref = f32[2,32,1024]{2,1,0:T(8,128)S(1)} fusion(bf16[2,32,1024]{2,1,0:T(8,128)(2,1)S(1)} %get-tuple-element.9, f32[1,1024,1024]{2,1,0:T(8,128)S(1)} %bitcast.29, f32[1,1024,1024]{2,1,0:T(8,128)S(1)} %bitcast.25, f32[2,64,1024]{2,1,0:T(8,128)S(1)} %fusion.2, f32[2,96,1024]{2,1,0:T(8,128)S(1)} %fusion.1), kind=kOutput, calls=%fused_computation.15 | convolution fusion | flops 147128320 | bytes 10092544 | tf_op jit(solution)/shard_map/bkj,bij->bki/dot_general | solution.py:418
  12.4 62.2 %shard_map.76 = (f32[2,32,1024]{2,1,0:T(8,128)}, bf16[2,192,1024]{2,1,0:T(8,128)(2,1)S(1)}, f32[2,32,1024]{2,1,0:T(8,128)}, bf16[2,192,1024]{2,1,0:T(8,128)(2,1)S(1)}) custom-call(f32[2,32,1024]{2,1,0:T(8,128)S(1)} %fusion.14.x_ref, f32[1024,1024]{1,0:T(8,128)S(1)} %convert_add_fusion.1.mq_ref, f32[1024,1024]{1,0:T(8,128)S(1)} %convert_add_fusion.mk_ref), custom_call_target="tpu_custom_call" | custom-call | tf_op jit(solution)/shard_map/pallas_call | solution.py:314
  74.6 3.0 %subtract_convert_fusion = bf16[2,1024,1024]{2,1,0:T(8,128)(2,1)} fusion(f32[1,1024,1024]{2,1,0:T(8,128)S(1)} %bitcast.30, f32[1,1024,1024]{2,1,0:T(8,128)S(1)} %bitcast.26, bf16[2,192,1024]{2,1,0:T(8,128)(2,1)S(1)} %get-tuple-element.5, bf16[2,192,1024]{2,1,0:T(8,128)(2,1)S(1)} %get-tuple-element.6), kind=kOutput, calls=%fused_computation.6 | convolution fusion | flops 811597824 | bytes 14155776 | tf_op jit(solution)/shard_map/bki,bkj->bij/dot_general | solution.py:394
  77.6 0.9 %convert_add_fusion.2 = (f32[2,32,1024]{2,1,0:T(8,128)}, f32[2,32,1024]{2,1,0:T(8,128)}) fusion(bf16[2,192,1024]{2,1,0:T(8,128)(2,1)S(1)} %get-tuple-element.6, bf16[2,192,1024]{2,1,0:T(8,128)(2,1)S(1)} %get-tuple-element.5), kind=kLoop, calls=%fused_computation.31 | loop fusion | flops 655360 | bytes 1310720 | tf_op jit(solution)/shard_map/add | solution.py:403
Async XLA Ops:
  0.6 1.4 %copy-start = (bf16[640,1024]{1,0:T(8,128)(2,1)S(1)}, bf16[640,1024]{1,0:T(8,128)(2,1)}, u32[]{:S(2)}) copy-start(bf16[640,1024]{1,0:T(8,128)(2,1)} %param.5) | copy-start | bytes 3932164
  2.0 4.0 %copy-start.1 = (bf16[2,1024,1024]{2,1,0:T(8,128)(2,1)S(1)}, bf16[2,1024,1024]{2,1,0:T(8,128)(2,1)}, u32[]{:S(2)}) copy-start(bf16[2,1024,1024]{2,1,0:T(8,128)(2,1)} %param.8) | copy-start | bytes 12582916
  2.0 4.0 %copy-start.2 = (bf16[640,1024]{1,0:T(8,128)(2,1)S(1)}, bf16[640,1024]{1,0:T(8,128)(2,1)}, u32[]{:S(2)}) copy-start(bf16[640,1024]{1,0:T(8,128)(2,1)} %param.7) | copy-start | bytes 3932164

commit v16 on v15

--- a/solution.py
+++ b/solution.py
@@ -93,8 +93,6 @@
             produce(b)
             start_part(b)
     recv_a[a] = x_ref[:, :, pl.ds(pl.multiple_of(a * LANES, LANES), LANES)]
-    if idle_work is not None:
-        idle_work()
 
     def wait_a(j, carry):
         copy_a(lax.rem(a + j, ny), a).wait_send()
@@ -124,6 +122,8 @@
     lax.fori_loop(1, nx, start_b, 0)
     own = lax.rem(h, nt)
     recv_b[h] = p_t[own]
+    if idle_work is not None:
+        idle_work()
 
     def wait_b(j, carry):
         peer = lax.rem(h + j, nx)

time: 78.6 us -> 78.6 us (level)
  no operation moved by 1% of the time
where the time goes in v16:
time: 78.6 us; the launch traced here: 78.5 us
  Pallas kernels  62.2 us (79%)
  matrix products  13.3 us (17%)
  other arithmetic  2 us (3%)
    pallas_call x1, Pallas kernels, factors(): pl.pallas_call(functools.partial(factors_kernel, nx, ny, divisor), out_sh...  62.2 us
    dot_general x3, matrix products, rows_times(): jnp.einsum(spec, jnp.concatenate(group, axis=1), big, preferred_element_t...  4.44 us
    dot_general x1, matrix products, on_device(): lax.dot_general(normed, grad_query, CONTRACT, preferred_element_type=jnp....  3.99 us
    dot_general x1, matrix products, on_device(): jnp.einsum('bki,bkj->bij', lefts, rights, preferred_element_type=jnp.floa...  2.99 us
    dot_general x1, matrix products, on_device(): lax.dot_general(normed, grad_key, CONTRACT, preferred_element_type=jnp.fl...  1.9 us

profile of v16, /device:TPU:1, one launch (start us, length us, event | category | flops | bytes accessed | tf_op | source)
XLA Modules:
  0.0 78.5 jit_solution(17668984340447930112)
XLA Ops:
  0.6 0.0 copy-start
  0.6 1.1 %fusion.22 = (bf16[2,32,1024]{2,1,0:T(8,128)(2,1)S(1)}, bf16[2,32,1024]{2,1,0:T(8,128)(2,1)S(1)}, bf16[2,32,1024]{2,1,0:T(8,128)(2,1)S(1)}) fusion(f32[2,32,1024]{2,1,0:T(8,128)} %param.9), kind=kLoop, calls=%fused_computation.25 | loop fusion | flops 458752 | bytes 655360 | tf_op jit(solution)/shard_map/convert_element_type | solution.py:411
  1.8 0.3 copy-done
  2.0 0.0 copy-start.1
  2.0 0.0 copy-start.2
  2.0 4.0 %convert_add_fusion.1.mq_ref = f32[1024,1024]{1,0:T(8,128)S(1)} fusion(bf16[2,1024,1024]{2,1,0:T(8,128)(2,1)} %param.8, bf16[640,1024]{1,0:T(8,128)(2,1)S(1)} %copy-done, bf16[640,1024]{1,0:T(8,128)(2,1)} %param.6), kind=kOutput, calls=%fused_computation.9 | convolution fusion | flops 1344274432 | bytes 8912896 | tf_op jit(solution)/shard_map/dot_general | solution.py:383
  6.0 0.0 copy-done.1
  6.0 0.0 copy-done.2
  6.1 1.9 %convert_add_fusion.mk_ref = f32[1024,1024]{1,0:T(8,128)S(1)} fusion(bf16[2,1024,1024]{2,1,0:T(8,128)(2,1)S(1)} %copy-done.1, bf16[640,1024]{1,0:T(8,128)(2,1)S(1)} %copy-done, bf16[640,1024]{1,0:T(8,128)(2,1)S(1)} %copy-done.2), kind=kOutput, calls=%fused_computation.8 | convolution fusion | flops 1344274432 | bytes 8912896 | tf_op jit(solution)/shard_map/dot_general | solution.py:384
  8.0 1.4 %fusion.2 = f32[2,64,1024]{2,1,0:T(8,128)S(1)} fusion(f32[1,1024,1024]{2,1,0:T(8,128)S(1)} %bitcast.27, f32[1,1024,1024]{2,1,0:T(8,128)S(1)} %bitcast.23, bf16[2,32,1024]{2,1,0:T(8,128)(2,1)S(1)} %get-tuple-element.8, bf16[2,32,1024]{2,1,0:T(8,128)(2,1)S(1)} %get-tuple-element.9), kind=kOutput, calls=%fused_computation.10 | convolution fusion | flops 279445504 | bytes 9175040 | tf_op jit(solution)/shard_map/bkj,bij->bki/dot_general | solution.py:418
  9.4 1.4 %fusion.1 = f32[2,96,1024]{2,1,0:T(8,128)S(1)} fusion(f32[1,1024,1024]{2,1,0:T(8,128)S(1)} %bitcast.28, f32[1,1024,1024]{2,1,0:T(8,128)S(1)} %bitcast.24, bf16[2,32,1024]{2,1,0:T(8,128)(2,1)S(1)} %get-tuple-element.7, bf16[2,32,1024]{2,1,0:T(8,128)(2,1)S(1)} %get-tuple-element.8, bf16[2,32,1024]{2,1,0:T(8,128)(2,1)S(1)} %get-tuple-element.9), kind=kOutput, calls=%fused_computation.7 | convolution fusion | flops 410124288 | bytes 9568256 | tf_op jit(solution)/shard_map/bkj,bij->bki/dot_general | solution.py:418
  10.8 1.6 %fusion.14.x_ref = f32[2,32,1024]{2,1,0:T(8,128)S(1)} fusion(bf16[2,32,1024]{2,1,0:T(8,128)(2,1)S(1)} %get-tuple-element.9, f32[1,1024,1024]{2,1,0:T(8,128)S(1)} %bitcast.29, f32[1,1024,1024]{2,1,0:T(8,128)S(1)} %bitcast.25, f32[2,64,1024]{2,1,0:T(8,128)S(1)} %fusion.2, f32[2,96,1024]{2,1,0:T(8,128)S(1)} %fusion.1), kind=kOutput, calls=%fused_computation.15 | convolution fusion | flops 147128320 | bytes 10092544 | tf_op jit(solution)/shard_map/bkj,bij->bki/dot_general | solution.py:418
  12.4 62.2 %shard_map.76 = (f32[2,32,1024]{2,1,0:T(8,128)}, bf16[2,192,1024]{2,1,0:T(8,128)(2,1)S(1)}, f32[2,32,1024]{2,1,0:T(8,128)}, bf16[2,192,1024]{2,1,0:T(8,128)(2,1)S(1)}) custom-call(f32[2,32,1024]{2,1,0:T(8,128)S(1)} %fusion.14.x_ref, f32[1024,1024]{1,0:T(8,128)S(1)} %convert_add_fusion.1.mq_ref, f32[1024,1024]{1,0:T(8,128)S(1)} %convert_add_fusion.mk_ref), custom_call_target="tpu_custom_call" | custom-call | tf_op jit(solution)/shard_map/pallas_call | solution.py:314
  74.6 3.0 %subtract_convert_fusion = bf16[2,1024,1024]{2,1,0:T(8,128)(2,1)} fusion(f32[1,1024,1024]{2,1,0:T(8,128)S(1)} %bitcast.30, f32[1,1024,1024]{2,1,0:T(8,128)S(1)} %bitcast.26, bf16[2,192,1024]{2,1,0:T(8,128)(2,1)S(1)} %get-tuple-element.5, bf16[2,192,1024]{2,1,0:T(8,128)(2,1)S(1)} %get-tuple-element.6), kind=kOutput, calls=%fused_computation.6 | convolution fusion | flops 811597824 | bytes 14155776 | tf_op jit(solution)/shard_map/bki,bkj->bij/dot_general | solution.py:394
  77.6 0.9 %convert_add_fusion.2 = (f32[2,32,1024]{2,1,0:T(8,128)}, f32[2,32,1024]{2,1,0:T(8,128)}) fusion(bf16[2,192,1024]{2,1,0:T(8,128)(2,1)S(1)} %get-tuple-element.6, bf16[2,192,1024]{2,1,0:T(8,128)(2,1)S(1)} %get-tuple-element.5), kind=kLoop, calls=%fused_computation.31 | loop fusion | flops 655360 | bytes 1310720 | tf_op jit(solution)/shard_map/add | solution.py:403
Async XLA Ops:
  0.6 1.4 %copy-start = (bf16[640,1024]{1,0:T(8,128)(2,1)S(1)}, bf16[640,1024]{1,0:T(8,128)(2,1)}, u32[]{:S(2)}) copy-start(bf16[640,1024]{1,0:T(8,128)(2,1)} %param.5) | copy-start | bytes 3932164
  2.0 4.0 %copy-start.1 = (bf16[2,1024,1024]{2,1,0:T(8,128)(2,1)S(1)}, bf16[2,1024,1024]{2,1,0:T(8,128)(2,1)}, u32[]{:S(2)}) copy-start(bf16[2,1024,1024]{2,1,0:T(8,128)(2,1)} %param.8) | copy-start | bytes 12582916
  2.0 4.0 %copy-start.2 = (bf16[640,1024]{1,0:T(8,128)(2,1)S(1)}, bf16[640,1024]{1,0:T(8,128)(2,1)}, u32[]{:S(2)}) copy-start(bf16[640,1024]{1,0:T(8,128)(2,1)} %param.7) | copy-start | bytes 3932164
